TPU v7x, 32 devices: a whole 2x2x4 slice. The times are simulated.
32 devices in a mesh: wide: 8 (over z, y), narrow: 4 (over x, core).
Axes of the slice: x: 2, y: 2, z: 4, core: 2. Of those that a mesh axis runs over, the one named last changes fastest.
Arguments:
- latents: bfloat16 [32, 256, 768], P('wide', None, 'narrow'), may hold values from -6 to 6
- cotangent: bfloat16 [32, 256, 768], P('wide', None, 'narrow'), may hold values from -6 to 6
- timesteps: int32 [32], replicated, may hold values from 0 to 999, as said below
- time_in: float32 [256, 768], replicated, may hold values from -0.375 to 0.375
- time_out: float32 [768, 768], replicated, may hold values from -0.21875 to 0.21875
- ada_weight: float32 [768, 4608], replicated, may hold values from -0.21875 to 0.21875
- ada_bias: float32 [4608], replicated, may hold values from -3 to 3
- attn_kernel: float32 [9, 768], replicated, may hold values from -2 to 2
- qkv_weight: bfloat16 [3, 768, 768], P(None, None, 'narrow'), may hold values from -0.21875 to 0.21875
- out_weight: bfloat16 [768, 768], P('narrow'), may hold values from -0.875 to 0.875
- up_weight: bfloat16 [768, 3072], P(None, 'narrow'), may hold values from -0.21875 to 0.21875
- ffn_kernel: float32 [9, 3072], P(None, 'narrow'), may hold values from -2 to 2
- down_weight: bfloat16 [3072, 768], P('narrow'), may hold values from -0.21875 to 0.21875
Outputs:
- outputs: bfloat16 [32, 256, 768], P('wide', None, 'narrow')
- input_grad: bfloat16 [32, 256, 768], P('wide', None, 'narrow')
- time_in_grad: float32 [256, 768], replicated
- time_out_grad: float32 [768, 768], replicated
- ada_weight_grad: float32 [768, 4608], replicated
- ada_bias_grad: float32 [4608], replicated
- attn_kernel_grad: float32 [9, 768], replicated
- qkv_weight_grad: float32 [3, 768, 768], P(None, None, 'narrow')
- out_weight_grad: float32 [768, 768], P('narrow')
- up_weight_grad: float32 [768, 3072], P(None, 'narrow')
- ffn_kernel_grad: float32 [9, 3072], P(None, 'narrow')
- down_weight_grad: float32 [3072, 768], P('narrow')
Inputs may be any that keep to these rules, and one draw needn't show every extreme that they name: `timesteps`: no two latents of one wide index fall into the same bucket; each bucket holds at most 2 * 4 latents, and some bucket holds exactly 2 * 4.
All inputs are finite; a program needn't handle non-finite values.
Results may differ from a plain program's by a relative error of at most 0.022.
Values may be sent and summed in bfloat16 or wider, within the bound.
No kernel may reach another device: no remote copies, remote signals or barrier semaphores. Data moves between devices by JAX's collectives and lax.ppermute only.
A program may use at most 256 MiB of HBM per device.

v0:
```python
import math

import jax
import jax.numpy as jnp
from jax import lax
from jax.sharding import PartitionSpec as P

HEAD_DIM = 64
FREQ = 256
SIDE = 16


HIGHEST = lax.Precision.HIGHEST


def layer_norm(values):
    center = values - jnp.mean(values, -1, keepdims=True)
    spread = jnp.mean(center * center, -1, keepdims=True)
    return center * lax.rsqrt(spread + 1e-06)


def conv_taps(values, kernel):
    extent = values.shape[1]
    padded = jnp.pad(values, ((0, 0), (1, 1), (1, 1), (0, 0)))
    result = jnp.zeros(values.shape, jnp.float32)
    for r in range(3):
        for c in range(3):
            result = result + padded[:, r : r + extent, c : c + extent, :] * kernel[3 * r + c]
    return result


def unshuffle(values):
    leading, extent, _, channels = values.shape
    halved = extent // 2
    moved = values.reshape(leading, halved, 2, halved, 2, channels).transpose(0, 2, 4, 1, 3, 5)
    return moved.reshape(leading, 4, halved * halved, channels)


def shuffle(values, extent):
    leading, _, _, channels = values.shape
    halved = extent // 2
    moved = values.reshape(leading, 2, 2, halved, halved, channels).transpose(0, 3, 1, 4, 2, 5)
    return moved.reshape(leading, extent * extent, channels)


def embed_times(stamps):
    halved = FREQ // 2
    freqs = jnp.exp(-math.log(10000.0) * jnp.arange(halved, dtype=jnp.float32) / halved)
    angles = stamps[:, None] * freqs[None, :]
    return jnp.concatenate([jnp.cos(angles), jnp.sin(angles)], 1)


def condition(stamps, time_in, time_out, ada_weight, ada_bias):
    embedded = embed_times(stamps)
    inner = jax.nn.silu(jnp.dot(embedded, time_in, precision=HIGHEST))
    outer = jax.nn.silu(jnp.dot(inner, time_out, precision=HIGHEST))
    return jnp.dot(outer, ada_weight, precision=HIGHEST) + ada_bias


def modulate(values, modulation, offset):
    width = values.shape[2]
    shifted = modulation[:, None, offset * width : (offset + 1) * width]
    scaled = modulation[:, None, (offset + 1) * width : (offset + 2) * width]
    return layer_norm(values) * (1.0 + scaled) + shifted


def pre_attention(inputs, modulation, attn_kernel):
    leading, _, width = inputs.shape
    first = modulate(inputs, modulation, 0)
    return unshuffle(conv_taps(first.reshape(leading, SIDE, SIDE, width), attn_kernel))


def hidden_act(hidden, ffn_kernel):
    leading, tokens_per, units = hidden.shape
    mixed = conv_taps(hidden.reshape(leading, SIDE, SIDE, units), ffn_kernel)
    return jax.nn.gelu(mixed.reshape(leading, tokens_per, units))


def attend(grouped_low, qkv_weight):
    blocks, quarter, _ = grouped_low.shape
    head_count = qkv_weight.shape[2] // HEAD_DIM
    factor = 1.0 / math.sqrt(HEAD_DIM)
    project = jnp.einsum(
        "nqd,tde->tnqe", grouped_low, qkv_weight, preferred_element_type=jnp.float32
    )
    project = project.astype(jnp.bfloat16).reshape(3, blocks, quarter, head_count, HEAD_DIM)
    scores = (
        jnp.einsum("nqhe,nkhe->nhqk", project[0], project[1], preferred_element_type=jnp.float32)
        * factor
    )
    attention = jax.nn.softmax(scores, axis=-1)
    attention_low = attention.astype(jnp.bfloat16)
    context = jnp.einsum(
        "nhqk,nkhe->nqhe", attention_low, project[2], preferred_element_type=jnp.float32
    )
    context = context.astype(jnp.bfloat16).reshape(blocks, quarter, head_count * HEAD_DIM)
    return (project, attention, attention_low, context)


def body(
    latents,
    cotangent,
    timesteps,
    time_in,
    time_out,
    ada_weight,
    ada_bias,
    attn_kernel,
    qkv_weight,
    out_weight,
    up_weight,
    ffn_kernel,
    down_weight,
):
    wide_count = lax.axis_size("wide")
    position = lax.axis_index("wide")
    narrow_at = lax.axis_index("narrow")
    per_dev = latents.shape[0]
    tokens_per = latents.shape[1]
    capacity = 2 * per_dev
    latent_total = timesteps.shape[0]
    bucket = timesteps * wide_count // 1000
    latent_ids = jnp.arange(latent_total, dtype=jnp.int32)
    owners = latent_ids // per_dev
    devices = jnp.arange(wide_count, dtype=jnp.int32)
    own_dest = lax.dynamic_slice_in_dim(bucket, position * per_dev, per_dev)
    outgoing = (own_dest[None, :] == devices[:, None]).astype(jnp.bfloat16)
    from_owner = (owners[None, :] == devices[:, None]) & (bucket == position)[None, :]
    arrivals = jnp.sum(from_owner.astype(jnp.int32), 1)
    placed = jnp.cumsum(arrivals) - arrivals
    slot_ids = jnp.arange(capacity, dtype=jnp.int32)
    packing = (placed[None, :] == slot_ids[:, None]) & (arrivals[None, :] > 0)
    owner_times = jnp.sum(jnp.where(from_owner, timesteps[None, :], 0), 1)
    slot_times = jnp.sum(jnp.where(packing, owner_times[None, :], 0), 1).astype(jnp.float32)
    packing_low = packing.astype(jnp.bfloat16)
    send_in = jnp.einsum(
        "wj,jpd->wpd", outgoing, latents, preferred_element_type=jnp.float32
    ).astype(jnp.bfloat16)
    send_up = jnp.einsum(
        "wj,jpd->wpd", outgoing, cotangent, preferred_element_type=jnp.float32
    ).astype(jnp.bfloat16)
    recv_in, recv_up = (
        lax.all_to_all(send_in, "wide", split_axis=0, concat_axis=0, tiled=True),
        lax.all_to_all(send_up, "wide", split_axis=0, concat_axis=0, tiled=True),
    )
    pack_in = jnp.einsum(
        "cw,wpd->cpd", packing_low, recv_in, preferred_element_type=jnp.float32
    ).astype(jnp.bfloat16)
    pack_up = jnp.einsum(
        "cw,wpd->cpd", packing_low, recv_up, preferred_element_type=jnp.float32
    ).astype(jnp.bfloat16)
    full_in, full_up = (
        lax.all_gather(pack_in, "narrow", axis=2, tiled=True),
        lax.all_gather(pack_up, "narrow", axis=2, tiled=True),
    )
    inputs = full_in.astype(jnp.float32)
    upstream = full_up.astype(jnp.float32)
    width = inputs.shape[2]
    share = width // lax.axis_size("narrow")
    quarter = tokens_per // 4
    blocks = capacity * 4

    def cond_local(first_w, second_w, ada_w, ada_b):
        return condition(slot_times, first_w, second_w, ada_w, ada_b)

    modulation, cond_back = jax.vjp(cond_local, time_in, time_out, ada_weight, ada_bias)
    gate_attn = modulation[:, None, 2 * width : 3 * width]
    gate_ffn = modulation[:, None, 5 * width : 6 * width]
    grouped = pre_attention(inputs, modulation, attn_kernel)
    grouped_low = grouped.astype(jnp.bfloat16).reshape(blocks, quarter, width)
    project, attention, attention_low, context = attend(grouped_low, qkv_weight)
    partial_attn = jnp.einsum(
        "nqe,ed->nqd", context, out_weight, preferred_element_type=jnp.float32
    )
    attended = lax.psum(partial_attn.astype(jnp.bfloat16), "narrow").astype(jnp.float32)
    attended_tok = shuffle(attended.reshape(capacity, 4, quarter, width), SIDE)
    middle = inputs + gate_attn * attended_tok
    second = modulate(middle, modulation, 3).astype(jnp.bfloat16)
    hidden = jnp.einsum("cpd,df->cpf", second, up_weight, preferred_element_type=jnp.float32)
    active = hidden_act(hidden, ffn_kernel).astype(jnp.bfloat16)
    partial_ffn = jnp.einsum("cpf,fd->cpd", active, down_weight, preferred_element_type=jnp.float32)
    fed = lax.psum(partial_ffn.astype(jnp.bfloat16), "narrow").astype(jnp.float32)
    outputs = middle + gate_ffn * fed
    gate_ffn_grad = jnp.sum(fed * upstream, 1)
    out_part = lax.dynamic_slice_in_dim(outputs, narrow_at * share, share, 2).astype(jnp.bfloat16)
    grad_fed = (gate_ffn * upstream).astype(jnp.bfloat16)

    def second_local(values, mods):
        return modulate(values, mods, 3)

    second_full, second_back = jax.vjp(second_local, middle, modulation)
    second = second_full.astype(jnp.bfloat16)
    hidden = jnp.einsum("cpd,df->cpf", second, up_weight, preferred_element_type=jnp.float32)
    active_full, active_back = jax.vjp(hidden_act, hidden, ffn_kernel)
    active = active_full.astype(jnp.bfloat16)
    down_grad = jnp.einsum("cpf,cpd->fd", active, grad_fed, preferred_element_type=jnp.float32)
    grad_active = jnp.einsum(
        "cpd,fd->cpf", grad_fed, down_weight, preferred_element_type=jnp.float32
    ).astype(jnp.bfloat16)
    grad_hidden_full, ffn_kernel_grad = active_back(grad_active.astype(jnp.float32))
    grad_hidden = grad_hidden_full.astype(jnp.bfloat16)
    up_grad = jnp.einsum("cpd,cpf->df", second, grad_hidden, preferred_element_type=jnp.float32)
    partial_second = jnp.einsum(
        "cpf,df->cpd", grad_hidden, up_weight, preferred_element_type=jnp.float32
    )
    grad_second = lax.psum(partial_second.astype(jnp.bfloat16), "narrow").astype(jnp.float32)
    grad_middle_norm, mod_grad_ffn = second_back(grad_second)
    grad_middle = upstream + grad_middle_norm
    gate_attn_grad = jnp.sum(attended_tok * grad_middle, 1)
    grad_attended = (gate_attn * grad_middle).reshape(capacity, SIDE, SIDE, width)
    grad_rows = unshuffle(grad_attended).reshape(blocks, quarter, width).astype(jnp.bfloat16)
    grouped, pre_back = jax.vjp(pre_attention, inputs, modulation, attn_kernel)
    grouped_low = grouped.astype(jnp.bfloat16).reshape(blocks, quarter, width)
    project, attention, attention_low, context = attend(grouped_low, qkv_weight)
    head_count = qkv_weight.shape[2] // HEAD_DIM
    factor = 1.0 / math.sqrt(HEAD_DIM)
    out_grad = jnp.einsum("nqe,nqd->ed", context, grad_rows, preferred_element_type=jnp.float32)
    grad_context = jnp.einsum(
        "nqd,ed->nqe", grad_rows, out_weight, preferred_element_type=jnp.float32
    )
    grad_context = grad_context.astype(jnp.bfloat16).reshape(blocks, quarter, head_count, HEAD_DIM)
    grad_value = jnp.einsum(
        "nhqk,nqhe->nkhe", attention_low, grad_context, preferred_element_type=jnp.float32
    ).astype(jnp.bfloat16)
    grad_probs = jnp.einsum(
        "nqhe,nkhe->nhqk", grad_context, project[2], preferred_element_type=jnp.float32
    )
    grad_probs = lax.optimization_barrier(grad_probs.astype(jnp.bfloat16)).astype(jnp.float32)
    grad_scores = attention * (grad_probs - jnp.sum(attention * grad_probs, -1, keepdims=True))
    grad_scores = grad_scores.astype(jnp.bfloat16)
    grad_query = (
        jnp.einsum("nhqk,nkhe->nqhe", grad_scores, project[1], preferred_element_type=jnp.float32)
        * factor
    ).astype(jnp.bfloat16)
    grad_key = (
        jnp.einsum("nhqk,nqhe->nkhe", grad_scores, project[0], preferred_element_type=jnp.float32)
        * factor
    ).astype(jnp.bfloat16)
    grad_project = jnp.stack([grad_query, grad_key, grad_value]).reshape(
        3, blocks, quarter, head_count * HEAD_DIM
    )
    qkv_grad = jnp.einsum(
        "nqd,tnqe->tde", grouped_low, grad_project, preferred_element_type=jnp.float32
    )
    partial_grouped = jnp.einsum(
        "tnqe,tde->nqd", grad_project, qkv_weight, preferred_element_type=jnp.float32
    )
    grad_grouped = lax.psum(partial_grouped.astype(jnp.bfloat16), "narrow").astype(jnp.float32)
    grad_inputs, mod_grad_attn, attn_kernel_grad = pre_back(
        grad_grouped.reshape(capacity, 4, quarter, width)
    )
    input_full = grad_middle + grad_inputs
    blank = jnp.zeros((capacity, width), jnp.float32)
    mod_grad = (
        mod_grad_attn
        + mod_grad_ffn
        + jnp.concatenate([blank, blank, gate_attn_grad, blank, blank, gate_ffn_grad], 1)
    )
    grad_part = lax.dynamic_slice_in_dim(
        input_full.astype(jnp.bfloat16), narrow_at * share, share, 2
    )
    back_out = jnp.einsum(
        "cw,cpd->wpd", packing_low, out_part, preferred_element_type=jnp.float32
    ).astype(jnp.bfloat16)
    back_grad = jnp.einsum(
        "cw,cpd->wpd", packing_low, grad_part, preferred_element_type=jnp.float32
    ).astype(jnp.bfloat16)
    home_out, home_grad = (
        lax.all_to_all(back_out, "wide", split_axis=0, concat_axis=0, tiled=True),
        lax.all_to_all(back_grad, "wide", split_axis=0, concat_axis=0, tiled=True),
    )
    final_out = jnp.einsum(
        "wj,wpd->jpd", outgoing, home_out, preferred_element_type=jnp.float32
    ).astype(jnp.bfloat16)
    final_grad = jnp.einsum(
        "wj,wpd->jpd", outgoing, home_grad, preferred_element_type=jnp.float32
    ).astype(jnp.bfloat16)
    factor_sum = 1.0 / latent_total
    cond_grads = cond_back(mod_grad)
    summed = (
        lax.psum((qkv_grad * factor_sum).astype(jnp.bfloat16), "wide").astype(jnp.float32),
        lax.psum((out_grad * factor_sum).astype(jnp.bfloat16), "wide").astype(jnp.float32),
        lax.psum((up_grad * factor_sum).astype(jnp.bfloat16), "wide").astype(jnp.float32),
        lax.psum((ffn_kernel_grad * factor_sum).astype(jnp.bfloat16), "wide").astype(jnp.float32),
        lax.psum((down_grad * factor_sum).astype(jnp.bfloat16), "wide").astype(jnp.float32),
        lax.psum((attn_kernel_grad * factor_sum).astype(jnp.bfloat16), "wide").astype(jnp.float32),
        lax.psum((cond_grads[0] * factor_sum).astype(jnp.bfloat16), "wide").astype(jnp.float32),
        lax.psum((cond_grads[1] * factor_sum).astype(jnp.bfloat16), "wide").astype(jnp.float32),
        lax.psum((cond_grads[2] * factor_sum).astype(jnp.bfloat16), "wide").astype(jnp.float32),
        lax.psum((cond_grads[3] * factor_sum).astype(jnp.bfloat16), "wide").astype(jnp.float32),
    )
    time_in_grad, time_out_grad, ada_weight_grad, ada_bias_grad = (
        summed[6],
        summed[7],
        summed[8],
        summed[9],
    )
    return (
        final_out,
        final_grad,
        time_in_grad,
        time_out_grad,
        ada_weight_grad,
        ada_bias_grad,
        summed[5],
        summed[0],
        summed[1],
        summed[2],
        summed[3],
        summed[4],
    )


def solution(mesh):
    return jax.shard_map(
        body,
        mesh=mesh,
        in_specs=(
            P("wide", None, "narrow"),
            P("wide", None, "narrow"),
            P(),
            P(),
            P(),
            P(),
            P(),
            P(),
            P(None, None, "narrow"),
            P("narrow", None),
            P(None, "narrow"),
            P(None, "narrow"),
            P("narrow", None),
        ),
        out_specs=(
            P("wide", None, "narrow"),
            P("wide", None, "narrow"),
            P(),
            P(),
            P(),
            P(),
            P(),
            P(None, None, "narrow"),
            P("narrow", None),
            P(None, "narrow"),
            P(None, "narrow"),
            P("narrow", None),
        ),
        check_vma=False,
    )
```

profile of v0, /device:TPU:0, one launch (start us, length us, event | category | flops | bytes accessed | tf_op | source)
XLA Modules:
  0.0 1158.2 jit_solution(13615977940565312786)
XLA Ops:
  10.7 7.3 all-to-all-start
  20.2 17.9 %all-to-all-done = bf16[8,256,192]{1,2,0:T(8,128)(2,1)S(1)} async-done(((bf16[8,256,192]{1,2,0:T(8,128)(2,1)}), bf16[8,256,192]{1,2,0:T(8,128)(2,1)S(1)}, u32[]{:S(2)}, u32[]{:S(2)}) %all-to-all-start) | async-done | bytes 786464 | tf_op jit(solution)/shard_map/all_to_all | solution.py:143
  41.3 4.2 all-to-all-start.2
  50.6 9.9 convolution_add_fusion
  61.1 6.2 all-gather.3.cloned.1.call-done
  76.5 6.6 copy.422
  83.2 22.2 %add_convert_fusion.1 = bf16[8,16,16,768]{3,2,1,0:T(8,128)(2,1)} fusion(f32[8,16,16,768]{3,2,1,0:T(8,128)} %bitcast.161, f32[768]{0:T(1024)S(1)} %get-tuple-element.134, f32[768]{0:T(1024)S(1)} %get-tuple-element.135, f32[768]{0:T(1024)S(1)} %get-tuple-element.128, f32[768]{0:T(1024)S(1)} %get-tuple-element.129, f32[768]{0:T(1024)S(1)} %get-tuple-element.130, ...), kind=kLoop, calls=%fused_computation.100 | loop fusion | flops 28311552 | bytes 9464832 | tf_op jit(solution)/shard_map/convert_element_type | solution.py:170
  121.5 4.9 fusion.129
  135.2 5.1 copy.433
  143.9 65.1 %all-reduce.50.cloned.1.call-done = bf16[8,256,768]{1,2,0:T(8,128)(2,1)} async-done(((bf16[8,256,768]{1,2,0:T(8,128)(2,1)}), bf16[8,256,768]{1,2,0:T(8,128)(2,1)}) %all-reduce.50.cloned.1.call-update) | async-done | bytes 3145744 | tf_op jit(solution)/shard_map/psum | solution.py:175
  209.0 4.5 fusion.126
  215.7 6.2 fusion.61
  221.9 22.4 %multiply_add_fusion = f32[8,16,16,768]{3,2,1,0:T(8,128)} fusion(f32[8,16,16,768]{3,2,1,0:T(8,128)} %bitcast.165, f32[768]{0:T(1024)} %get-tuple-element.125, f32[768]{0:T(1024)} %get-tuple-element.126, f32[768]{0:T(1024)} %get-tuple-element.119, f32[768]{0:T(1024)} %get-tuple-element.120, f32[768]{0:T(1024)} %get-tuple-element.121, ...), kind=kLoop, calls=%fused_computation.97 | loop fusion | flops 26738688 | bytes 12610560 | tf_op jit(solution)/shard_map/add | solution.py:28
  244.3 27.4 %broadcast_multiply_fusion = (f32[8,16,16,768]{3,2,1,0:T(8,128)}, f32[8,16,16,768]{3,2,1,0:T(8,128)}, f32[8,16,16,768]{3,2,1,0:T(8,128)}, f32[8,16,16,768]{3,2,1...) fusion(f32[768]{0:T(1024)} %get-tuple-element.125, ...), kind=kOutput, calls=%fused_computation.111 | convolution fusion | flops 2467823616 | bytes 73583616 | tf_op jit(solution)/shard_map/cpd,fd->cpf/dot_general | solution.py:197
  271.7 14.1 %pad_add_fusion.1 = f32[8,18,18,768]{3,2,1,0:T(8,128)} fusion(f32[8,16,16,768]{3,2,1,0:T(8,128)} %get-tuple-element.172, f32[8,16,16,768]{3,2,1,0:T(8,128)} %get-tuple-element.171, f32[8,16,16,768]{3,2,1,0:T(8,128)} %get-tuple-element.170, f32[8,16,16,768]{3,2,1,0:T(8,128)} %get-tuple-element.169), kind=kLoop, calls=%fused_computation.19 | loop fusion | flops 5971968 | bytes 33128448 | tf_op jit(solution)/shard_map/transpose(jvp())/add_any | solution.py:28
  285.8 14.9 %fusion.27 = bf16[8,16,16,768]{3,2,1,0:T(8,128)(2,1)S(1)} fusion(f32[8,16,16,768]{3,2,1,0:T(8,128)} %get-tuple-element.177, f32[8,16,16,768]{3,2,1,0:T(8,128)} %get-tuple-element.176, f32[8,16,16,768]{3,2,1,0:T(8,128)} %get-tuple-element.175, f32[8,16,16,768]{3,2,1,0:T(8,128)} %get-tuple-element.174, f32[8,16,16,768]{3,2,1,0:T(8,128)} %get-tuple-element.173, ...), kind=kLoop, calls=%fused_computation.70 | loop fusion | flops 9437184 | bytes 40894464 | tf_op jit(solution)/shard_map/convert.5
  302.5 4.0 convolution_convert_fusion
  312.0 4.1 convolution_convert_fusion.1
  316.1 59.1 %all-reduce.52.cloned.1.call-done = bf16[8,256,768]{1,2,0:T(8,128)(2,1)} async-done(((bf16[8,256,768]{1,2,0:T(8,128)(2,1)}), bf16[8,256,768]{1,2,0:T(8,128)(2,1)}) %all-reduce.52.cloned.1.call-update) | async-done | bytes 3145744 | tf_op jit(solution)/shard_map/psum | solution.py:206
  375.2 4.7 fusion.11
  379.9 7.4 fusion.26
  387.3 4.8 fusion.12
  397.0 5.1 copy.446
  412.3 4.6 convolution_convert_fusion.3
  435.4 4.7 bitcast_convert_fusion
  443.8 7.7 fusion.42
  451.5 6.4 fusion.43
  460.0 4.2 fusion.57
  467.5 96.1 %all-reduce.56.cloned.1.call-done = (bf16[8,256,768]{1,2,0:T(8,128)(2,1)}, bf16[8,8,2,8,2,768]{5,0,4,3,2,1:T(8,128)(2,1)}) async-done(((bf16[8,256,768]{1,2,0:T(8,128)(2,1)}, bf16[8,8,2,8,2,768]{5,0,4,3,2,1:T(8,128)(2,1)}), (bf16[8,256,768]{1,2,0:T(8,128)(2,1)}, bf16[8,8,2,8,2,768]{5,0,4,3,2,1:T(8,128)(2,1)})) %all-reduce.56.cloned.1.call-update) | async-done | bytes 6291472 | tf_op jit(solution)/shard_map/psum | solution.py:182
  563.5 4.0 fusion.25
  568.4 5.5 transpose.109
  574.0 6.6 copy.487
  580.7 36.7 %multiply_reduce_fusion.17 = (f32[768]{0:T(1024)}, f32[768]{0:T(1024)}, f32[768]{0:T(1024)}, f32[768]{0:T(1024)}, f32[768]{0:T(1024)}, /*index=5*/f32[768]{0:T(1...) fusion(f32[8,16,16,768]{3,2,1,0:T(8,128)} %bitcast.162, ...), kind=kLoop, calls=%fused_computation.95 | loop fusion | flops 39315456 | bytes 69258240 | tf_op jit(solution)/shard_map/transpose(jvp())/reduce_sum | solution.py:28
  617.3 10.5 pad_add_fusion
  627.9 19.9 %fusion.124 = (f32[8,768]{1,0:T(8,128)S(1)}, f32[8,16,16,768]{3,2,1,0:T(8,128)}) fusion(f32[8,16,16,768]{3,2,1,0:T(8,128)} %get-tuple-element.160, f32[8,16,16,768]{3,2,1,0:T(8,128)} %get-tuple-element.167, f32[8,16,16,768]{3,2,1,0:T(8,128)} %get-tuple-element.161, f32[8,16,16,768]{3,2,1,0:T(8,128)} %get-tuple-element.162, ...), kind=kLoop, calls=%fused_computation.281 | loop fusion | flops 11003904 | bytes 50356224 | tf_op jit(solution)/shard_map/transpose(jvp())/reduce_sum | solution.py:64
  647.8 6.6 copy.472
  654.5 8.3 fusion.10
  664.8 17.6 %fusion.123 = f32[8,768]{1,0:T(8,128)S(1)} fusion(f32[768,4608]{1,0:T(8,128)} %param.18, f32[8,768]{0,1:T(8,128)} %copy.526, f32[8,1536]{0,1:T(8,128)S(1)} %broadcast.263, f32[8,768]{0,1:T(8,128)S(1)} %copy.525, f32[8,768]{0,1:T(8,128)} %copy.524, f32[8,768]{0,1:T(8,128)} %copy.523, f32[8,768]{0,1:T(8,128)} %copy.478, f32[8,768]{0,1:T(8,128)} %copy.522), kind=kOutput, calls=%fused_computation.280 | convolution fusion | flops 339996672 | bytes 14376960 | tf_op jit(solution)/shard_map/transpose(jvp())/dot_general | solution.py:57
  687.5 17.0 %multiply_convert_fusion = bf16[768,4608]{1,0:T(8,128)(2,1)} fusion(f32[8,768]{1,0:T(8,128)S(1)} %copy-done.42, f32[8,768]{0,1:T(8,128)S(1)} %copy-done.15, f32[8,1536]{0,1:T(8,128)S(1)} %broadcast.263, f32[8,768]{0,1:T(8,128)S(1)} %copy.525, f32[8,768]{0,1:T(8,128)S(1)} %copy-done.13, f32[8,768]{0,1:T(8,128)S(1)} %copy-done.11, ...), kind=kOutput, calls=%fused_computation.17 | convolution fusion | flops 347099136 | bytes 7299072 | tf_op jit(solution)/shard_map/transpose(jvp())/dot_general | solution.py:57
  709.7 4.9 fusion.125
  719.4 6.0 all-to-all-start.3
  725.4 21.9 %multiply_reduce_fusion.8 = (f32[768]{0:T(1024)}, f32[768]{0:T(1024)}, f32[768]{0:T(1024)}, f32[768]{0:T(1024)}, f32[768]{0:T(1024)S(1)}, /*index=5*/f32[768]{0:T(1024)S(1)}, f32[768]{0:T(1024)S(1)}, f32[768]{0:T(1024)S(1)}) fusion(f32[8,16,16,768]{3,2,1,0:T(8,128)} %bitcast.160, f32[8,16,16,768]{3,2,1,0:T(8,128)} %bitcast.166), kind=kLoop, calls=%fused_computation.86 | loop fusion | flops 25159680 | bytes 12607488 | tf_op jit(solution)/shard_map/transpose(jvp())/reduce_sum | solution.py:28
  749.0 19.0 %all-to-all-done.3 = bf16[8,256,192]{1,2,0:T(8,128)(2,1)} async-done(((bf16[8,256,192]{1,2,0:T(8,128)(2,1)}), bf16[8,256,192]{1,2,0:T(8,128)(2,1)}, u32[]{:S(2)}, u32[]{:S(2)}) %all-to-all-start.3) | async-done | bytes 786464 | tf_op jit(solution)/shard_map/all_to_all | solution.py:270
  768.1 4.2 all-to-all-start.1
  772.5 5.7 multiply_reduce_fusion.4
  779.9 57.0 %all-reduce.42 = (bf16[4608]{0:T(1024)(128)(2,1)S(1)}, bf16[9,768]{1,0:T(8,128)(2,1)S(1)}, bf16[9,768]{1,0:T(8,128)(2,1)S(1)}) all-reduce(bf16[4608]{0:T(1024)(128)(2,1)S(1)} %multiply_convert_fusion.7, bf16[9,768]{1,0:T(8,128)(2,1)} %get-tuple-element.195, ...), channel_id=1, replica_groups=mesh['wide'=8,'narrow'=4] {'wide'}, use_global_device_ids=true, to_apply=%region_29.30 | all-reduce | flops 18432 | bytes 73728 | tf_op jit(solution)/shard_map/psum | solution.py:290
  843.9 287.1 %all-reduce.54.cloned.1.call-done = (bf16[256,768]{1,0:T(8,128)(2,1)}, bf16[768,768]{1,0:T(8,128)(2,1)}, bf16[768,4608]{1,0:T(8,128)(2,1)}, bf16[3,768,192]{1,2,...) async-done(((bf16[256,768]{1,0:T(8,128)(2,1)}, bf16[768,768]{1,0:T(8,128)(2,1)}, bf16[768,4608]{1,0:T(8,128)(2,1)}, ...) | async-done | bytes 12189712 | tf_op jit(solution)/shard_map/psum | solution.py:287
  1143.9 7.2 convert_element_type.289
  (371 shorter events, 144.3 us)
Async XLA Ops:
  7.2 42.1 %copy-start = (f32[768,768]{1,0:T(8,128)S(1)}, f32[768,768]{1,0:T(8,128)}, u32[]{:S(2)}) copy-start(f32[768,768]{1,0:T(8,128)} %param.17) | copy-start | bytes 7077892
  7.2 32.5 %copy-start.43 = (bf16[4,256,192]{1,2,0:T(8,128)(2,1)S(1)}, bf16[4,256,192]{1,2,0:T(8,128)(2,1)}, u32[]{:S(2)}) copy-start(bf16[4,256,192]{1,2,0:T(8,128)(2,1)} %param.14) | copy-start | bytes 1179652
  8.1 42.4 %copy-start.112 = (s32[4]{0:T(128)}, s32[4]{0:T(128)S(1)}, u32[]{:S(2)}) copy-start(s32[4]{0:T(128)S(1)} %dynamic_slice.9) | copy-start | bytes 52
  10.7 27.5 %all-to-all-start = ((bf16[8,256,192]{1,2,0:T(8,128)(2,1)}), bf16[8,256,192]{1,2,0:T(8,128)(2,1)S(1)}, u32[]{:S(2)}, u32[]{:S(2)}) async-start(bf16[8,256,192]{1,2,0:T(8,128)(2,1)} %copy.418), calls=%async_computation | async-start | bytes 1572864 | tf_op jit(solution)/shard_map/all_to_all | solution.py:143
  18.0 49.4 %all-gather.3.cloned.1.call-start = ((), (), s32[]{:S(2)}) async-start(), calls=%async_computation.4 | async-start | bytes 3932160 | tf_op jit(solution)/shard_map/all_gather | solution.py:153
  19.5 120.9 %copy-start.106 = (pred[8]{0:T(512)(128)(4,1)}, pred[8]{0:T(512)(128)(4,1)S(1)}, u32[]{:S(2)}) copy-start(pred[8]{0:T(512)(128)(4,1)S(1)} %broadcast_compare_fusion) | copy-start | bytes 28
  20.2 120.2 %copy-start.109 = (s32[8]{0:T(128)}, s32[8]{0:T(128)S(1)}, u32[]{:S(2)}) copy-start(s32[8]{0:T(128)S(1)} %bitcast_subtract_fusion) | copy-start | bytes 100
  41.3 99.1 %all-to-all-start.2 = ((bf16[8,256,192]{1,2,0:T(8,128)(2,1)}), bf16[8,256,192]{1,2,0:T(8,128)(2,1)}, u32[]{:S(2)}, u32[]{:S(2)}) async-start(bf16[8,256,192]{1,2,0:T(8,128)(2,1)} %copy.440), calls=%async_computation.2 | async-start | bytes 1572864 | tf_op jit(solution)/shard_map/all_to_all | solution.py:144
  45.5 163.4 %all-reduce.50.cloned.1.call-start = ((), (), s32[]{:S(2)}) async-start(), calls=%async_computation.5 | async-start | bytes 6291456 | tf_op jit(solution)/shard_map/psum | solution.py:175
  46.8 36.3 %copy-start.66 = (f32[768]{0:T(1024)}, f32[768]{0:T(1024)S(1)}, u32[]{:S(2)}) copy-start(f32[768]{0:T(1024)S(1)} %get-tuple-element.127) | copy-start | bytes 9220
  46.8 36.3 %copy-start.68 = (f32[768]{0:T(1024)}, f32[768]{0:T(1024)S(1)}, u32[]{:S(2)}) copy-start(f32[768]{0:T(1024)S(1)} %get-tuple-element.128) | copy-start | bytes 9220
  46.8 36.3 %copy-start.70 = (f32[768]{0:T(1024)}, f32[768]{0:T(1024)S(1)}, u32[]{:S(2)}) copy-start(f32[768]{0:T(1024)S(1)} %get-tuple-element.129) | copy-start | bytes 9220
  46.8 36.3 %copy-start.72 = (f32[768]{0:T(1024)}, f32[768]{0:T(1024)S(1)}, u32[]{:S(2)}) copy-start(f32[768]{0:T(1024)S(1)} %get-tuple-element.130) | copy-start | bytes 9220
  46.8 36.3 %copy-start.74 = (f32[768]{0:T(1024)}, f32[768]{0:T(1024)S(1)}, u32[]{:S(2)}) copy-start(f32[768]{0:T(1024)S(1)} %get-tuple-element.131) | copy-start | bytes 9220
  46.8 36.3 %copy-start.76 = (f32[768]{0:T(1024)}, f32[768]{0:T(1024)S(1)}, u32[]{:S(2)}) copy-start(f32[768]{0:T(1024)S(1)} %get-tuple-element.132) | copy-start | bytes 9220
  46.9 36.3 %copy-start.78 = (f32[768]{0:T(1024)}, f32[768]{0:T(1024)S(1)}, u32[]{:S(2)}) copy-start(f32[768]{0:T(1024)S(1)} %get-tuple-element.133) | copy-start | bytes 9220
  46.9 36.3 %copy-start.80 = (f32[768]{0:T(1024)}, f32[768]{0:T(1024)S(1)}, u32[]{:S(2)}) copy-start(f32[768]{0:T(1024)S(1)} %get-tuple-element.134) | copy-start | bytes 9220
  46.9 36.3 %copy-start.82 = (f32[768]{0:T(1024)}, f32[768]{0:T(1024)S(1)}, u32[]{:S(2)}) copy-start(f32[768]{0:T(1024)S(1)} %get-tuple-element.135) | copy-start | bytes 9220
  61.1 15.4 %copy-start.38 = (f32[8,768]{1,0:T(8,128)}, f32[8,768]{1,0:T(8,128)S(1)}, u32[]{:S(2)}) copy-start(f32[8,768]{1,0:T(8,128)S(1)} %get-tuple-element.185) | copy-start | bytes 73732
  61.1 15.4 %copy-start.48 = (f32[8,768]{1,0:T(8,128)}, f32[8,768]{1,0:T(8,128)S(1)}, u32[]{:S(2)}) copy-start(f32[8,768]{1,0:T(8,128)S(1)} %get-tuple-element.184) | copy-start | bytes 73732
  61.1 147.9 %copy-start.52 = (f32[8,768]{1,0:T(8,128)}, f32[8,768]{1,0:T(8,128)S(1)}, u32[]{:S(2)}) copy-start(f32[8,768]{1,0:T(8,128)S(1)} %get-tuple-element.186) | copy-start | bytes 73732
  61.1 153.1 %copy-start.44 = (f32[8,768]{1,0:T(8,128)}, f32[8,768]{1,0:T(8,128)S(1)}, u32[]{:S(2)}) copy-start(f32[8,768]{1,0:T(8,128)S(1)} %get-tuple-element.183) | copy-start | bytes 73732
  61.1 153.1 %copy-start.85 = (f32[8,768]{1,0:T(8,128)}, f32[8,768]{1,0:T(8,128)S(1)}, u32[]{:S(2)}) copy-start(f32[8,768]{1,0:T(8,128)S(1)} %get-tuple-element.182) | copy-start | bytes 73732
  140.4 103.9 %all-gather.5.cloned.1.call-start = ((), (), s32[]{:S(2)}) async-start(), calls=%async_computation.6 | async-start | bytes 3932160 | tf_op jit(solution)/shard_map/all_gather | solution.py:154
  143.1 232.0 %all-reduce.52.cloned.1.call-start = ((), (), s32[]{:S(2)}) async-start(), calls=%async_computation.7 | async-start | bytes 6291456 | tf_op jit(solution)/shard_map/psum | solution.py:206
  221.9 22.4 %copy-start.31 = (bf16[768,768]{1,0:T(8,128)(2,1)S(1)}, bf16[768,768]{1,0:T(8,128)(2,1)}, u32[]{:S(2)}) copy-start(bf16[768,768]{1,0:T(8,128)(2,1)} %param.25) | copy-start | bytes 3538948
  285.8 16.6 %copy-start.115 = (bf16[768,768]{1,0:T(8,128)(2,1)S(1)}, bf16[768,768]{1,0:T(8,128)(2,1)}, u32[]{:S(2)}) copy-start(bf16[768,768]{1,0:T(8,128)(2,1)} %param.23) | copy-start | bytes 3538948
  306.5 257.1 %all-reduce.56.cloned.1.call-start = ((), (), s32[]{:S(2)}) async-start(), calls=%async_computation.9 | async-start | bytes 12582912 | tf_op jit(solution)/shard_map/psum | solution.py:182
  316.1 63.8 %copy-start.45 = (f32[8,768]{1,0:T(8,128)S(1)}, f32[8,768]{1,0:T(8,128)}, u32[]{:S(2)}) copy-start(f32[8,768]{1,0:T(8,128)} %copy-done.44) | copy-start | bytes 73732
  316.1 63.8 %copy-start.65 = (f32[8,256]{1,0:T(8,128)S(1)}, f32[8,256]{1,0:T(8,128)}, u32[]{:S(2)}) copy-start(f32[8,256]{1,0:T(8,128)} %copy-done.64) | copy-start | bytes 24580
  375.2 12.2 %slice-start = ((s8[6291456]{0:T(1024)(128)(4,1)}), s8[4194304]{0:T(1024)(128)(4,1)S(1)}, s32[]{:S(2)}) async-start(s8[6291456]{0:T(1024)(128)(4,1)} %bitcast.158), calls=%async_computation.10 | async-start | bytes 8388608
  424.7 15.4 %copy-start.32 = (bf16[1,32,64,192]{3,2,0,1:T(8,128)(2,1)}, bf16[1,32,64,192]{3,2,0,1:T(8,128)(2,1)S(1)}, u32[]{:S(2)}) copy-start(bf16[1,32,64,192]{3,2,0,1:T(8,128)(2,1)S(1)} %copy.461) | copy-start | bytes 2359300
  443.5 687.5 %all-reduce.54.cloned.1.call-start = ((), (), s32[]{:S(2)}) async-start(), calls=%async_computation.8 | async-start | bytes 24379392 | tf_op jit(solution)/shard_map/psum | solution.py:287
  664.7 17.6 %copy-start.42 = (f32[8,768]{1,0:T(8,128)S(1)}, f32[8,768]{1,0:T(8,128)}, u32[]{:S(2)}) copy-start(f32[8,768]{1,0:T(8,128)} %copy-done.41) | copy-start | bytes 73732
  664.7 19.6 %copy-start.51 = (f32[8,768]{1,0:T(8,128)S(1)}, f32[8,768]{1,0:T(8,128)}, u32[]{:S(2)}) copy-start(f32[8,768]{1,0:T(8,128)} %copy-done.50) | copy-start | bytes 73732
  664.7 22.8 %copy-start.11 = (f32[8,768]{0,1:T(8,128)S(1)}, f32[8,768]{0,1:T(8,128)}, u32[]{:S(2)}) copy-start(f32[8,768]{0,1:T(8,128)} %copy.523) | copy-start | bytes 73732
  664.7 22.7 %copy-start.13 = (f32[8,768]{0,1:T(8,128)S(1)}, f32[8,768]{0,1:T(8,128)}, u32[]{:S(2)}) copy-start(f32[8,768]{0,1:T(8,128)} %copy.524) | copy-start | bytes 73732
  664.8 22.7 %copy-start.15 = (f32[8,768]{0,1:T(8,128)S(1)}, f32[8,768]{0,1:T(8,128)}, u32[]{:S(2)}) copy-start(f32[8,768]{0,1:T(8,128)} %copy.526) | copy-start | bytes 73732
  664.8 22.7 %copy-start.17 = (f32[8,768]{0,1:T(8,128)S(1)}, f32[8,768]{0,1:T(8,128)}, u32[]{:S(2)}) copy-start(f32[8,768]{0,1:T(8,128)} %copy.522) | copy-start | bytes 73732
  664.8 22.7 %copy-start.19 = (f32[8,768]{0,1:T(8,128)S(1)}, f32[8,768]{0,1:T(8,128)}, u32[]{:S(2)}) copy-start(f32[8,768]{0,1:T(8,128)} %copy.478) | copy-start | bytes 73732
  687.5 17.0 %copy-start.102 = (f32[8,128]{1,0:T(8,128)S(1)}, f32[8,128]{1,0:T(8,128)}, u32[]{:S(2)}) copy-start(f32[8,128]{1,0:T(8,128)} %copy-done.101) | copy-start | bytes 12292
  687.5 17.0 %copy-start.104 = (f32[8,128]{1,0:T(8,128)S(1)}, f32[8,128]{1,0:T(8,128)}, u32[]{:S(2)}) copy-start(f32[8,128]{1,0:T(8,128)} %copy-done.103) | copy-start | bytes 12292
  719.4 48.7 %all-to-all-start.3 = ((bf16[8,256,192]{1,2,0:T(8,128)(2,1)}), bf16[8,256,192]{1,2,0:T(8,128)(2,1)}, u32[]{:S(2)}, u32[]{:S(2)}) async-start(bf16[8,256,192]{1,2,0:T(8,128)(2,1)} %copy.474), calls=%async_computation.3 | async-start | bytes 1572864 | tf_op jit(solution)/shard_map/all_to_all | solution.py:270
  725.4 22.0 %copy-start.27 = (bf16[8,256,192]{1,2,0:T(8,128)(2,1)S(1)}, bf16[8,256,192]{1,2,0:T(8,128)(2,1)}, u32[]{:S(2)}) copy-start(bf16[8,256,192]{1,2,0:T(8,128)(2,1)} %get-tuple-element.193) | copy-start | bytes 2359300
  725.4 22.0 %copy-start.108 = (pred[8]{0:T(512)(128)(4,1)S(1)}, pred[8]{0:T(512)(128)(4,1)}, u32[]{:S(2)}) copy-start(pred[8]{0:T(512)(128)(4,1)} %copy-done.106) | copy-start | bytes 28
  725.4 22.0 %copy-start.111 = (s32[8]{0:T(128)S(1)}, s32[8]{0:T(128)}, u32[]{:S(2)}) copy-start(s32[8]{0:T(128)} %copy-done.109) | copy-start | bytes 100
  768.1 73.3 %all-to-all-start.1 = ((bf16[8,256,192]{1,2,0:T(8,128)(2,1)}), bf16[8,256,192]{1,2,0:T(8,128)(2,1)}, u32[]{:S(2)}, u32[]{:S(2)}) async-start(bf16[8,256,192]{1,2,0:T(8,128)(2,1)} %copy.437), calls=%async_computation.1 | async-start | bytes 1572864 | tf_op jit(solution)/shard_map/all_to_all | solution.py:269
  1131.1 12.8 %slice-start.2 = ((s8[7077888]{0:T(1024)(128)(4,1)}), s8[4194304]{0:T(1024)(128)(4,1)S(1)}, s32[]{:S(2)}) async-start(s8[7077888]{0:T(1024)(128)(4,1)} %bitcast.177), calls=%async_computation.12 | async-start | bytes 8388608
  (83 other events, 470.3 us)
Sparse Core Ops, SparseCore 0:
  39.8 27.4 all-gather.2
  140.5 68.4 all-reduce.49
  211.1 28.6 all-gather.4
  306.6 68.5 all-reduce.51
  443.6 119.8 all-reduce.55
  706.3 424.7 all-reduce.53
where the time goes:
time: 1160 us
  waiting for transfers between devices  551 us (48%)
  other arithmetic  262 us (23%)
  matrix products  158 us (14%)
  local copies, waits for them, and re-layouts  92.2 us (8%)
  blocking collectives  57 us (5%)
  starting transfers between devices  22.2 us (2%)
  between operations  16.1 us (1%)
    psum x1, waiting for transfers between devices, body(): lax.psum((cond_grads[0] * factor_sum).astype(jnp.bfloat16), 'wide')  287 us
    psum x1, waiting for transfers between devices, body(): lax.psum(partial_ffn.astype(jnp.bfloat16), 'narrow').astype(jnp.float32)  96.1 us
    psum x1, waiting for transfers between devices, body(): lax.psum(partial_attn.astype(jnp.bfloat16), 'narrow').astype(jnp.float32)  65.1 us
    reduce_sum x3, other arithmetic, conv_taps(): padded[:, r:r + extent, c:c + extent, :] * kernel[3 * r + c]  64.3 us
    psum x1, waiting for transfers between devices, body(): lax.psum(partial_second.astype(jnp.bfloat16), 'narrow').astype(jnp.float32)  59.1 us
    psum x1, blocking collectives, body(): lax.psum((cond_grads[3] * factor_sum).astype(jnp.bfloat16), 'wide')  57 us
    dot_general x3, matrix products, condition(): return jnp.dot(outer, ada_weight, precision=HIGHEST) + ada_bias  44.5 us
    reduce_sum x3, other arithmetic, modulate(): return layer_norm(values) * (1.0 + scaled) + shifted  35.7 us
  transfers between devices with their start and end apart: 10, of which 7 were waited for; matrix products, arithmetic and copies ran while one was open for 18% of the time, Pallas kernels for 0%

commit v1 on v0

v1 whole, which is shorter than its diff:
```python
import functools
import math

import jax
import jax.numpy as jnp
from jax import lax
from jax.experimental import pallas as pl
from jax.experimental.pallas import tpu as pltpu
from jax.sharding import PartitionSpec as P

HEAD_DIM = 64
FREQ = 256
SIDE = 16
PAIR = 2

BF = jnp.bfloat16
F32 = jnp.float32
HIGHEST = lax.Precision.HIGHEST
LANES = 128
ROWS = 32
BAND = 64
GELU_A = math.sqrt(2.0 / math.pi)
GELU_B = 0.044715
EPS = 1e-06
VMEM_LIMIT = 56 * 1024 * 1024


def dot(a, b):
    return lax.dot_general(a, b, (((1,), (0,)), ((), ())), preferred_element_type=F32)


def dot_nt(a, b):
    return lax.dot_general(a, b, (((1,), (1,)), ((), ())), preferred_element_type=F32)


def dot_tn(a, b):
    return lax.dot_general(a, b, (((0,), (0,)), ((), ())), preferred_element_type=F32)


def column_of(rows):
    return lax.broadcasted_iota(jnp.int32, (rows, LANES), 0) % SIDE


def from_left(v):
    moved = pltpu.roll(v, 1, 0)
    return jnp.where(column_of(v.shape[0]) == 0, 0.0, moved)


def from_right(v):
    moved = pltpu.roll(v, v.shape[0] - 1, 0)
    return jnp.where(column_of(v.shape[0]) == SIDE - 1, 0.0, moved)


def conv_band(padded, at, lanes, kern):
    rows = [padded[at + SIDE * r : at + SIDE * r + BAND, lanes] for r in range(3)]
    mixed = [
        rows[0] * kern[c] + rows[1] * kern[3 + c] + rows[2] * kern[6 + c] for c in range(3)
    ]
    return from_left(mixed[0]) + mixed[1] + from_right(mixed[2])


def conv_back_band(padded_grad, at, lanes, kern):
    wide = padded_grad[at : at + BAND + 2 * SIDE, lanes]
    shifted = [from_right(wide), wide, from_left(wide)]
    total = None
    for r in range(3):
        for c in range(3):
            low = SIDE * (2 - r)
            term = shifted[c][low : low + BAND] * kern[3 * r + c]
            total = term if total is None else total + term
    return total, [s[SIDE : SIDE + BAND] for s in shifted]


def fold_rows(v):
    total = v[0:8]
    for at in range(8, v.shape[0], 8):
        total = total + v[at : at + 8]
    return total


def taps_of(kern_ref, lanes):
    block = kern_ref[:, lanes]
    return [block[t : t + 1] for t in range(9)]


def zero_edges(ref):
    edge = jnp.zeros((SIDE, ref.shape[1]), F32)
    ref[0:SIDE, :] = edge
    ref[ref.shape[0] - SIDE :, :] = edge


def gather_features(n, parts, held, width):
    for step, part in enumerate(parts):
        held[jnp.bitwise_xor(n, step)] = part[0]
    return jnp.concatenate([held[k] for k in range(len(parts))], axis=1)


def own_slice(n, values, share):
    out = values[:, 0:share]
    for k in range(1, values.shape[1] // share):
        out = jnp.where(n == k, values[:, k * share : (k + 1) * share], out)
    return out


def norm_stats(v):
    width = v.shape[1]
    mean = jnp.sum(v, -1, keepdims=True) * (1.0 / width)
    center = v - mean
    spread = jnp.sum(center * center, -1, keepdims=True) * (1.0 / width)
    scale = lax.rsqrt(spread + EPS)
    return center * scale, scale


def head_masks(share):
    lane = lax.broadcasted_iota(jnp.int32, (1, share), 1) // HEAD_DIM
    return [(lane == h).astype(F32).astype(BF) for h in range(share // HEAD_DIM)]


def half_rows(v, parity):
    tokens, width = v.shape
    split = v.reshape(tokens // (2 * SIDE), 2, SIDE, width)
    return split[:, parity].reshape(tokens // 2, width)


def join_rows(even, odd):
    half, width = even.shape
    both = jnp.stack([even.reshape(half // SIDE, SIDE, width), odd.reshape(half // SIDE, SIDE, width)], 1)
    return both.reshape(2 * half, width)


def softmax_rows(queries, keys):
    scores = dot_nt(queries, keys) * (1.0 / math.sqrt(HEAD_DIM))
    rows = lax.broadcasted_iota(jnp.int32, scores.shape, 0)
    cols = lax.broadcasted_iota(jnp.int32, scores.shape, 1)
    same = (rows + cols) % 2 == 0
    scores = jnp.where(same, scores, -1e30)
    top = jnp.max(scores, -1, keepdims=True)
    grown = jnp.where(same, jnp.exp(scores - top), 0.0)
    return grown / jnp.sum(grown, -1, keepdims=True)


def beside(stacked, heads):
    rows = stacked.shape[0] // heads
    return jnp.concatenate([stacked[h * rows : (h + 1) * rows] for h in range(heads)], axis=1)


def lane_loop(width, body):
    def step(j, carry):
        body(pl.ds(pl.multiple_of(j * LANES, LANES), LANES))
        return carry

    lax.fori_loop(0, width // LANES, step, 0)


def row_loop(tokens, body):
    def step(j, carry):
        body(pl.multiple_of(j * ROWS, ROWS))
        return carry

    lax.fori_loop(0, tokens // ROWS, step, 0)


def attn_kernel_body(
    s_ref, xo, xc, xx, xd, mod, kern, wqkv, wout,
    full_out, grouped_out, q_out, k_out, v_out, ctx_out, keep_out, send_out,
    held, padded,
):
    rel = pl.program_id(0)
    n = s_ref[0]
    tokens, share = xo.shape[1], xo.shape[2]
    width = full_out.shape[2]
    full_out[0] = gather_features(n, (xo, xc, xx, xd), held, width)
    zero_edges(padded)
    shift, scale = mod[0, 0:1, :], 1.0 + mod[0, 1:2, :]

    def rows(at):
        normed, _ = norm_stats(full_out[0, pl.ds(at, ROWS), :].astype(F32))
        padded[pl.ds(at + SIDE, ROWS), :] = normed * scale + shift

    row_loop(tokens, rows)

    def lanes(at):
        taps = taps_of(kern, at)
        for band in range(0, tokens, BAND):
            grouped_out[0, band : band + BAND, at] = conv_band(padded, band, at, taps).astype(BF)

    lane_loop(width, lanes)
    grouped = grouped_out[0]
    query = dot(grouped, wqkv[0]).astype(BF)
    key = dot(grouped, wqkv[1]).astype(BF)
    value = dot(grouped, wqkv[2]).astype(BF)
    q_out[0], k_out[0], v_out[0] = query, key, value
    masks = head_masks(share)
    heads = len(masks)
    parts = []
    for parity in range(2):
        q = half_rows(query, parity)
        k = half_rows(key, parity)
        v = half_rows(value, parity)
        probs = softmax_rows(jnp.concatenate([q * m for m in masks], axis=0), k)
        low = beside(probs.astype(BF), heads)
        parts.append(dot(low, jnp.concatenate([v * m for m in masks], axis=0)).astype(BF))
    context = join_rows(*parts)
    ctx_out[0] = context
    partial = dot(context, wout[...]).astype(BF)

    @pl.when(rel == 0)
    def _():
        keep_out[...] = partial

    @pl.when(rel == 1)
    def _():
        send_out[...] = partial


def ffn_kernel_body(
    s_ref, full, att_own, att_peer, go, gc, gx, gd, mod, up, down, kern,
    g_out, second_out, active_out, gfed_out, ghid_out, mid_out, fkeep_out, fsend_out, keep_out, send_out, kgrad_out,
    held, padded, slope, gpad, att,
):
    rel = pl.program_id(0)
    n = s_ref[0]
    core = jnp.bitwise_and(n, 1)
    tokens, width = full.shape[1], full.shape[2]
    share = go.shape[2]
    units = up.shape[1]
    g_out[0] = gather_features(n, (go, gc, gx, gd), held, width)
    zero_edges(padded)
    zero_edges(gpad)

    @pl.when(rel == 0)
    def _():
        att[...] = att_own[...]
        kgrad_out[...] = jnp.zeros(kgrad_out.shape, F32)

    @pl.when(rel == 1)
    def _():
        att[...] = att_peer[...]

    gate1, gate2 = mod[0, 2:3, :], mod[0, 5:6, :]
    shift, scale = mod[0, 3:4, :], 1.0 + mod[0, 4:5, :]

    def rows(at):
        here = pl.ds(at, ROWS)
        middle = full[0, here, :].astype(F32) + gate1 * att[here, :].astype(F32)
        mid_out[0, here, :] = own_slice(n, middle, share)
        normed, _ = norm_stats(middle)
        second_out[0, here, :] = (normed * scale + shift).astype(BF)
        gfed_out[0, here, :] = (gate2 * g_out[0, here, :].astype(F32)).astype(BF)

    row_loop(tokens, rows)
    padded[SIDE : SIDE + tokens, :] = dot(second_out[0], up[...])

    def lanes(at):
        taps = taps_of(kern, at)
        for band in range(0, tokens, BAND):
            mixed = conv_band(padded, band, at, taps)
            square = mixed * mixed
            curve = jnp.tanh(GELU_A * mixed * (1.0 + GELU_B * square))
            half = 0.5 * (1.0 + curve)
            active_out[0, band : band + BAND, at] = (mixed * half).astype(BF)
            slope[band : band + BAND, at] = half + (0.5 * GELU_A) * mixed * (1.0 - curve * curve) * (
                1.0 + (3.0 * GELU_B) * square
            )

    lane_loop(units, lanes)
    fed = dot(active_out[0], down[...]).astype(BF)
    pieces = [fed[:, k * share : (k + 1) * share] for k in range(4)]
    for x in range(2):
        even, odd = pieces[2 * x], pieces[2 * x + 1]
        fkeep_out[x, 0] = jnp.where(core == 0, even, odd)
        fsend_out[x, 0] = jnp.where(core == 0, odd, even)
    gact = dot_nt(gfed_out[0], down[...]).astype(BF).astype(F32)
    gpad[SIDE : SIDE + tokens, :] = gact * slope[...]

    def lanes_back(at):
        taps = taps_of(kern, at)
        sums = [None] * 9
        for band in range(0, tokens, BAND):
            total, shifted = conv_back_band(gpad, band, at, taps)
            ghid_out[0, band : band + BAND, at] = total.astype(BF)
            for r in range(3):
                values = padded[band + SIDE * r : band + SIDE * r + BAND, at]
                for c in range(3):
                    part = fold_rows(values * shifted[c])
                    sums[3 * r + c] = part if sums[3 * r + c] is None else sums[3 * r + c] + part
        for t in range(9):
            kgrad_out[t : t + 1, at] += jnp.sum(sums[t], 0, keepdims=True)

    lane_loop(units, lanes_back)
    partial = dot_nt(ghid_out[0], up[...]).astype(BF)

    @pl.when(rel == 0)
    def _():
        keep_out[...] = partial

    @pl.when(rel == 1)
    def _():
        send_out[...] = partial


def attn_back_body(
    s_ref, full, att_own, att_peer, gs_own, gs_peer, gfull, mod, q_in, k_in, v_in, kern, wqkv, wout,
    gatt_out, gq_out, gk_out, gv_out, gmid_out, keep_out, send_out, mods_out, kgrad_out,
    att, gsec, normed1, scale1, first, gpad, gback,
):
    rel = pl.program_id(0)
    n = s_ref[0]
    core = jnp.bitwise_and(n, 1)
    tokens, width = full.shape[1], full.shape[2]
    share = q_in.shape[2]
    zero_edges(first)
    zero_edges(gpad)

    @pl.when(rel == 0)
    def _():
        att[...] = att_own[...]
        gsec[...] = gs_own[...]
        kgrad_out[...] = jnp.zeros(kgrad_out.shape, F32)

    @pl.when(rel == 1)
    def _():
        att[...] = att_peer[...]
        gsec[...] = gs_peer[...]

    mods_out[...] = jnp.zeros(mods_out.shape, F32)
    gate1 = mod[0, 2:3, :]
    low_scale, low_shift = 1.0 + mod[0, 1:2, :], mod[0, 0:1, :]
    scale2 = 1.0 + mod[0, 4:5, :]

    def rows(at):
        here = pl.ds(at, ROWS)
        x = full[0, here, :].astype(F32)
        attended = att[here, :].astype(F32)
        normed, inv = norm_stats(x + gate1 * attended)
        grad = gsec[here, :].astype(F32)
        inner = grad * scale2
        mean_a = jnp.sum(inner, -1, keepdims=True) * (1.0 / width)
        mean_b = jnp.sum(inner * normed, -1, keepdims=True) * (1.0 / width)
        gmid = gfull[0, here, :].astype(F32) + inv * (inner - mean_a - normed * mean_b)
        gmid_out[0, here, :] = own_slice(n, gmid, share)
        gatt_out[0, here, :] = (gate1 * gmid).astype(BF)
        mods_out[0, 2:3, :] += jnp.sum(fold_rows(attended * gmid), 0, keepdims=True)
        mods_out[0, 3:4, :] += jnp.sum(fold_rows(grad), 0, keepdims=True)
        mods_out[0, 4:5, :] += jnp.sum(fold_rows(grad * normed), 0, keepdims=True)
        low, inv1 = norm_stats(x)
        normed1[here, :] = low
        scale1[here, :] = jnp.broadcast_to(inv1, (ROWS, LANES))
        first[pl.ds(at + SIDE, ROWS), :] = low * low_scale + low_shift

    row_loop(tokens, rows)
    gctx = dot_nt(gatt_out[0], wout[...]).astype(BF)
    masks = head_masks(share)
    heads = len(masks)
    factor = 1.0 / math.sqrt(HEAD_DIM)
    parts_q, parts_k, parts_v = [], [], []
    for parity in range(2):
        q = half_rows(q_in[0], parity)
        k = half_rows(k_in[0], parity)
        v = half_rows(v_in[0], parity)
        gc = half_rows(gctx, parity)
        q_all = jnp.concatenate([q * m for m in masks], axis=0)
        k_all = jnp.concatenate([k * m for m in masks], axis=0)
        gc_all = jnp.concatenate([gc * m for m in masks], axis=0)
        probs = softmax_rows(q_all, k)
        parts_v.append(dot_tn(probs.astype(BF), gc_all).astype(BF))
        gprobs = dot_nt(gc_all, v).astype(BF).astype(F32)
        gscores = (probs * (gprobs - jnp.sum(probs * gprobs, -1, keepdims=True))).astype(BF)
        parts_q.append((dot(beside(gscores, heads), k_all) * factor).astype(BF))
        parts_k.append((dot_tn(gscores, q_all) * factor).astype(BF))
    gq, gk, gv = join_rows(*parts_q), join_rows(*parts_k), join_rows(*parts_v)
    gq_out[0], gk_out[0], gv_out[0] = gq, gk, gv
    gpad[SIDE : SIDE + tokens, :] = dot_nt(gq, wqkv[0]) + dot_nt(gk, wqkv[1]) + dot_nt(gv, wqkv[2])

    def lanes(at):
        taps = taps_of(kern, at)
        sums = [None] * 9
        shift_sum, scale_sum = None, None
        for band in range(0, tokens, BAND):
            total, shifted = conv_back_band(gpad, band, at, taps)
            gback[band : band + BAND, at] = total
            part_a, part_b = fold_rows(total), fold_rows(total * normed1[band : band + BAND, at])
            shift_sum = part_a if shift_sum is None else shift_sum + part_a
            scale_sum = part_b if scale_sum is None else scale_sum + part_b
            for r in range(3):
                values = first[band + SIDE * r : band + SIDE * r + BAND, at]
                for c in range(3):
                    part = fold_rows(values * shifted[c])
                    sums[3 * r + c] = part if sums[3 * r + c] is None else sums[3 * r + c] + part
        for t in range(9):
            kgrad_out[t : t + 1, at] += jnp.sum(sums[t], 0, keepdims=True)
        mods_out[0, 0:1, at] = jnp.sum(shift_sum, 0, keepdims=True)
        mods_out[0, 1:2, at] = jnp.sum(scale_sum, 0, keepdims=True)

    lane_loop(width, lanes)

    def rows_back(at):
        here = pl.ds(at, ROWS)
        inner = gback[here, :] * low_scale
        normed = normed1[here, :]
        mean_a = jnp.sum(inner, -1, keepdims=True) * (1.0 / width)
        mean_b = jnp.sum(inner * normed, -1, keepdims=True) * (1.0 / width)
        grad = scale1[here, 0:1] * (inner - mean_a - normed * mean_b)
        low = grad.astype(BF)
        pieces = [low[:, k * share : (k + 1) * share] for k in range(4)]
        for x in range(2):
            even, odd = pieces[2 * x], pieces[2 * x + 1]
            keep_out[x, 0, here, :] = jnp.where(core == 0, even, odd)
            send_out[x, 0, here, :] = jnp.where(core == 0, odd, even)

    row_loop(tokens, rows_back)


def call(body, name, grid, scalars, ins, outs, scratch, flops):
    in_specs = [s for _, s in ins]
    bytes_moved = sum(math.prod(o.shape) * o.dtype.itemsize for o, _ in outs)
    return pl.pallas_call(
        body,
        name=name,
        out_shape=[o for o, _ in outs],
        grid_spec=pltpu.PrefetchScalarGridSpec(
            num_scalar_prefetch=1,
            grid=grid,
            in_specs=in_specs,
            out_specs=[s for _, s in outs],
            scratch_shapes=scratch,
        ),
        compiler_params=pltpu.CompilerParams(vmem_limit_bytes=VMEM_LIMIT),
        cost_estimate=pl.CostEstimate(flops=flops, bytes_accessed=bytes_moved, transcendentals=0),
    )(scalars, *[a for a, _ in ins])


def shape_of(dims, dtype):
    return jax.ShapeDtypeStruct(dims, dtype)


def whole(array):
    dims = array.shape
    return (array, pl.BlockSpec(dims, lambda i, s: (0,) * len(dims)))


def whole_out(dims, dtype):
    return (shape_of(dims, dtype), pl.BlockSpec(dims, lambda i, s: (0,) * len(dims)))


def by_latent(array, base):
    dims = (1,) + array.shape[1:]
    rest = (0,) * (len(dims) - 1)
    return (array, pl.BlockSpec(dims, lambda i, s: (base + jnp.bitwise_xor(i, jnp.bitwise_and(s[0], 1)),) + rest))


def by_step(array):
    dims = (1,) + array.shape[1:]
    rest = (0,) * (len(dims) - 1)
    return (array, pl.BlockSpec(dims, lambda i, s: (i,) + rest))


def step_out(dims, dtype):
    rest = (0,) * (len(dims) - 1)
    return (shape_of(dims, dtype), pl.BlockSpec((1,) + dims[1:], lambda i, s: (i,) + rest))


def latent_out(dims, dtype):
    rest = (0,) * (len(dims) - 1)
    return (
        shape_of(dims, dtype),
        pl.BlockSpec((1,) + dims[1:], lambda i, s: (jnp.bitwise_xor(i, jnp.bitwise_and(s[0], 1)),) + rest),
    )


def halves_out(tokens, share):
    return (
        shape_of((2, PAIR, tokens, share), BF),
        pl.BlockSpec(
            (2, 1, tokens, share), lambda i, s: (0, jnp.bitwise_xor(i, jnp.bitwise_and(s[0], 1)), 0, 0)
        ),
    )


def core_swap(v):
    return lax.ppermute(v, "narrow", [(0, 1), (1, 0), (2, 3), (3, 2)])


def x_swap(v):
    return lax.ppermute(v, "narrow", [(0, 2), (2, 0), (1, 3), (3, 1)])


def sum_pair(a, b):
    return (a.astype(F32) + b.astype(F32)).astype(BF)


def reduce_pair(keep, send):
    here = sum_pair(keep, core_swap(send))
    own = sum_pair(here, x_swap(here))
    return own, core_swap(own)


def reduce_slices(n, keep, send):
    x = n // 2
    both = sum_pair(keep, core_swap(send))
    mine = lax.dynamic_index_in_dim(both, x, 0, keepdims=False)
    other = lax.dynamic_index_in_dim(both, 1 - x, 0, keepdims=False)
    return mine.astype(F32) + x_swap(other).astype(F32)


def wide_swap(v, bit, count):
    return lax.ppermute(v, "wide", [(i, i ^ bit) for i in range(count)])


def wide_gather(v, count):
    held = v[None]
    bit = 1
    while bit < count:
        held = jnp.concatenate([held, wide_swap(held, bit, count)], 0)
        bit *= 2
    return held


def wide_sum(v, count):
    rows, width = v.shape
    groups = count // 2
    at = lax.axis_index("wide")
    half, place = at % 2, at // 2
    split = v.reshape(2, groups, rows // count, width)
    mine = lax.dynamic_index_in_dim(split, half, 0, keepdims=False)
    other = lax.dynamic_index_in_dim(split, 1 - half, 0, keepdims=False)
    both = sum_pair(mine, wide_swap(other, 1, count))
    total = lax.dynamic_index_in_dim(both, place, 0, keepdims=False).astype(F32)

    def shift(v, d):
        return lax.ppermute(v, "wide", [(i, (i + 2 * d) % count) for i in range(count)])

    arrived = [
        shift(lax.dynamic_index_in_dim(both, (place + d) % groups, 0, keepdims=False), d)
        for d in range(1, groups)
    ]
    for part in arrived:
        total = total + part.astype(F32)
    total = total.astype(BF)
    gathered = jnp.zeros((groups, rows // count, width), BF)
    gathered = lax.dynamic_update_index_in_dim(gathered, total, place, 0)
    for d in range(1, groups):
        gathered = lax.dynamic_update_index_in_dim(gathered, shift(total, d), (place - d) % groups, 0)
    peer = wide_swap(gathered, 1, count)
    low = jnp.where(half == 0, gathered, peer)
    high = jnp.where(half == 0, peer, gathered)
    return jnp.concatenate([low, high], 0).reshape(rows, width)


def embed_times(stamps):
    halved = FREQ // 2
    freqs = jnp.exp(-math.log(10000.0) * jnp.arange(halved, dtype=F32) / halved)
    angles = stamps[:, None] * freqs[None, :]
    return jnp.concatenate([jnp.cos(angles), jnp.sin(angles)], 1)


def silu_slope(v):
    gate = jax.nn.sigmoid(v)
    return gate * (1.0 + v * (1.0 - gate))


def body(
    latents, cotangent, timesteps, time_in, time_out, ada_weight, ada_bias,
    attn_kernel, qkv_weight, out_weight, up_weight, ffn_kernel, down_weight,
):
    wide_count = lax.axis_size("wide")
    wide_at = lax.axis_index("wide")
    n = lax.axis_index("narrow")
    per_dev, tokens, share = latents.shape
    width = out_weight.shape[1]
    units = up_weight.shape[1]
    latent_total = timesteps.shape[0]
    scalars = jnp.stack([n, n]).astype(jnp.int32)

    order = jnp.bitwise_xor(jnp.arange(wide_count, dtype=jnp.int32), wide_at)
    stamps = timesteps.reshape(wide_count, per_dev)[order].reshape(latent_total).astype(F32)
    embedded = embed_times(stamps)
    inner_pre = jnp.dot(embedded, time_in, precision=HIGHEST)
    inner = jax.nn.silu(inner_pre)
    outer_pre = jnp.dot(inner, time_out, precision=HIGHEST)
    outer = jax.nn.silu(outer_pre)
    modulation = jnp.dot(outer[:per_dev], ada_weight, precision=HIGHEST) + ada_bias
    mod = modulation.reshape(per_dev, 6, width)

    x_across = x_swap(latents)
    x_core = core_swap(latents)
    x_diag = core_swap(x_across)
    g_across = x_swap(cotangent)
    g_core = core_swap(cotangent)
    g_diag = core_swap(g_across)

    pairs = range(0, per_dev, PAIR)
    tile = (PAIR, tokens, width)
    thin = (PAIR, tokens, share)
    flat = (tokens, width)

    forward = []
    for base in pairs:
        res = call(
            attn_kernel_body, "attn_fwd", (PAIR,), scalars,
            [by_latent(latents, base), by_latent(x_core, base), by_latent(x_across, base), by_latent(x_diag, base),
             by_latent(mod, base), whole(attn_kernel), whole(qkv_weight), whole(out_weight)],
            [step_out(tile, BF), step_out(tile, BF), step_out(thin, BF), step_out(thin, BF), step_out(thin, BF),
             step_out(thin, BF), whole_out(flat, BF), whole_out(flat, BF)],
            [pltpu.VMEM((4, tokens, share), BF), pltpu.VMEM((tokens + 2 * SIDE, width), F32)],
            2_000_000_000,
        )
        forward.append(res)
    attended = [reduce_pair(res[6], res[7]) for res in forward]

    middle = []
    for base, res, att in zip(pairs, forward, attended):
        out = call(
            ffn_kernel_body, "ffn", (PAIR,), scalars,
            [by_step(res[0]), whole(att[0]), whole(att[1]),
             by_latent(cotangent, base), by_latent(g_core, base), by_latent(g_across, base), by_latent(g_diag, base),
             by_latent(mod, base), whole(up_weight), whole(down_weight), whole(ffn_kernel)],
            [step_out(tile, BF), step_out(tile, BF), step_out((PAIR, tokens, units), BF), step_out(tile, BF),
             step_out((PAIR, tokens, units), BF), latent_out(thin, F32), halves_out(tokens, share),
             halves_out(tokens, share), whole_out(flat, BF), whole_out(flat, BF), whole_out((9, units), F32)],
            [pltpu.VMEM((4, tokens, share), BF), pltpu.VMEM((tokens + 2 * SIDE, units), F32),
             pltpu.VMEM((tokens, units), F32), pltpu.VMEM((tokens + 2 * SIDE, units), F32),
             pltpu.VMEM(flat, BF)],
            4_000_000_000,
        )
        middle.append(out)
    grad_second = [reduce_pair(out[8], out[9]) for out in middle]
    fed = [reduce_slices(n, out[6], out[7]) for out in middle]

    back = []
    for base, res, att, out, gsec in zip(pairs, forward, attended, middle, grad_second):
        got = call(
            attn_back_body, "attn_bwd", (PAIR,), scalars,
            [by_step(res[0]), whole(att[0]), whole(att[1]), whole(gsec[0]), whole(gsec[1]), by_step(out[0]),
             by_latent(mod, base), by_step(res[2]), by_step(res[3]), by_step(res[4]),
             whole(attn_kernel), whole(qkv_weight), whole(out_weight)],
            [step_out(tile, BF), step_out(thin, BF), step_out(thin, BF), step_out(thin, BF), latent_out(thin, F32),
             halves_out(tokens, share), halves_out(tokens, share), latent_out((PAIR, 8, width), F32),
             whole_out((9, width), F32)],
            [pltpu.VMEM(flat, BF), pltpu.VMEM(flat, BF), pltpu.VMEM(flat, F32), pltpu.VMEM((tokens, LANES), F32),
             pltpu.VMEM((tokens + 2 * SIDE, width), F32), pltpu.VMEM((tokens + 2 * SIDE, width), F32),
             pltpu.VMEM(flat, F32)],
            3_000_000_000,
        )
        back.append(got)
    grad_in = [reduce_slices(n, got[5], got[6]) for got in back]

    own = lambda v: lax.dynamic_slice_in_dim(v, n * share, share, v.ndim - 1)
    gate2 = own(mod[:, 5, :])[:, None, :]
    fed_all = jnp.concatenate(fed, 0)
    mid_all = jnp.concatenate([out[5] for out in middle], 0)
    final_out = (mid_all + gate2 * fed_all).astype(BF)
    gate2_grad = jnp.sum(fed_all * cotangent.astype(F32), 1)
    gmid_all = jnp.concatenate([got[4] for got in back], 0)
    final_grad = (gmid_all + jnp.concatenate(grad_in, 0)).astype(BF)

    factor = 1.0 / latent_total

    def token_product(lefts, rights):
        total = None
        for a, b in zip(lefts, rights):
            part = lax.dot_general(
                a.reshape(-1, a.shape[-1]), b.reshape(-1, b.shape[-1]),
                (((0,), (0,)), ((), ())), preferred_element_type=F32,
            )
            total = part if total is None else total + part
        return (total * factor).astype(BF)

    down_grad = token_product([o[2] for o in middle], [o[3] for o in middle])
    up_grad = token_product([o[1] for o in middle], [o[4] for o in middle])
    out_grad = token_product([r[5] for r in forward], [g[0] for g in back])
    qkv_grads = [token_product([g[k] for g in back], [r[1] for r in forward]) for k in (1, 2, 3)]
    down_grad = wide_sum(down_grad, wide_count).astype(F32)
    up_grad = wide_sum(up_grad, wide_count).astype(F32)
    attn_grads = wide_sum(jnp.concatenate([out_grad] + qkv_grads, 0), wide_count).astype(F32)
    out_grad = attn_grads[:share]
    qkv_grad = jnp.swapaxes(attn_grads[share:].reshape(3, share, width), 1, 2)

    mods = jnp.concatenate([got[7] for got in back], 0)
    gate2_row = lax.dynamic_update_slice_in_dim(jnp.zeros((per_dev, width), F32), gate2_grad, n * share, 1)
    pieces = jnp.stack(
        [mods[:, 0], mods[:, 1], 0.25 * mods[:, 2], 0.25 * mods[:, 3], 0.25 * mods[:, 4], gate2_row], 1
    ).reshape(per_dev, 6 * width)
    attn_taps = sum(got[8] for got in back)
    ffn_taps = sum(out[10] for out in middle)

    def narrow_sum(v):
        v = v + core_swap(v)
        return v + x_swap(v)

    packed = narrow_sum(jnp.concatenate([pieces.reshape(-1), attn_taps.reshape(-1)]).reshape(-1, LANES))
    packed = jnp.concatenate([packed, ffn_taps.reshape(-1, LANES)], 0)
    gathered = wide_gather(packed, wide_count)
    count_a = per_dev * 6 * width // LANES
    count_b = count_a + 9 * width // LANES
    gmod = gathered[:, :count_a].reshape(latent_total, 6 * width)
    attn_taps = jnp.sum(gathered[:, count_a:count_b], 0).reshape(9, width) * factor
    ffn_taps = jnp.sum(gathered[:, count_b:], 0).reshape(9, units) * factor

    scaled = gmod * factor
    ada_bias_grad = jnp.sum(scaled, 0)
    ada_weight_grad = jnp.dot(outer.T, scaled, precision=HIGHEST)
    outer_grad = jnp.dot(scaled, ada_weight.T, precision=HIGHEST) * silu_slope(outer_pre)
    time_out_grad = jnp.dot(inner.T, outer_grad, precision=HIGHEST)
    inner_grad = jnp.dot(outer_grad, time_out.T, precision=HIGHEST) * silu_slope(inner_pre)
    time_in_grad = jnp.dot(embedded.T, inner_grad, precision=HIGHEST)
    return (
        final_out, final_grad, time_in_grad, time_out_grad, ada_weight_grad, ada_bias_grad,
        attn_taps, qkv_grad, out_grad, up_grad, ffn_taps, down_grad,
    )


def solution(mesh):
    tokens = P("wide", None, "narrow")
    weights = (P(None, None, "narrow"), P("narrow", None), P(None, "narrow"), P(None, "narrow"), P("narrow", None))
    return jax.shard_map(
        body,
        mesh=mesh,
        in_specs=(tokens, tokens, P(), P(), P(), P(), P(), P()) + weights,
        out_specs=(tokens, tokens, P(), P(), P(), P(), P()) + weights,
        check_vma=False,
    )
```

time: 1160 us -> 422 us (0.36)
  waiting for transfers between devices: 551 us -> 109 us
  other arithmetic: 262 us -> 31.6 us
  Pallas kernels: 0 us -> 112 us
  matrix products: 158 us -> 62.4 us
  local copies, waits for them, and re-layouts: 92.2 us -> 35.1 us
  blocking collectives: 57 us -> 0 us
  starting transfers between devices: 22.2 us -> 65.8 us
  between operations: 16.1 us -> 2.01 us
    psum x4 -> x0, waiting for transfers between devices: 507 us -> none  [the longest x1 287 us: body(): lax.psum((cond_grads[0] * factor_sum).astype(jnp.bfloat16), 'wide')]
    reduce_sum x18 -> x3, other arithmetic: 131 us -> 1.77 us  [the longest x1 1.07 us: body(): gate2_grad = jnp.sum(fed_all * cotangent.astype(F32), 1)]
    pallas_call x0 -> x6, Pallas kernels: none -> 112 us  [call(): pl.pallas_call(body, name=name, out_shape=[o for o, _ in outs], grid_spec...]
    ppermute x0 -> x55, waiting for transfers between devices: none -> 109 us  [the longest x11 51.4 us: x_swap(): return lax.ppermute(v, 'narrow', [(0, 2), (2, 0), (1, 3), (3, 1)])]
    dot_general x33 -> x20, matrix products: 153 us -> 62.4 us  [the longest x1 16 us: body(): jnp.dot(scaled, ada_weight.T, precision=HIGHEST) * silu_slope(outer_pre)]
    ppermute x0 -> x55, starting transfers between devices: none -> 65.8 us  [the longest x18 32.2 us: shift(): lax.ppermute(v, 'wide', [(i, (i + 2 * d) % count) for i in range(count)])]
    psum x1 -> x0, blocking collectives: 57 us -> none  [body(): lax.psum((cond_grads[3] * factor_sum).astype(jnp.bfloat16), 'wide')]
    convert_element_type x19, other arithmetic: 57.1 us -> 16.4 us  [the longest x15 13.3 us: sum_pair(): return (a.astype(F32) + b.astype(F32)).astype(BF)]
  transfers between devices with their start and end apart: 10 -> 55, of which waited for: 7 -> 18; matrix products, arithmetic and copies ran while one was open for 18% -> 28% of each run, Pallas kernels for 0% -> 24%
where the time goes in v1:
time: 422 us; the launch traced here: 418 us
  Pallas kernels  112 us (27%)
  waiting for transfers between devices  109 us (26%)
  starting transfers between devices  65.8 us (16%)
  matrix products  62.4 us (15%)
  local copies, waits for them, and re-layouts  35.1 us (8%)
  other arithmetic  31.6 us (7%)
    pallas_call x6, Pallas kernels, call(): pl.pallas_call(body, name=name, out_shape=[o for o, _ in outs], grid_spec...  112 us
    ppermute x11, waiting for transfers between devices, x_swap(): return lax.ppermute(v, 'narrow', [(0, 2), (2, 0), (1, 3), (3, 1)])  51.4 us
    ppermute x18, waiting for transfers between devices, shift(): lax.ppermute(v, 'wide', [(i, (i + 2 * d) % count) for i in range(count)])  43.1 us
    ppermute x18, starting transfers between devices, shift(): lax.ppermute(v, 'wide', [(i, (i + 2 * d) % count) for i in range(count)])  32.2 us
    dot_general x1, matrix products, body(): jnp.dot(scaled, ada_weight.T, precision=HIGHEST) * silu_slope(outer_pre)  16 us
    ppermute x11, starting transfers between devices, x_swap(): return lax.ppermute(v, 'narrow', [(0, 2), (2, 0), (1, 3), (3, 1)])  15.8 us
    dot_general x1, matrix products, body(): ada_weight_grad = jnp.dot(outer.T, scaled, precision=HIGHEST)  14.8 us
    ppermute x9, waiting for transfers between devices, wide_swap(): return lax.ppermute(v, 'wide', [(i, i ^ bit) for i in range(count)])  14.8 us
  transfers between devices with their start and end apart: 55, of which 18 were waited for; matrix products, arithmetic and copies ran while one was open for 28% of the time, Pallas kernels for 24%

profile of v1, /device:TPU:0, one launch (start us, length us, event | category | flops | bytes accessed | tf_op | source)
XLA Modules:
  0.0 417.9 jit_solution(1214377508611479087)
XLA Ops:
  0.7 2.1 copy.108.xo
  2.8 2.9 collective-permute-start.1
  10.3 2.1 fusion.30
  12.3 5.6 %collective-permute-done.1.xx = bf16[4,256,192]{2,1,0:T(8,128)(2,1)} collective-permute-done((bf16[4,256,192]{2,1,0:T(8,128)(2,1)}, bf16[4,256,192]{2,1,0:T(8,128)(2,1)}, u32[]{:S(2)}, u32[]{:S(2)}) %collective-permute-start.1) | collective-permute-done | bytes 393248 | tf_op jit(solution)/shard_map/ppermute | solution.py:485
  18.0 9.6 %convolution_add_fusion = f32[4,4608]{1,0:T(4,128)S(1)} fusion(f32[768,4608]{1,0:T(8,128)} %param.18, f32[4608]{0:T(1024)S(1)} %copy-done.44, f32[32,768]{1,0:T(8,128)S(1)} %get-tuple-element.202), kind=kOutput, calls=%fused_computation.1 | convolution fusion | flops 169887744 | bytes 14262272 | tf_op jit(solution)/shard_map/dot_general | solution.py:582
  30.3 11.7 %attn_fwd.2 = (bf16[2,256,768]{2,1,0:T(8,128)(2,1)}, bf16[2,256,768]{2,1,0:T(8,128)(2,1)}, bf16[2,256,192]{2,1,0:T(8,128)(2,1)}, bf16[2,256,192]{2,1,0:T(8,128)(...) custom-call(s32[2]{0:T(128)} %pad_add_fusion.s_ref, ...), custom_call_target="tpu_custom_call" | custom-call | flops 2000000000 | bytes 3145728 | tf_op jit(solution)/shard_map/attn_fwd/pallas_call | solution.py:417
  42.6 11.7 %attn_fwd.3 = (bf16[2,256,768]{2,1,0:T(8,128)(2,1)}, bf16[2,256,768]{2,1,0:T(8,128)(2,1)}, bf16[2,256,192]{2,1,0:T(8,128)(2,1)}, bf16[2,256,192]{2,1,0:T(8,128)(...) custom-call(s32[2]{0:T(128)} %pad_add_fusion.s_ref, ...), custom_call_target="tpu_custom_call" | custom-call | flops 2000000000 | bytes 3145728 | tf_op jit(solution)/shard_map/attn_fwd/pallas_call | solution.py:417
  54.7 1.8 collective-permute-start.7
  59.3 1.8 collective-permute-start.10
  61.1 8.5 %collective-permute-done.7.gx = bf16[4,256,192]{2,1,0:T(8,128)(2,1)} collective-permute-done((bf16[4,256,192]{2,1,0:T(8,128)(2,1)S(1)}, bf16[4,256,192]{2,1,0:T(8,128)(2,1)}, u32[]{:S(2)}, u32[]{:S(2)}) %collective-permute-start.7) | collective-permute-done | bytes 393248 | tf_op jit(solution)/shard_map/ppermute | solution.py:485
  69.7 8.3 %collective-permute-done.4 = bf16[256,768]{1,0:T(8,128)(2,1)S(1)} collective-permute-done((bf16[256,768]{1,0:T(8,128)(2,1)S(1)}, bf16[256,768]{1,0:T(8,128)(2,1)S(1)}, u32[]{:S(2)}, u32[]{:S(2)}) %collective-permute-start.4) | collective-permute-done | bytes 393248 | tf_op jit(solution)/shard_map/ppermute | solution.py:485
  79.7 6.2 %collective-permute-done.10 = bf16[256,768]{1,0:T(8,128)(2,1)} collective-permute-done((bf16[256,768]{1,0:T(8,128)(2,1)S(1)}, bf16[256,768]{1,0:T(8,128)(2,1)}, u32[]{:S(2)}, u32[]{:S(2)}) %collective-permute-start.10) | collective-permute-done | bytes 393248 | tf_op jit(solution)/shard_map/ppermute | solution.py:485
  85.9 1.8 add_convert_fusion.8.att_own
  88.6 19.2 %ffn.2 = (bf16[2,256,768]{2,1,0:T(8,128)(2,1)}, bf16[2,256,768]{2,1,0:T(8,128)(2,1)}, bf16[2,256,768]{2,1,0:T(8,128)(2,1)}, bf16[2,256,768]{2,1,0:T(8,128)(2,1)}...) custom-call(s32[2]{0:T(128)} %pad_add_fusion.s_ref, ...), custom_call_target="tpu_custom_call" | custom-call | flops 4000000000 | bytes 5925888 | tf_op jit(solution)/shard_map/ffn/pallas_call | solution.py:417
  108.4 19.4 %ffn.3 = (bf16[2,256,768]{2,1,0:T(8,128)(2,1)}, bf16[2,256,768]{2,1,0:T(8,128)(2,1)}, bf16[2,256,768]{2,1,0:T(8,128)(2,1)}, bf16[2,256,768]{2,1,0:T(8,128)(2,1)}...) custom-call(s32[2]{0:T(128)} %pad_add_fusion.s_ref, ...), custom_call_target="tpu_custom_call" | custom-call | flops 4000000000 | bytes 5925888 | tf_op jit(solution)/shard_map/ffn/pallas_call | solution.py:417
  131.2 2.1 fusion.51
  134.1 1.8 collective-permute-start.47
  145.5 4.8 %collective-permute-done.47 = bf16[4,96,768]{2,1,0:T(8,128)(2,1)S(1)} collective-permute-done((bf16[4,96,768]{2,1,0:T(8,128)(2,1)S(1)}, bf16[4,96,768]{2,1,0:T(8,128)(2,1)S(1)}, u32[]{:S(2)}, u32[]{:S(2)}) %collective-permute-start.47) | collective-permute-done | bytes 589856 | tf_op jit(solution)/shard_map/ppermute | solution.py:507
  150.3 1.7 collective-permute-start.15
  153.1 4.3 %collective-permute-done.13 = bf16[2,256,192]{2,1,0:T(8,128)(2,1)S(1)} collective-permute-done((bf16[2,256,192]{2,1,0:T(8,128)(2,1)S(1)}, bf16[2,256,192]{2,1,0:T(8,128)(2,1)S(1)}, u32[]{:S(2)}, u32[]{:S(2)}) %collective-permute-start.13) | collective-permute-done | bytes 196640 | tf_op jit(solution)/shard_map/ppermute | solution.py:485
  159.2 11.5 %collective-permute-done.15 = bf16[2,256,192]{2,1,0:T(8,128)(2,1)S(1)} collective-permute-done((bf16[2,256,192]{2,1,0:T(8,128)(2,1)S(1)}, bf16[2,256,192]{2,1,0:T(8,128)(2,1)S(1)}, u32[]{:S(2)}, u32[]{:S(2)}) %collective-permute-start.15) | collective-permute-done | bytes 196640 | tf_op jit(solution)/shard_map/ppermute | solution.py:485
  170.6 3.6 collective-permute-start.50
  176.2 2.0 copy.133
  181.3 2.8 collective-permute-start.42
  186.1 1.8 bitcast_dynamic-update-slice_fusion.3
  188.9 7.4 %collective-permute-start.52 = (bf16[96,768]{1,0:T(8,128)(2,1)S(1)}, bf16[96,768]{1,0:T(8,128)(2,1)S(1)}, u32[]{:S(2)}, u32[]{:S(2)}) collective-permute-start(bf16[96,768]{1,0:T(8,128)(2,1)S(1)} %get-tuple-element.175), channel_id=1, source_target_pairs={{0,16},{4,20},{8,24},{12,28},{16,0},{20,4},{24,8},{28,12},{1,17},{... | collective-permute-start | bytes 442376 | tf_op jit(solution)/shard_map/ppermute | solution.py:531
  196.3 6.3 %collective-permute-done.41 = bf16[96,768]{1,0:T(8,128)(2,1)S(1)} collective-permute-done((bf16[96,768]{1,0:T(8,128)(2,1)S(1)}, bf16[96,768]{1,0:T(8,128)(2,1)S(1)}, u32[]{:S(2)}, u32[]{:S(2)}) %collective-permute-start.41) | collective-permute-done | bytes 147488 | tf_op jit(solution)/shard_map/ppermute | solution.py:531
  205.5 2.1 collective-permute-start.43
  208.8 2.5 collective-permute-start.45
  216.0 3.6 collective-permute-done.44
  223.2 24.9 %attn_bwd.2 = (bf16[2,256,768]{2,1,0:T(8,128)(2,1)}, bf16[2,256,192]{2,1,0:T(8,128)(2,1)}, bf16[2,256,192]{2,1,0:T(8,128)(2,1)}, bf16[2,256,192]{2,1,0:T(8,128)(...) custom-call(s32[2]{0:T(128)} %pad_add_fusion.s_ref, ...), custom_call_target="tpu_custom_call" | custom-call | flops 3000000000 | bytes 2632704 | tf_op jit(solution)/shard_map/attn_bwd/pallas_call | solution.py:417
  249.8 24.7 %attn_bwd.3 = (bf16[2,256,768]{2,1,0:T(8,128)(2,1)}, bf16[2,256,192]{2,1,0:T(8,128)(2,1)}, bf16[2,256,192]{2,1,0:T(8,128)(2,1)}, bf16[2,256,192]{2,1,0:T(8,128)(...) custom-call(s32[2]{0:T(128)} %pad_add_fusion.s_ref, ...), custom_call_target="tpu_custom_call" | custom-call | flops 3000000000 | bytes 2632704 | tf_op jit(solution)/shard_map/attn_bwd/pallas_call | solution.py:417
  283.9 4.0 collective-permute-done.27
  293.0 2.7 bitcast_convert_fusion
  295.7 10.0 %collective-permute-done.28 = f32[1,252,128]{2,1,0:T(8,128)S(1)} collective-permute-done((f32[1,252,128]{2,1,0:T(8,128)S(1)}, f32[1,252,128]{2,1,0:T(8,128)S(1)}, u32[]{:S(2)}, u32[]{:S(2)}) %collective-permute-start.28) | collective-permute-done | bytes 129056 | tf_op jit(solution)/shard_map/ppermute | solution.py:507
  306.4 3.6 collective-permute-start.29
  314.9 3.8 collective-permute-start.34
  318.7 1.8 collective-permute-done.23
  320.5 1.9 collective-permute-start.33
  323.7 6.2 %collective-permute-done.33 = bf16[96,768]{1,0:T(8,128)(2,1)S(1)} collective-permute-done((bf16[96,768]{1,0:T(8,128)(2,1)S(1)}, bf16[96,768]{1,0:T(8,128)(2,1)S(1)}, u32[]{:S(2)}, u32[]{:S(2)}) %collective-permute-start.33) | collective-permute-done | bytes 147488 | tf_op jit(solution)/shard_map/ppermute | solution.py:531
  332.8 2.8 collective-permute-start.30
  335.8 3.8 collective-permute-start.37
  342.1 24.7 %collective-permute-done.36 = bf16[96,768]{1,0:T(8,128)(2,1)S(1)} collective-permute-done((bf16[96,768]{1,0:T(8,128)(2,1)}, bf16[96,768]{1,0:T(8,128)(2,1)S(1)}, u32[]{:S(2)}, u32[]{:S(2)}) %collective-permute-start.36) | collective-permute-done | bytes 147488 | tf_op jit(solution)/shard_map/ppermute | solution.py:531
  372.9 16.0 %convolution_multiply_fusion = f32[32,768]{1,0:T(8,128)S(1)} fusion(f32[32,4608]{1,0:T(8,128)S(1)} %mul.124, f32[768,4608]{1,0:T(8,128)} %param.18, f32[32,768]{1,0:T(8,128)} %get-tuple-element.203), kind=kOutput, calls=%fused_computation.40 | convolution fusion | flops 1359151104 | bytes 14942208 | tf_op jit(solution)/shard_map/dot_general | solution.py:703
  388.9 2.9 convolution_multiply_fusion.1
  391.8 3.5 fusion.34
  396.6 2.6 fusion.32
  399.2 14.8 %fusion.45 = f32[768,4608]{1,0:T(8,128)} fusion(f32[32,4608]{1,0:T(8,128)S(1)} %mul.124, f32[32,768]{1,0:T(8,128)} %get-tuple-element.203), kind=kOutput, calls=%fused_computation.150 | convolution fusion | flops 1359052800 | bytes 14843904 | tf_op jit(solution)/shard_map/dot_general | solution.py:702
  (285 shorter events, 90.0 us)
Async XLA Ops:
  2.8 15.2 %collective-permute-start.1 = (bf16[4,256,192]{2,1,0:T(8,128)(2,1)}, bf16[4,256,192]{2,1,0:T(8,128)(2,1)}, u32[]{:S(2)}, u32[]{:S(2)}) collective-permute-start(bf16[4,256,192]{2,1,0:T(8,128)(2,1)} %copy.108.xo), channel_id=1, source_target_pairs={{0,2},{2,0},{1,3},{3,1},{4,6},{6,4},{5,7},{7,5},{8,10},{10,8},{9,1... | collective-permute-start | bytes 1179656 | tf_op jit(solution)/shard_map/ppermute | solution.py:485
  5.8 24.6 %collective-permute-start = (bf16[4,256,192]{2,1,0:T(8,128)(2,1)}, bf16[4,256,192]{2,1,0:T(8,128)(2,1)}, u32[]{:S(2)}, u32[]{:S(2)}) collective-permute-start(bf16[4,256,192]{2,1,0:T(8,128)(2,1)} %copy.108.xo), channel_id=1, source_target_pairs={{0,1},{1,0},{2,3},{3,2},{4,5},{5,4},{6,7},{7,6},{8,9},{9,8},{10,11... | collective-permute-start | bytes 1179656 | tf_op jit(solution)/shard_map/ppermute | solution.py:481
  18.0 12.3 %collective-permute-start.2 = (bf16[4,256,192]{2,1,0:T(8,128)(2,1)}, bf16[4,256,192]{2,1,0:T(8,128)(2,1)}, u32[]{:S(2)}, u32[]{:S(2)}) collective-permute-start(bf16[4,256,192]{2,1,0:T(8,128)(2,1)} %collective-permute-done.1.xx), channel_id=1, source_target_pairs={{0,1},{1,0},{2,3},{3,2},{4,5},{5,4},{6,7},{7,6},{8,9},{9,8},{10,11... | collective-permute-start | bytes 1179656 | tf_op jit(solution)/shard_map/ppermute | solution.py:481
  42.0 14.5 %collective-permute-start.3 = (bf16[256,768]{1,0:T(8,128)(2,1)}, bf16[256,768]{1,0:T(8,128)(2,1)}, u32[]{:S(2)}, u32[]{:S(2)}) collective-permute-start(bf16[256,768]{1,0:T(8,128)(2,1)} %get-tuple-element.70), channel_id=1, source_target_pairs={{0,1},{1,0},{2,3},{3,2},{4,5},{5,4},{6,7},{7,6},{8,9},{9,8},{10,11... | collective-permute-start | bytes 1179656 | tf_op jit(solution)/shard_map/ppermute | solution.py:481
  54.7 14.9 %collective-permute-start.7 = (bf16[4,256,192]{2,1,0:T(8,128)(2,1)S(1)}, bf16[4,256,192]{2,1,0:T(8,128)(2,1)}, u32[]{:S(2)}, u32[]{:S(2)}) collective-permute-start(bf16[4,256,192]{2,1,0:T(8,128)(2,1)S(1)} %copy.112.go), channel_id=1, source_target_pairs={{0,2},{2,0},{1,3},{3,1},{4,6},{6,4},{5,7},{7,5},{8,10},{10,8},{9,1... | collective-permute-start | bytes 1179656 | tf_op jit(solution)/shard_map/ppermute | solution.py:485
  57.8 20.2 %collective-permute-start.4 = (bf16[256,768]{1,0:T(8,128)(2,1)S(1)}, bf16[256,768]{1,0:T(8,128)(2,1)S(1)}, u32[]{:S(2)}, u32[]{:S(2)}) collective-permute-start(bf16[256,768]{1,0:T(8,128)(2,1)S(1)} %add_convert_fusion.11), channel_id=1, source_target_pairs={{0,2},{2,0},{1,3},{3,1},{4,6},{6,4},{5,7},{7,5},{8,10},{10,8},{9,1... | collective-permute-start | bytes 1179656 | tf_op jit(solution)/shard_map/ppermute | solution.py:485
  59.3 26.6 %collective-permute-start.10 = (bf16[256,768]{1,0:T(8,128)(2,1)S(1)}, bf16[256,768]{1,0:T(8,128)(2,1)}, u32[]{:S(2)}, u32[]{:S(2)}) collective-permute-start(bf16[256,768]{1,0:T(8,128)(2,1)S(1)} %add_convert_fusion.9), channel_id=1, source_target_pairs={{0,2},{2,0},{1,3},{3,1},{4,6},{6,4},{5,7},{7,5},{8,10},{10,8},{9,1... | collective-permute-start | bytes 1179656 | tf_op jit(solution)/shard_map/ppermute | solution.py:485
  61.1 27.4 %collective-permute-start.6 = (bf16[4,256,192]{2,1,0:T(8,128)(2,1)S(1)}, bf16[4,256,192]{2,1,0:T(8,128)(2,1)}, u32[]{:S(2)}, u32[]{:S(2)}) collective-permute-start(bf16[4,256,192]{2,1,0:T(8,128)(2,1)S(1)} %copy.112.go), channel_id=1, source_target_pairs={{0,1},{1,0},{2,3},{3,2},{4,5},{5,4},{6,7},{7,6},{8,9},{9,8},{10,11... | collective-permute-start | bytes 1179656 | tf_op jit(solution)/shard_map/ppermute | solution.py:481
  69.7 18.9 %collective-permute-start.8 = (bf16[4,256,192]{2,1,0:T(8,128)(2,1)}, bf16[4,256,192]{2,1,0:T(8,128)(2,1)}, u32[]{:S(2)}, u32[]{:S(2)}) collective-permute-start(bf16[4,256,192]{2,1,0:T(8,128)(2,1)} %collective-permute-done.7.gx), channel_id=1, source_target_pairs={{0,1},{1,0},{2,3},{3,2},{4,5},{5,4},{6,7},{7,6},{8,9},{9,8},{10,11... | collective-permute-start | bytes 1179656 | tf_op jit(solution)/shard_map/ppermute | solution.py:481
  78.8 9.7 %collective-permute-start.5 = (bf16[256,768]{1,0:T(8,128)(2,1)}, bf16[256,768]{1,0:T(8,128)(2,1)}, u32[]{:S(2)}, u32[]{:S(2)}) collective-permute-start(bf16[256,768]{1,0:T(8,128)(2,1)} %add_convert_fusion.10.att_own), channel_id=1, source_target_pairs={{0,1},{1,0},{2,3},{3,2},{4,5},{5,4},{6,7},{7,6},{8,9},{9,8},{10,11... | collective-permute-start | bytes 1179656 | tf_op jit(solution)/shard_map/ppermute | solution.py:481
  87.8 20.6 %collective-permute-start.11 = (bf16[256,768]{1,0:T(8,128)(2,1)}, bf16[256,768]{1,0:T(8,128)(2,1)}, u32[]{:S(2)}, u32[]{:S(2)}) collective-permute-start(bf16[256,768]{1,0:T(8,128)(2,1)} %add_convert_fusion.8.att_own), channel_id=1, source_target_pairs={{0,1},{1,0},{2,3},{3,2},{4,5},{5,4},{6,7},{7,6},{8,9},{9,8},{10,11... | collective-permute-start | bytes 1179656 | tf_op jit(solution)/shard_map/ppermute | solution.py:481
  107.8 30.5 %collective-permute-start.16 = (bf16[256,768]{1,0:T(8,128)(2,1)}, bf16[256,768]{1,0:T(8,128)(2,1)S(1)}, u32[]{:S(2)}, u32[]{:S(2)}) collective-permute-start(bf16[256,768]{1,0:T(8,128)(2,1)} %get-tuple-element.81), channel_id=1, source_target_pairs={{0,1},{1,0},{2,3},{3,2},{4,5},{5,4},{6,7},{7,6},{8,9},{9,8},{10,11... | collective-permute-start | bytes 1179656 | tf_op jit(solution)/shard_map/ppermute | solution.py:481
  108.3 31.3 %collective-permute-start.12 = (bf16[2,2,256,192]{3,2,1,0:T(8,128)(2,1)}, bf16[2,2,256,192]{3,2,1,0:T(8,128)(2,1)}, u32[]{:S(2)}, u32[]{:S(2)}) collective-permute-start(bf16[2,2,256,192]{3,2,1,0:T(8,128)(2,1)} %get-tuple-element.77), channel_id=1, source_target_pairs={{0,1},{1,0},{2,3},{3,2},{4,5},{5,4},{6,7},{7,6},{8,9},{9,8},{10,11... | collective-permute-start | bytes 1179656 | tf_op jit(solution)/shard_map/ppermute | solution.py:481
  130.6 11.8 %collective-permute-start.19 = (bf16[256,768]{1,0:T(8,128)(2,1)}, bf16[256,768]{1,0:T(8,128)(2,1)S(1)}, u32[]{:S(2)}, u32[]{:S(2)}) collective-permute-start(bf16[256,768]{1,0:T(8,128)(2,1)} %get-tuple-element.88), channel_id=1, source_target_pairs={{0,1},{1,0},{2,3},{3,2},{4,5},{5,4},{6,7},{7,6},{8,9},{9,8},{10,11... | collective-permute-start | bytes 1179656 | tf_op jit(solution)/shard_map/ppermute | solution.py:481
  131.0 12.7 %collective-permute-start.14 = (bf16[2,2,256,192]{3,2,1,0:T(8,128)(2,1)}, bf16[2,2,256,192]{3,2,1,0:T(8,128)(2,1)S(1)}, u32[]{:S(2)}, u32[]{:S(2)}) collective-permute-start(bf16[2,2,256,192]{3,2,1,0:T(8,128)(2,1)} %get-tuple-element.79), channel_id=1, source_target_pairs={{0,1},{1,0},{2,3},{3,2},{4,5},{5,4},{6,7},{7,6},{8,9},{9,8},{10,11... | collective-permute-start | bytes 1179656 | tf_op jit(solution)/shard_map/ppermute | solution.py:481
  134.1 16.2 %collective-permute-start.47 = (bf16[4,96,768]{2,1,0:T(8,128)(2,1)S(1)}, bf16[4,96,768]{2,1,0:T(8,128)(2,1)S(1)}, u32[]{:S(2)}, u32[]{:S(2)}) collective-permute-start(bf16[4,96,768]{2,1,0:T(8,128)(2,1)S(1)} %dynamic-slice_bitcast_fusion), channel_id=1, source_target_pairs={{0,4},{4,0},{8,12},{12,8},{16,20},{20,16},{24,28},{28,24},{1,5},{5... | collective-permute-start | bytes 1769480 | tf_op jit(solution)/shard_map/ppermute | solution.py:507
  138.3 36.0 %collective-permute-start.39 = (bf16[4,96,768]{2,1,0:T(8,128)(2,1)S(1)}, bf16[4,96,768]{2,1,0:T(8,128)(2,1)S(1)}, u32[]{:S(2)}, u32[]{:S(2)}) collective-permute-start(bf16[4,96,768]{2,1,0:T(8,128)(2,1)S(1)} %dynamic-slice_bitcast_fusion.1), channel_id=1, source_target_pairs={{0,4},{4,0},{8,12},{12,8},{16,20},{20,16},{24,28},{28,24},{1,5},{5... | collective-permute-start | bytes 1769480 | tf_op jit(solution)/shard_map/ppermute | solution.py:507
  139.6 64.7 %collective-permute-start.17 = (bf16[256,768]{1,0:T(8,128)(2,1)}, bf16[256,768]{1,0:T(8,128)(2,1)}, u32[]{:S(2)}, u32[]{:S(2)}) collective-permute-start(bf16[256,768]{1,0:T(8,128)(2,1)} %add_convert_fusion.7), channel_id=1, source_target_pairs={{0,2},{2,0},{1,3},{3,1},{4,6},{6,4},{5,7},{7,5},{8,10},{10,8},{9,1... | collective-permute-start | bytes 1179656 | tf_op jit(solution)/shard_map/ppermute | solution.py:485
  142.4 15.0 %collective-permute-start.13 = (bf16[2,256,192]{2,1,0:T(8,128)(2,1)S(1)}, bf16[2,256,192]{2,1,0:T(8,128)(2,1)S(1)}, u32[]{:S(2)}, u32[]{:S(2)}) collective-permute-start(bf16[2,256,192]{2,1,0:T(8,128)(2,1)S(1)} %dynamic-slice_bitcast_fusion.6), channel_id=1, source_target_pairs={{0,2},{2,0},{1,3},{3,1},{4,6},{6,4},{5,7},{7,5},{8,10},{10,8},{9,1... | collective-permute-start | bytes 589832 | tf_op jit(solution)/shard_map/ppermute | solution.py:485
  143.7 61.8 %collective-permute-start.20 = (bf16[256,768]{1,0:T(8,128)(2,1)}, bf16[256,768]{1,0:T(8,128)(2,1)}, u32[]{:S(2)}, u32[]{:S(2)}) collective-permute-start(bf16[256,768]{1,0:T(8,128)(2,1)} %add_convert_fusion.5), channel_id=1, source_target_pairs={{0,2},{2,0},{1,3},{3,1},{4,6},{6,4},{5,7},{7,5},{8,10},{10,8},{9,1... | collective-permute-start | bytes 1179656 | tf_op jit(solution)/shard_map/ppermute | solution.py:485
  150.3 20.3 %collective-permute-start.15 = (bf16[2,256,192]{2,1,0:T(8,128)(2,1)S(1)}, bf16[2,256,192]{2,1,0:T(8,128)(2,1)S(1)}, u32[]{:S(2)}, u32[]{:S(2)}) collective-permute-start(bf16[2,256,192]{2,1,0:T(8,128)(2,1)S(1)} %dynamic-slice_bitcast_fusion.5), channel_id=1, source_target_pairs={{0,2},{2,0},{1,3},{3,1},{4,6},{6,4},{5,7},{7,5},{8,10},{10,8},{9,1... | collective-permute-start | bytes 589832 | tf_op jit(solution)/shard_map/ppermute | solution.py:485
  157.4 22.9 %collective-permute-start.48 = (bf16[96,768]{1,0:T(8,128)(2,1)}, bf16[96,768]{1,0:T(8,128)(2,1)}, u32[]{:S(2)}, u32[]{:S(2)}) collective-permute-start(bf16[96,768]{1,0:T(8,128)(2,1)} %get-tuple-element.188), channel_id=1, source_target_pairs={{0,8},{4,12},{8,16},{12,20},{16,24},{20,28},{24,0},{28,4},{1,9},{5... | collective-permute-start | bytes 442376 | tf_op jit(solution)/shard_map/ppermute | solution.py:531
  170.6 10.7 %collective-permute-start.50 = (bf16[96,768]{1,0:T(8,128)(2,1)}, bf16[96,768]{1,0:T(8,128)(2,1)}, u32[]{:S(2)}, u32[]{:S(2)}) collective-permute-start(bf16[96,768]{1,0:T(8,128)(2,1)} %get-tuple-element.189), channel_id=1, source_target_pairs={{0,24},{4,28},{8,0},{12,4},{16,8},{20,12},{24,16},{28,20},{1,25},{... | collective-permute-start | bytes 442376 | tf_op jit(solution)/shard_map/ppermute | solution.py:531
  174.3 9.9 %collective-permute-start.49 = (bf16[96,768]{1,0:T(8,128)(2,1)}, bf16[96,768]{1,0:T(8,128)(2,1)}, u32[]{:S(2)}, u32[]{:S(2)}) collective-permute-start(bf16[96,768]{1,0:T(8,128)(2,1)} %get-tuple-element.190), channel_id=1, source_target_pairs={{0,16},{4,20},{8,24},{12,28},{16,0},{20,4},{24,8},{28,12},{1,17},{... | collective-permute-start | bytes 442376 | tf_op jit(solution)/shard_map/ppermute | solution.py:531
  181.3 15.0 %collective-permute-start.42 = (bf16[96,768]{1,0:T(8,128)(2,1)S(1)}, bf16[96,768]{1,0:T(8,128)(2,1)S(1)}, u32[]{:S(2)}, u32[]{:S(2)}) collective-permute-start(bf16[96,768]{1,0:T(8,128)(2,1)S(1)} %get-tuple-element.192), channel_id=1, source_target_pairs={{0,24},{4,28},{8,0},{12,4},{16,8},{20,12},{24,16},{28,20},{1,25},{... | collective-permute-start | bytes 442376 | tf_op jit(solution)/shard_map/ppermute | solution.py:531
  184.2 18.5 %collective-permute-start.41 = (bf16[96,768]{1,0:T(8,128)(2,1)S(1)}, bf16[96,768]{1,0:T(8,128)(2,1)S(1)}, u32[]{:S(2)}, u32[]{:S(2)}) collective-permute-start(bf16[96,768]{1,0:T(8,128)(2,1)S(1)} %get-tuple-element.193), channel_id=1, source_target_pairs={{0,16},{4,20},{8,24},{12,28},{16,0},{20,4},{24,8},{28,12},{1,17},{... | collective-permute-start | bytes 442376 | tf_op jit(solution)/shard_map/ppermute | solution.py:531
  188.9 23.1 %collective-permute-start.52 = (bf16[96,768]{1,0:T(8,128)(2,1)S(1)}, bf16[96,768]{1,0:T(8,128)(2,1)S(1)}, u32[]{:S(2)}, u32[]{:S(2)}) collective-permute-start(bf16[96,768]{1,0:T(8,128)(2,1)S(1)} %get-tuple-element.175), channel_id=1, source_target_pairs={{0,16},{4,20},{8,24},{12,28},{16,0},{20,4},{24,8},{28,12},{1,17},{... | collective-permute-start | bytes 442376 | tf_op jit(solution)/shard_map/ppermute | solution.py:531
  196.3 12.5 %collective-permute-start.51 = (bf16[96,768]{1,0:T(8,128)(2,1)S(1)}, bf16[96,768]{1,0:T(8,128)(2,1)S(1)}, u32[]{:S(2)}, u32[]{:S(2)}) collective-permute-start(bf16[96,768]{1,0:T(8,128)(2,1)S(1)} %get-tuple-element.175), channel_id=1, source_target_pairs={{0,8},{4,12},{8,16},{12,20},{16,24},{20,28},{24,0},{28,4},{1,9},{5... | collective-permute-start | bytes 442376 | tf_op jit(solution)/shard_map/ppermute | solution.py:531
  202.6 10.0 %collective-permute-start.53 = (bf16[96,768]{1,0:T(8,128)(2,1)S(1)}, bf16[96,768]{1,0:T(8,128)(2,1)S(1)}, u32[]{:S(2)}, u32[]{:S(2)}) collective-permute-start(bf16[96,768]{1,0:T(8,128)(2,1)S(1)} %get-tuple-element.175), channel_id=1, source_target_pairs={{0,24},{4,28},{8,0},{12,4},{16,8},{20,12},{24,16},{28,20},{1,25},{... | collective-permute-start | bytes 442376 | tf_op jit(solution)/shard_map/ppermute | solution.py:531
  204.3 15.3 %collective-permute-start.44 = (bf16[96,768]{1,0:T(8,128)(2,1)S(1)}, bf16[96,768]{1,0:T(8,128)(2,1)S(1)}, u32[]{:S(2)}, u32[]{:S(2)}) collective-permute-start(bf16[96,768]{1,0:T(8,128)(2,1)S(1)} %get-tuple-element.177), channel_id=1, source_target_pairs={{0,16},{4,20},{8,24},{12,28},{16,0},{20,4},{24,8},{28,12},{1,17},{... | collective-permute-start | bytes 442376 | tf_op jit(solution)/shard_map/ppermute | solution.py:531
  208.8 11.7 %collective-permute-start.45 = (bf16[96,768]{1,0:T(8,128)(2,1)S(1)}, bf16[96,768]{1,0:T(8,128)(2,1)S(1)}, u32[]{:S(2)}, u32[]{:S(2)}) collective-permute-start(bf16[96,768]{1,0:T(8,128)(2,1)S(1)} %get-tuple-element.177), channel_id=1, source_target_pairs={{0,24},{4,28},{8,0},{12,4},{16,8},{20,12},{24,16},{28,20},{1,25},{... | collective-permute-start | bytes 442376 | tf_op jit(solution)/shard_map/ppermute | solution.py:531
  212.0 10.5 %collective-permute-start.18 = (bf16[256,768]{1,0:T(8,128)(2,1)S(1)}, bf16[256,768]{1,0:T(8,128)(2,1)S(1)}, u32[]{:S(2)}, u32[]{:S(2)}) collective-permute-start(bf16[256,768]{1,0:T(8,128)(2,1)S(1)} %add_convert_fusion.6.gs_own), channel_id=1, source_target_pairs={{0,1},{1,0},{2,3},{3,2},{4,5},{5,4},{6,7},{7,6},{8,9},{9,8},{10,11... | collective-permute-start | bytes 1179656 | tf_op jit(solution)/shard_map/ppermute | solution.py:481
  212.7 36.3 %collective-permute-start.21 = (bf16[256,768]{1,0:T(8,128)(2,1)S(1)}, bf16[256,768]{1,0:T(8,128)(2,1)S(1)}, u32[]{:S(2)}, u32[]{:S(2)}) collective-permute-start(bf16[256,768]{1,0:T(8,128)(2,1)S(1)} %add_convert_fusion.4.gs_own), channel_id=1, source_target_pairs={{0,1},{1,0},{2,3},{3,2},{4,5},{5,4},{6,7},{7,6},{8,9},{9,8},{10,11... | collective-permute-start | bytes 1179656 | tf_op jit(solution)/shard_map/ppermute | solution.py:481
  213.9 74.9 %collective-permute-start.54 = (bf16[4,96,768]{2,1,0:T(8,128)(2,1)}, bf16[4,96,768]{2,1,0:T(8,128)(2,1)}, u32[]{:S(2)}, u32[]{:S(2)}) collective-permute-start(bf16[4,96,768]{2,1,0:T(8,128)(2,1)} %bitcast_dynamic-update-slice_fusion), channel_id=1, source_target_pairs={{0,4},{4,0},{8,12},{12,8},{16,20},{20,16},{24,28},{28,24},{1,5},{5... | collective-permute-start | bytes 1769480 | tf_op jit(solution)/shard_map/ppermute | solution.py:507
  221.2 70.3 %collective-permute-start.46 = (bf16[4,96,768]{2,1,0:T(8,128)(2,1)}, bf16[4,96,768]{2,1,0:T(8,128)(2,1)}, u32[]{:S(2)}, u32[]{:S(2)}) collective-permute-start(bf16[4,96,768]{2,1,0:T(8,128)(2,1)} %bitcast_dynamic-update-slice_fusion.4), channel_id=1, source_target_pairs={{0,4},{4,0},{8,12},{12,8},{16,20},{20,16},{24,28},{28,24},{1,5},{5... | collective-permute-start | bytes 1769480 | tf_op jit(solution)/shard_map/ppermute | solution.py:507
  275.3 34.7 %collective-permute-start.22 = (bf16[2,2,256,192]{3,2,1,0:T(8,128)(2,1)}, bf16[2,2,256,192]{3,2,1,0:T(8,128)(2,1)}, u32[]{:S(2)}, u32[]{:S(2)}) collective-permute-start(bf16[2,2,256,192]{3,2,1,0:T(8,128)(2,1)} %get-tuple-element.95), channel_id=1, source_target_pairs={{0,1},{1,0},{2,3},{3,2},{4,5},{5,4},{6,7},{7,6},{8,9},{9,8},{10,11... | collective-permute-start | bytes 1179656 | tf_op jit(solution)/shard_map/ppermute | solution.py:481
  276.2 36.6 %collective-permute-start.24 = (bf16[2,2,256,192]{3,2,1,0:T(8,128)(2,1)}, bf16[2,2,256,192]{3,2,1,0:T(8,128)(2,1)}, u32[]{:S(2)}, u32[]{:S(2)}) collective-permute-start(bf16[2,2,256,192]{3,2,1,0:T(8,128)(2,1)} %get-tuple-element.97), channel_id=1, source_target_pairs={{0,1},{1,0},{2,3},{3,2},{4,5},{5,4},{6,7},{7,6},{8,9},{9,8},{10,11... | collective-permute-start | bytes 1179656 | tf_op jit(solution)/shard_map/ppermute | solution.py:481
  287.9 26.7 %collective-permute-start.31 = (bf16[4,96,768]{2,1,0:T(8,128)(2,1)S(1)}, bf16[4,96,768]{2,1,0:T(8,128)(2,1)S(1)}, u32[]{:S(2)}, u32[]{:S(2)}) collective-permute-start(bf16[4,96,768]{2,1,0:T(8,128)(2,1)S(1)} %dynamic-slice_bitcast_fusion.2), channel_id=1, source_target_pairs={{0,4},{4,0},{8,12},{12,8},{16,20},{20,16},{24,28},{28,24},{1,5},{5... | collective-permute-start | bytes 1769480 | tf_op jit(solution)/shard_map/ppermute | solution.py:507
  288.8 16.9 %collective-permute-start.28 = (f32[1,252,128]{2,1,0:T(8,128)S(1)}, f32[1,252,128]{2,1,0:T(8,128)S(1)}, u32[]{:S(2)}, u32[]{:S(2)}) collective-permute-start(f32[1,252,128]{2,1,0:T(8,128)S(1)} %maximum_bitcast_fusion), channel_id=1, source_target_pairs={{0,4},{4,0},{8,12},{12,8},{16,20},{20,16},{24,28},{28,24},{1,5},{5... | collective-permute-start | bytes 387080 | tf_op jit(solution)/shard_map/ppermute | solution.py:507
  306.4 26.4 %collective-permute-start.29 = (f32[2,252,128]{2,1,0:T(8,128)}, f32[2,252,128]{2,1,0:T(8,128)S(1)}, u32[]{:S(2)}, u32[]{:S(2)}) collective-permute-start(f32[2,252,128]{2,1,0:T(8,128)} %pad_maximum_fusion.6), channel_id=1, source_target_pairs={{0,8},{4,12},{8,0},{12,4},{16,24},{20,28},{24,16},{28,20},{1,9},{5... | collective-permute-start | bytes 774152 | tf_op jit(solution)/shard_map/ppermute | solution.py:507
  311.2 9.3 %collective-permute-start.23 = (bf16[2,256,192]{2,1,0:T(8,128)(2,1)S(1)}, bf16[2,256,192]{2,1,0:T(8,128)(2,1)S(1)}, u32[]{:S(2)}, u32[]{:S(2)}) collective-permute-start(bf16[2,256,192]{2,1,0:T(8,128)(2,1)S(1)} %dynamic-slice_bitcast_fusion.4), channel_id=1, source_target_pairs={{0,2},{2,0},{1,3},{3,1},{4,6},{6,4},{5,7},{7,5},{8,10},{10,8},{9,1... | collective-permute-start | bytes 589832 | tf_op jit(solution)/shard_map/ppermute | solution.py:485
  314.0 9.6 %collective-permute-start.25 = (bf16[2,256,192]{2,1,0:T(8,128)(2,1)S(1)}, bf16[2,256,192]{2,1,0:T(8,128)(2,1)S(1)}, u32[]{:S(2)}, u32[]{:S(2)}) collective-permute-start(bf16[2,256,192]{2,1,0:T(8,128)(2,1)S(1)} %dynamic-slice_bitcast_fusion.3), channel_id=1, source_target_pairs={{0,2},{2,0},{1,3},{3,1},{4,6},{6,4},{5,7},{7,5},{8,10},{10,8},{9,1... | collective-permute-start | bytes 589832 | tf_op jit(solution)/shard_map/ppermute | solution.py:485
  320.5 9.4 %collective-permute-start.33 = (bf16[96,768]{1,0:T(8,128)(2,1)S(1)}, bf16[96,768]{1,0:T(8,128)(2,1)S(1)}, u32[]{:S(2)}, u32[]{:S(2)}) collective-permute-start(bf16[96,768]{1,0:T(8,128)(2,1)S(1)} %get-tuple-element.196), channel_id=1, source_target_pairs={{0,16},{4,20},{8,24},{12,28},{16,0},{20,4},{24,8},{28,12},{1,17},{... | collective-permute-start | bytes 442376 | tf_op jit(solution)/shard_map/ppermute | solution.py:531
  331.6 9.0 %collective-permute-start.35 = (bf16[96,768]{1,0:T(8,128)(2,1)}, bf16[96,768]{1,0:T(8,128)(2,1)}, u32[]{:S(2)}, u32[]{:S(2)}) collective-permute-start(bf16[96,768]{1,0:T(8,128)(2,1)} %get-tuple-element.179), channel_id=1, source_target_pairs={{0,8},{4,12},{8,16},{12,20},{16,24},{20,28},{24,0},{28,4},{1,9},{5... | collective-permute-start | bytes 442376 | tf_op jit(solution)/shard_map/ppermute | solution.py:531
  332.8 36.6 %collective-permute-start.30 = (f32[4,252,128]{2,1,0:T(8,128)S(1)}, f32[4,252,128]{2,1,0:T(8,128)S(1)}, u32[]{:S(2)}, u32[]{:S(2)}) collective-permute-start(f32[4,252,128]{2,1,0:T(8,128)S(1)} %pad_maximum_fusion.5), channel_id=1, source_target_pairs={{0,16},{4,20},{8,24},{12,28},{16,0},{20,4},{24,8},{28,12},{1,17},{... | collective-permute-start | bytes 1548296 | tf_op jit(solution)/shard_map/ppermute | solution.py:507
  335.6 31.3 %collective-permute-start.36 = (bf16[96,768]{1,0:T(8,128)(2,1)}, bf16[96,768]{1,0:T(8,128)(2,1)S(1)}, u32[]{:S(2)}, u32[]{:S(2)}) collective-permute-start(bf16[96,768]{1,0:T(8,128)(2,1)} %get-tuple-element.179), channel_id=1, source_target_pairs={{0,16},{4,20},{8,24},{12,28},{16,0},{20,4},{24,8},{28,12},{1,17},{... | collective-permute-start | bytes 442376 | tf_op jit(solution)/shard_map/ppermute | solution.py:531
  335.8 31.7 %collective-permute-start.37 = (bf16[96,768]{1,0:T(8,128)(2,1)}, bf16[96,768]{1,0:T(8,128)(2,1)S(1)}, u32[]{:S(2)}, u32[]{:S(2)}) collective-permute-start(bf16[96,768]{1,0:T(8,128)(2,1)} %get-tuple-element.179), channel_id=1, source_target_pairs={{0,24},{4,28},{8,0},{12,4},{16,8},{20,12},{24,16},{28,20},{1,25},{... | collective-permute-start | bytes 442376 | tf_op jit(solution)/shard_map/ppermute | solution.py:531
  368.2 45.8 %collective-permute-start.38 = (bf16[4,96,768]{2,1,0:T(8,128)(2,1)}, bf16[4,96,768]{2,1,0:T(8,128)(2,1)}, u32[]{:S(2)}, u32[]{:S(2)}) collective-permute-start(bf16[4,96,768]{2,1,0:T(8,128)(2,1)} %bitcast_dynamic-update-slice_fusion.8), channel_id=1, source_target_pairs={{0,4},{4,0},{8,12},{12,8},{16,20},{20,16},{24,28},{28,24},{1,5},{5... | collective-permute-start | bytes 1769480 | tf_op jit(solution)/shard_map/ppermute | solution.py:507
  (55 other events, 551.2 us)

commit v2 on v1

v2 whole, which is shorter than its diff:
```python
import functools
import math

import jax
import jax.numpy as jnp
from jax import lax
from jax.experimental import pallas as pl
from jax.experimental.pallas import tpu as pltpu
from jax.sharding import PartitionSpec as P

HEAD_DIM = 64
FREQ = 256
SIDE = 16
PAIR = 2

BF = jnp.bfloat16
F32 = jnp.float32
HIGHEST = lax.Precision.HIGHEST
LANES = 128
ROWS = 128
BAND = 64
GELU_A = math.sqrt(2.0 / math.pi)
GELU_B = 0.044715
EPS = 1e-06
VMEM_LIMIT = 60 * 1024 * 1024


def dot(a, b):
    return lax.dot_general(a, b, (((1,), (0,)), ((), ())), preferred_element_type=F32)


def dot_nt(a, b):
    return lax.dot_general(a, b, (((1,), (1,)), ((), ())), preferred_element_type=F32)


def dot_tn(a, b):
    return lax.dot_general(a, b, (((0,), (0,)), ((), ())), preferred_element_type=F32)


def column_of(rows):
    return lax.broadcasted_iota(jnp.int32, (rows, LANES), 0) % SIDE


def from_left(v):
    moved = pltpu.roll(v, 1, 0)
    return jnp.where(column_of(v.shape[0]) == 0, 0.0, moved)


def from_right(v):
    moved = pltpu.roll(v, v.shape[0] - 1, 0)
    return jnp.where(column_of(v.shape[0]) == SIDE - 1, 0.0, moved)


def conv_band(padded, at, lanes, kern):
    rows = [padded[pl.ds(at + SIDE * r, BAND), lanes] for r in range(3)]
    mixed = [
        rows[0] * kern[c] + rows[1] * kern[3 + c] + rows[2] * kern[6 + c] for c in range(3)
    ]
    return from_left(mixed[0]) + mixed[1] + from_right(mixed[2])


def conv_back_band(padded_grad, at, lanes, kern):
    wide = padded_grad[pl.ds(at, BAND + 2 * SIDE), lanes]
    shifted = [from_right(wide), wide, from_left(wide)]
    total = None
    for r in range(3):
        for c in range(3):
            low = SIDE * (2 - r)
            term = shifted[c][low : low + BAND] * kern[3 * r + c]
            total = term if total is None else total + term
    return total, [s[SIDE : SIDE + BAND] for s in shifted]


def fold_rows(v):
    total = v[0:8]
    for at in range(8, v.shape[0], 8):
        total = total + v[at : at + 8]
    return total


def taps_of(kern_ref, lanes):
    block = kern_ref[:, lanes]
    return [block[t : t + 1] for t in range(9)]


def zero_edges(ref):
    edge = jnp.zeros((SIDE, ref.shape[1]), F32)
    tall = ref.shape[0] // PAIR
    for rel in range(PAIR):
        ref[rel * tall : rel * tall + SIDE, :] = edge
        ref[(rel + 1) * tall - SIDE : (rel + 1) * tall, :] = edge


def inside(ref, rel):
    tall = ref.shape[0] // PAIR
    return slice(rel * tall + SIDE, (rel + 1) * tall - SIDE)


def gather_features(n, lats, parts, held, out):
    _, share, tokens = parts[0].shape
    for rel, lat in enumerate(lats):
        for step, part in enumerate(parts):
            held[jnp.bitwise_xor(n, step)] = part[lat]
        out[rel * tokens : (rel + 1) * tokens, :] = held[...].reshape(len(parts) * share, tokens).T


def by_core(core, lats, low, share, keep_out, send_out):
    tokens = low.shape[0] // PAIR
    for rel, lat in enumerate(lats):
        turned = low[rel * tokens : (rel + 1) * tokens, :].T
        for parity in range(2):

            @pl.when(core == parity)
            def _():
                for x in range(2):
                    here, there = 2 * x + parity, 2 * x + 1 - parity
                    keep_out[x, lat] = turned[here * share : (here + 1) * share]
                    send_out[x, lat] = turned[there * share : (there + 1) * share]


def norm_stats(v):
    width = v.shape[1]
    mean = jnp.sum(v, -1, keepdims=True) * (1.0 / width)
    center = v - mean
    spread = jnp.sum(center * center, -1, keepdims=True) * (1.0 / width)
    scale = lax.rsqrt(spread + EPS)
    return center * scale, scale


def head_masks(share):
    lane = lax.broadcasted_iota(jnp.int32, (1, share), 1) // HEAD_DIM
    return [(lane == h).astype(F32).astype(BF) for h in range(share // HEAD_DIM)]


def half_rows(v, parity):
    tokens, width = v.shape
    split = v.reshape(tokens // (2 * SIDE), 2, SIDE, width)
    return split[:, parity].reshape(tokens // 2, width)


def join_rows(even, odd):
    half, width = even.shape
    both = jnp.stack([even.reshape(half // SIDE, SIDE, width), odd.reshape(half // SIDE, SIDE, width)], 1)
    return both.reshape(2 * half, width)


def softmax_rows(queries, keys):
    scores = dot_nt(queries, keys) * (1.0 / math.sqrt(HEAD_DIM))
    rows = lax.broadcasted_iota(jnp.int32, scores.shape, 0)
    cols = lax.broadcasted_iota(jnp.int32, scores.shape, 1)
    same = (rows + cols) % 2 == 0
    scores = jnp.where(same, scores, -1e30)
    top = jnp.max(scores, -1, keepdims=True)
    grown = jnp.where(same, jnp.exp(scores - top), 0.0)
    return grown / jnp.sum(grown, -1, keepdims=True)


def beside(stacked, heads):
    rows = stacked.shape[0] // heads
    return jnp.concatenate([stacked[h * rows : (h + 1) * rows] for h in range(heads)], axis=1)


def lane_loop(width, body):
    count = width // LANES

    def step(j, carry):
        body(j // count, pl.ds(pl.multiple_of((j % count) * LANES, LANES), LANES))
        return carry

    lax.fori_loop(0, PAIR * count, step, 0)


def row_loop(tokens, body):
    def step(j, carry):
        body(pl.multiple_of(j * ROWS, ROWS))
        return carry

    lax.fori_loop(0, tokens // ROWS, step, 0)


def pair_loop(body):
    def step(j, carry):
        body(j)
        return carry

    lax.fori_loop(0, PAIR, step, 0)


def attn_kernel_body(
    s_ref, xo, xc, xx, xd, mod, kern, wqkv, wout,
    full_out, grouped_out, q_out, k_out, v_out, ctx_out, keep_out, send_out,
    held, padded,
):
    n = s_ref[0]
    core = jnp.bitwise_and(n, 1)
    share, tokens = xo.shape[1], xo.shape[2]
    width = full_out.shape[1]
    tall = tokens + 2 * SIDE
    lats = [core, 1 - core]
    gather_features(n, lats, (xo, xc, xx, xd), held, full_out)
    zero_edges(padded)
    for rel, lat in enumerate(lats):
        shift, scale = mod[lat, 0:1, :], 1.0 + mod[lat, 1:2, :]

        def rows(at):
            normed, _ = norm_stats(full_out[pl.ds(at + rel * tokens, ROWS), :].astype(F32))
            padded[pl.ds(at + rel * tall + SIDE, ROWS), :] = normed * scale + shift

        row_loop(tokens, rows)

    def lanes(rel, at):
        taps = taps_of(kern, at)
        for band in range(0, tokens, BAND):
            here = pl.ds(pl.multiple_of(rel * tokens + band, BAND), BAND)
            grouped_out[here, at] = conv_band(padded, pl.multiple_of(rel * tall + band, SIDE), at, taps).astype(BF)

    lane_loop(width, lanes)
    grouped = grouped_out[...]
    q_out[...] = dot_nt(grouped, wqkv[0]).astype(BF)
    k_out[...] = dot_nt(grouped, wqkv[1]).astype(BF)
    v_out[...] = dot_nt(grouped, wqkv[2]).astype(BF)
    masks = head_masks(share)
    heads = len(masks)

    def attend(rel):
        here = pl.ds(pl.multiple_of(rel * tokens, tokens), tokens)
        query, key, value = q_out[here, :], k_out[here, :], v_out[here, :]
        parts = []
        for parity in range(2):
            q = half_rows(query, parity)
            k = half_rows(key, parity)
            v = half_rows(value, parity)
            probs = softmax_rows(jnp.concatenate([q * m for m in masks], axis=0), k)
            low = beside(probs.astype(BF), heads)
            parts.append(dot(low, jnp.concatenate([v * m for m in masks], axis=0)).astype(BF))
        ctx_out[here, :] = join_rows(*parts)

    pair_loop(attend)
    keep_out[...] = dot(ctx_out[0:tokens, :], wout[...]).astype(BF)
    send_out[...] = dot(ctx_out[tokens : 2 * tokens, :], wout[...]).astype(BF)


def ffn_kernel_body(
    s_ref, full, att_own, att_peer, go, gc, gx, gd, mod, up, down, kern,
    g_out, second_out, active_out, gfed_out, ghid_out, keep_out, send_out, mods_out, kgrad_out, fkeep_out, fsend_out,
    held, padded, slope, gpad, mid, fed, low, sums,
):
    n = s_ref[0]
    core = jnp.bitwise_and(n, 1)
    share, tokens = go.shape[1], go.shape[2]
    units = up.shape[1]
    tall = tokens + 2 * SIDE
    lats = [core, 1 - core]
    gather_features(n, lats, (go, gc, gx, gd), held, g_out)
    zero_edges(padded)
    zero_edges(gpad)
    kgrad_out[...] = jnp.zeros(kgrad_out.shape, F32)
    for rel, (lat, att) in enumerate(zip(lats, (att_own, att_peer))):
        gate1, gate2 = mod[lat, 0:1, :], mod[lat, 3:4, :]
        shift, scale = mod[lat, 1:2, :], 1.0 + mod[lat, 2:3, :]

        def rows(at):
            here = pl.ds(at + rel * tokens, ROWS)
            middle = full[here, :].astype(F32) + gate1 * att[pl.ds(at, ROWS), :].astype(F32)
            mid[here, :] = middle
            normed, _ = norm_stats(middle)
            second_out[here, :] = (normed * scale + shift).astype(BF)
            gfed_out[here, :] = (gate2 * g_out[here, :].astype(F32)).astype(BF)

        row_loop(tokens, rows)

    hidden = dot(second_out[...], up[...])
    for rel in range(PAIR):
        padded[inside(padded, rel), :] = hidden[rel * tokens : (rel + 1) * tokens]

    def lanes(rel, at):
        taps = taps_of(kern, at)
        for band in range(0, tokens, BAND):
            here = pl.ds(pl.multiple_of(rel * tokens + band, BAND), BAND)
            mixed = conv_band(padded, pl.multiple_of(rel * tall + band, SIDE), at, taps)
            square = mixed * mixed
            curve = jnp.tanh(GELU_A * mixed * (1.0 + GELU_B * square))
            half = 0.5 * (1.0 + curve)
            active_out[here, at] = (mixed * half).astype(BF)
            slope[here, at] = half + (0.5 * GELU_A) * mixed * (1.0 - curve * curve) * (
                1.0 + (3.0 * GELU_B) * square
            )

    lane_loop(units, lanes)
    fed[...] = dot(active_out[...], down[...])
    sums[...] = jnp.zeros(sums.shape, F32)
    for rel, lat in enumerate(lats):
        gate2 = mod[lat, 3:4, :]

        def rows_fed(at):
            here = pl.ds(at + rel * tokens, ROWS)
            term = fed[here, :]
            sums[rel] += fold_rows(term * g_out[here, :].astype(F32))
            low[here, :] = (gate2 * term + 0.25 * mid[here, :]).astype(BF)

        row_loop(tokens, rows_fed)
        mods_out[lat] = jnp.sum(sums[rel], 0, keepdims=True)
    by_core(core, lats, low, share, fkeep_out, fsend_out)
    gact = dot_nt(gfed_out[...], down[...]).astype(BF).astype(F32)
    for rel in range(PAIR):
        here = slice(rel * tokens, (rel + 1) * tokens)
        gpad[inside(gpad, rel), :] = gact[here] * slope[here, :]

    def lanes_back(rel, at):
        taps = taps_of(kern, at)
        sums = [None] * 9
        for band in range(0, tokens, BAND):
            here = pl.ds(pl.multiple_of(rel * tokens + band, BAND), BAND)
            base = pl.multiple_of(rel * tall + band, SIDE)
            total, shifted = conv_back_band(gpad, base, at, taps)
            ghid_out[here, at] = total.astype(BF)
            for r in range(3):
                values = padded[pl.ds(base + SIDE * r, BAND), at]
                for c in range(3):
                    part = fold_rows(values * shifted[c])
                    sums[3 * r + c] = part if sums[3 * r + c] is None else sums[3 * r + c] + part
        for t in range(9):
            kgrad_out[t : t + 1, at] += jnp.sum(sums[t], 0, keepdims=True)

    lane_loop(units, lanes_back)
    keep_out[...] = dot_nt(ghid_out[0:tokens, :], up[...]).astype(BF)
    send_out[...] = dot_nt(ghid_out[tokens : 2 * tokens, :], up[...]).astype(BF)


def attn_back_body(
    s_ref, full, att_own, att_peer, gs_own, gs_peer, gfull, mod, mod_b, q_in, k_in, v_in, kern, wqkv, wout,
    gatt_out, gq_out, gk_out, gv_out, mods_out, kgrad_out, keep_out, send_out,
    sums2, gmid, normed1, scale1, first, gpad, gback, low,
):
    n = s_ref[0]
    core = jnp.bitwise_and(n, 1)
    tokens = att_own.shape[0]
    width = full.shape[1]
    share = q_in.shape[1]
    tall = tokens + 2 * SIDE
    lats = [core, 1 - core]
    zero_edges(first)
    zero_edges(gpad)
    kgrad_out[...] = jnp.zeros(kgrad_out.shape, F32)
    mods_out[...] = jnp.zeros(mods_out.shape, F32)
    sums2[...] = jnp.zeros(sums2.shape, F32)
    for rel, (lat, att, gs) in enumerate(zip(lats, (att_own, att_peer), (gs_own, gs_peer))):
        gate1 = mod_b[lat, 0:1, :]
        low_scale, low_shift = 1.0 + mod[lat, 1:2, :], mod[lat, 0:1, :]
        scale2 = 1.0 + mod_b[lat, 2:3, :]

        def rows(at):
            here = pl.ds(at + rel * tokens, ROWS)
            x = full[here, :].astype(F32)
            attended = att[pl.ds(at, ROWS), :].astype(F32)
            normed, inv = norm_stats(x + gate1 * attended)
            grad = gs[pl.ds(at, ROWS), :].astype(F32)
            inner = grad * scale2
            mean_a = jnp.sum(inner, -1, keepdims=True) * (1.0 / width)
            mean_b = jnp.sum(inner * normed, -1, keepdims=True) * (1.0 / width)
            whole_grad = gfull[here, :].astype(F32) + inv * (inner - mean_a - normed * mean_b)
            gmid[here, :] = whole_grad
            gatt_out[here, :] = (gate1 * whole_grad).astype(BF)
            sums2[3 * rel] += fold_rows(attended * whole_grad)
            sums2[3 * rel + 1] += fold_rows(grad)
            sums2[3 * rel + 2] += fold_rows(grad * normed)

        row_loop(tokens, rows)

        def rows_first(at):
            here = pl.ds(at + rel * tokens, ROWS)
            normed, inv = norm_stats(full[here, :].astype(F32))
            normed1[here, :] = normed
            scale1[here, :] = jnp.broadcast_to(inv, (ROWS, LANES))
            first[pl.ds(at + rel * tall + SIDE, ROWS), :] = normed * low_scale + low_shift

        row_loop(tokens, rows_first)
        for k in range(3):
            mods_out[lat, 2 + k : 3 + k, :] = 0.25 * jnp.sum(sums2[3 * rel + k], 0, keepdims=True)
    gctx = dot_nt(gatt_out[...], wout[...]).astype(BF)
    gv_out[...] = gctx
    masks = head_masks(share)
    heads = len(masks)
    factor = 1.0 / math.sqrt(HEAD_DIM)

    def attend(rel):
        here = pl.ds(pl.multiple_of(rel * tokens, tokens), tokens)
        query, key, value, grads = q_in[here, :], k_in[here, :], v_in[here, :], gv_out[here, :]
        parts_q, parts_k, parts_v = [], [], []
        for parity in range(2):
            q = half_rows(query, parity)
            k = half_rows(key, parity)
            v = half_rows(value, parity)
            gc = half_rows(grads, parity)
            q_all = jnp.concatenate([q * m for m in masks], axis=0)
            k_all = jnp.concatenate([k * m for m in masks], axis=0)
            gc_all = jnp.concatenate([gc * m for m in masks], axis=0)
            probs = softmax_rows(q_all, k)
            parts_v.append(dot_tn(probs.astype(BF), gc_all).astype(BF))
            gprobs = dot_nt(gc_all, v).astype(BF).astype(F32)
            gscores = (probs * (gprobs - jnp.sum(probs * gprobs, -1, keepdims=True))).astype(BF)
            parts_q.append((dot(beside(gscores, heads), k_all) * factor).astype(BF))
            parts_k.append((dot_tn(gscores, q_all) * factor).astype(BF))
        gq_out[here, :], gk_out[here, :], gv_out[here, :] = join_rows(*parts_q), join_rows(*parts_k), join_rows(*parts_v)

    pair_loop(attend)
    for rel in range(PAIR):
        here = slice(rel * tokens, (rel + 1) * tokens)
        gpad[inside(gpad, rel), :] = (
            dot(gq_out[here, :], wqkv[0]) + dot(gk_out[here, :], wqkv[1]) + dot(gv_out[here, :], wqkv[2])
        )

    def lanes(rel, at):
        taps = taps_of(kern, at)
        sums = [None] * 9
        shift_sum, scale_sum = None, None
        for band in range(0, tokens, BAND):
            here = pl.ds(pl.multiple_of(rel * tokens + band, BAND), BAND)
            base = pl.multiple_of(rel * tall + band, SIDE)
            total, shifted = conv_back_band(gpad, base, at, taps)
            gback[here, at] = total
            part_a, part_b = fold_rows(total), fold_rows(total * normed1[here, at])
            shift_sum = part_a if shift_sum is None else shift_sum + part_a
            scale_sum = part_b if scale_sum is None else scale_sum + part_b
            for r in range(3):
                values = first[pl.ds(base + SIDE * r, BAND), at]
                for c in range(3):
                    part = fold_rows(values * shifted[c])
                    sums[3 * r + c] = part if sums[3 * r + c] is None else sums[3 * r + c] + part
        for t in range(9):
            kgrad_out[t : t + 1, at] += jnp.sum(sums[t], 0, keepdims=True)
        lat = jnp.bitwise_xor(rel, core)
        mods_out[lat, 0:1, at] = jnp.sum(shift_sum, 0, keepdims=True)
        mods_out[lat, 1:2, at] = jnp.sum(scale_sum, 0, keepdims=True)

    lane_loop(width, lanes)
    for rel, lat in enumerate(lats):
        low_scale = 1.0 + mod[lat, 1:2, :]

        def rows_back(at):
            here = pl.ds(at + rel * tokens, ROWS)
            inner = gback[here, :] * low_scale
            normed = normed1[here, :]
            mean_a = jnp.sum(inner, -1, keepdims=True) * (1.0 / width)
            mean_b = jnp.sum(inner * normed, -1, keepdims=True) * (1.0 / width)
            grad = scale1[here, 0:1] * (inner - mean_a - normed * mean_b)
            low[here, :] = (grad + 0.25 * gmid[here, :]).astype(BF)

        row_loop(tokens, rows_back)
    by_core(core, lats, low, share, keep_out, send_out)


def call(body, name, scalars, ins, outs, scratch, flops, held=()):
    bytes_moved = sum(math.prod(o.shape) * o.dtype.itemsize for o, _ in outs)
    count = len(ins)

    def run(*refs):
        body(*refs[: 1 + count], *refs[1 + count + len(held) :])

    return pl.pallas_call(
        run,
        name=name,
        out_shape=[o for o, _ in outs],
        grid_spec=pltpu.PrefetchScalarGridSpec(
            num_scalar_prefetch=1,
            grid=(1,),
            in_specs=[s for _, s in ins] + [pl.BlockSpec(memory_space=pl.ANY)] * len(held),
            out_specs=[s for _, s in outs],
            scratch_shapes=scratch,
        ),
        input_output_aliases={1 + count + k: len(outs) - len(held) + k for k in range(len(held))},
        compiler_params=pltpu.CompilerParams(vmem_limit_bytes=VMEM_LIMIT),
        cost_estimate=pl.CostEstimate(flops=flops, bytes_accessed=bytes_moved, transcendentals=0),
    )(scalars, *[a for a, _ in ins], *held)


def slices_out(slots, slot, share, tokens):
    return (
        jax.ShapeDtypeStruct((2, slots, share, tokens), BF),
        pl.BlockSpec((2, PAIR, share, tokens), lambda i, s: (0, slot, 0, 0)),
    )


def whole(array):
    dims = array.shape
    return (array, pl.BlockSpec(dims, lambda i, s: (0,) * len(dims)))


def whole_out(dims, dtype):
    return (jax.ShapeDtypeStruct(dims, dtype), pl.BlockSpec(dims, lambda i, s: (0,) * len(dims)))


def pair_of(array, pair):
    dims = (PAIR,) + array.shape[1:]
    return (array, pl.BlockSpec(dims, lambda i, s: (pair,) + (0,) * (len(dims) - 1)))


def split_low(v):
    high = v.astype(BF)
    return high, (v - high.astype(F32)).astype(BF)


def rows_product(a, b):
    (ah, al), (bh, bl) = split_low(a), split_low(b)
    return dot_tn(jnp.concatenate([ah, al, ah], 0), jnp.concatenate([bh, bh, bl], 0))


def back_product(a, weight):
    (ah, al), (wh, wl) = split_low(a), split_low(weight)
    return dot_nt(ah, wh) + dot_nt(al, wh) + dot_nt(ah, wl)


def ada_step(factor, gmod, outer, ada, grad_out, bias_out, total):
    grads = gmod[0]
    high, low = split_low(outer[...])
    grad_out[...] = dot_tn(jnp.concatenate([high, low], 0), jnp.concatenate([grads, grads], 0)) * factor
    bias_out[...] = jnp.sum(grads.astype(F32), 0, keepdims=True) * factor
    high, low = split_low(ada[...])
    total[...] += (dot_nt(grads, high) + dot_nt(grads, low)) * factor


def ada_body(factor, gmod, outer, ada, grad_out, bias_out, total_out):
    @pl.when(pl.program_id(0) == 0)
    def _():
        total_out[...] = jnp.zeros(total_out.shape, F32)

    ada_step(factor, gmod, outer, ada, grad_out, bias_out, total_out)


def time_body(
    factor, gmod, outer, ada, held_grad, held_bias, so_far, embedded, inner, inner_pre, outer_pre, time_out,
    grad_out, bias_out, time_out_grad, time_in_grad, total,
):
    del held_grad, held_bias

    @pl.when(pl.program_id(0) == 0)
    def _():
        total[...] = so_far[...]

    ada_step(factor, gmod, outer, ada, grad_out, bias_out, total)

    @pl.when(pl.program_id(0) == pl.num_programs(0) - 1)
    def _():
        outer_grad = total[...] * silu_slope(outer_pre[...])
        time_out_grad[...] = rows_product(inner[...], outer_grad)
        inner_grad = back_product(outer_grad, time_out[...]) * silu_slope(inner_pre[...])
        time_in_grad[...] = rows_product(embedded[...], inner_grad)


def fixed(dims):
    return pl.BlockSpec(dims, lambda i: (0,) * len(dims))


def ada_specs(gmod, outer, ada_weight, first):
    depth, width = outer.shape[1], gmod.shape[2]
    columns = lambda rows: pl.BlockSpec((rows, width), lambda i: (0, i + first))
    ins = [pl.BlockSpec((1,) + gmod.shape[1:], lambda i: (i, 0, 0)), fixed(outer.shape), columns(depth)]
    shapes = [jax.ShapeDtypeStruct((rows, ada_weight.shape[1]), F32) for rows in (depth, 1)]
    return ins, [columns(depth), columns(1)], shapes


def ada_backward(gmod, outer, ada_weight, factor):
    ins, outs, shapes = ada_specs(gmod, outer, ada_weight, 2)
    return pl.pallas_call(
        functools.partial(ada_body, factor),
        name="ada_bwd",
        grid=(gmod.shape[0],),
        in_specs=ins,
        out_specs=outs + [fixed(outer.shape)],
        out_shape=shapes + [jax.ShapeDtypeStruct(outer.shape, F32)],
        compiler_params=pltpu.CompilerParams(vmem_limit_bytes=VMEM_LIMIT),
        cost_estimate=pl.CostEstimate(flops=10**9, bytes_accessed=24 * 10**6, transcendentals=0),
    )(gmod, outer, ada_weight)


def time_backward(gmod, outer, ada_weight, factor, held, so_far, *rest):
    embedded, time_out = rest[0], rest[-1]
    ins, outs, shapes = ada_specs(gmod, outer, ada_weight, 0)
    ins = ins + [pl.BlockSpec(memory_space=pl.ANY)] * 2 + [fixed(so_far.shape)] + [fixed(v.shape) for v in rest]
    more = [time_out.shape, (embedded.shape[1], time_out.shape[0])]
    return pl.pallas_call(
        functools.partial(time_body, factor),
        name="time_bwd",
        grid=(gmod.shape[0],),
        in_specs=ins,
        out_specs=outs + [fixed(dims) for dims in more],
        out_shape=shapes + [jax.ShapeDtypeStruct(dims, F32) for dims in more],
        scratch_shapes=[pltpu.VMEM(outer.shape, F32)],
        input_output_aliases={3: 0, 4: 1},
        compiler_params=pltpu.CompilerParams(vmem_limit_bytes=VMEM_LIMIT),
        cost_estimate=pl.CostEstimate(flops=10**9, bytes_accessed=16 * 10**6, transcendentals=0),
    )(gmod, outer, ada_weight, *held, so_far, *rest)


def attn_forward(scalars, pair, x_parts, mod, attn_kernel, qkv_weight, out_weight):
    _, share, tokens = x_parts[0].shape
    width = out_weight.shape[1]
    rows = PAIR * tokens
    thin = whole_out((rows, share), BF)
    half = whole_out((tokens, width), BF)
    return call(
        attn_kernel_body, "attn_fwd", scalars,
        [pair_of(v, pair) for v in x_parts] + [pair_of(mod, pair), whole(attn_kernel), whole(qkv_weight), whole(out_weight)],
        [whole_out((rows, width), BF), whole_out((rows, width), BF), thin, thin, thin, thin, half, half],
        [pltpu.VMEM((4, share, tokens), BF), pltpu.VMEM((PAIR * (tokens + 2 * SIDE), width), F32)],
        6_000_000_000,
    )


def feed_forward(scalars, pair, full, att, g_parts, mod, up_weight, down_weight, ffn_kernel, slots, held):
    _, share, tokens = g_parts[0].shape
    width, units = up_weight.shape
    rows = PAIR * tokens
    tall = PAIR * (tokens + 2 * SIDE)
    broad = whole_out((rows, width), BF)
    hidden = whole_out((rows, units), BF)
    half = whole_out((tokens, width), BF)
    slices = slices_out(slots, pair, share, tokens)
    return call(
        ffn_kernel_body, "ffn", scalars,
        [whole(full), whole(att[0]), whole(att[1])] + [pair_of(v, pair) for v in g_parts]
        + [pair_of(mod, pair), whole(up_weight), whole(down_weight), whole(ffn_kernel)],
        [broad, broad, hidden, broad, hidden, half, half, whole_out((PAIR, 1, width), F32), whole_out((9, units), F32),
         slices, slices],
        [pltpu.VMEM((4, share, tokens), BF), pltpu.VMEM((tall, units), F32), pltpu.VMEM((rows, units), F32),
         pltpu.VMEM((tall, units), F32), pltpu.VMEM((rows, width), F32), pltpu.VMEM((rows, width), F32),
         pltpu.VMEM((rows, width), BF), pltpu.VMEM((PAIR, 8, width), F32)],
        10_000_000_000, held,
    )


def attn_backward(
    scalars, pair, full, att, gsec, gfull, mod, mod_b, qkv, attn_kernel, qkv_weight, out_weight, slots, held
):
    tokens, width = att[0].shape
    share = out_weight.shape[0]
    rows = PAIR * tokens
    tall = PAIR * (tokens + 2 * SIDE)
    thin = whole_out((rows, share), BF)
    slices = slices_out(slots, slots // PAIR // 2 + pair, share, tokens)
    return call(
        attn_back_body, "attn_bwd", scalars,
        [whole(full), whole(att[0]), whole(att[1]), whole(gsec[0]), whole(gsec[1]), whole(gfull), pair_of(mod, pair),
         pair_of(mod_b, pair)]
        + [whole(v) for v in qkv] + [whole(attn_kernel), whole(qkv_weight), whole(out_weight)],
        [whole_out((rows, width), BF), thin, thin, thin, whole_out((PAIR, 8, width), F32), whole_out((9, width), F32),
         slices, slices],
        [pltpu.VMEM((3 * PAIR, 8, width), F32), pltpu.VMEM((rows, width), F32), pltpu.VMEM((rows, width), F32),
         pltpu.VMEM((rows, LANES), F32), pltpu.VMEM((tall, width), F32), pltpu.VMEM((tall, width), F32),
         pltpu.VMEM((rows, width), F32), pltpu.VMEM((rows, width), BF)],
        10_000_000_000, held,
    )


def core_swap(v):
    return lax.ppermute(v, "narrow", [(0, 1), (1, 0), (2, 3), (3, 2)])


def x_swap(v):
    return lax.ppermute(v, "narrow", [(0, 2), (2, 0), (1, 3), (3, 1)])


def sum_pair(a, b):
    return (a.astype(F32) + b.astype(F32)).astype(BF)


def slice_halves(x, keep, arrived):
    both = sum_pair(keep, arrived)
    return (
        lax.dynamic_index_in_dim(both, x, 0, keepdims=False),
        lax.dynamic_index_in_dim(both, 1 - x, 0, keepdims=False),
    )


def wide_swap(v, bit, count):
    return lax.ppermute(v, "wide", [(i, i ^ bit) for i in range(count)])


def pick(v, parts, at):
    rows = v.shape[0] // parts
    return lax.dynamic_slice_in_dim(v, at * rows, rows, 0)


def in_place(bit, own, came):
    return jnp.concatenate([jnp.where(bit == 0, own, came), jnp.where(bit == 0, came, own)], 0)


class WideSum:
    def __init__(self, order, product, at, count):
        self.order, self.count = order, count
        self.levels = count.bit_length() - 1
        self.bits = [at // (1 << k) % 2 for k in range(self.levels)]
        self.level, self.down = 0, True
        self.held = product
        self.swap(order(lambda v, bit: pick(v, 2, 1 - bit), product, self.bits[0]))

    def swap(self, sent):
        self.came = wide_swap(sent, 1 << self.level, self.count)

    def halve(self, held, came):
        if self.level == 0:
            held = pick(held, 2, self.bits[0])
        if self.level == self.levels - 1:
            return (sum_pair(held, came),)
        bit = self.bits[self.level + 1]
        return tuple(sum_pair(pick(held, 2, at), pick(came, 2, at)) for at in (1 - bit, bit))

    def step(self):
        if self.down:
            out = self.order(self.halve, self.held, self.came)
            self.held = out[-1]
            if len(out) == 1:
                self.down = False
            else:
                self.level += 1
            self.swap(out[0])
        else:
            self.held = self.order(functools.partial(in_place, self.bits[self.level]), self.held, self.came)
            self.level -= 1
            self.swap(self.held)

    def ready(self):
        return not self.down and self.level == 0

    def finish(self):
        return self.order(
            lambda a, b: in_place(self.bits[0], a.astype(F32), b.astype(F32)), self.held, self.came
        )


def after(value, *others):
    return lax.optimization_barrier((value, others))[0]


class Order:
    def __init__(self):
        self.last = ()

    def __call__(self, step, *inputs):
        inputs, _ = lax.optimization_barrier((inputs, self.last))
        out = step(*inputs)
        self.last = tuple(jax.tree.leaves(out)[:1])
        return out


def embed_times(stamps):
    halved = FREQ // 2
    freqs = jnp.exp(-math.log(10000.0) * jnp.arange(halved, dtype=F32) / halved)
    angles = stamps[:, None] * freqs[None, :]
    return jnp.concatenate([jnp.cos(angles), jnp.sin(angles)], 1)


def silu_slope(v):
    gate = jax.nn.sigmoid(v)
    return gate * (1.0 + v * (1.0 - gate))


def body(
    latents, cotangent, timesteps, time_in, time_out, ada_weight, ada_bias,
    attn_kernel, qkv_weight, out_weight, up_weight, ffn_kernel, down_weight,
):
    wide_count = lax.axis_size("wide")
    wide_at = lax.axis_index("wide")
    n = lax.axis_index("narrow")
    per_dev, tokens, share = latents.shape
    width = out_weight.shape[1]
    units = up_weight.shape[1]
    latent_total = timesteps.shape[0]
    scalars = jnp.stack([n, n]).astype(jnp.int32)

    met = jnp.bitwise_xor(jnp.arange(wide_count, dtype=jnp.int32), wide_at)
    stamps = timesteps.reshape(wide_count, per_dev)[met].reshape(latent_total).astype(F32)
    embedded = embed_times(stamps)
    high = lax.Precision.HIGH
    inner_pre = jnp.dot(embedded, time_in, precision=high)
    inner = jax.nn.silu(inner_pre)
    outer_pre = jnp.dot(inner, time_out, precision=high)
    outer = jax.nn.silu(outer_pre)
    x = n // 2
    factor = 1.0 / latent_total

    def pieces_of(first, count, rows):
        cols = slice(first * width, (first + count) * width)
        out = jnp.dot(rows, ada_weight[:, cols], precision=high) + ada_bias[cols]
        return out.reshape(per_dev, count, width)

    own_outer = outer[:per_dev]

    def token_product(lefts, rights):
        total = None
        for a, b in zip(lefts, rights):
            part = dot_tn(a, b)
            total = part if total is None else total + part
        return (total * factor).astype(BF)

    x_own = jnp.swapaxes(latents, 1, 2)
    g_own = jnp.swapaxes(cotangent, 1, 2)
    qkv_rows = jnp.swapaxes(qkv_weight, 1, 2)
    order = Order()
    x_across = x_swap(x_own)
    mod_a = order(lambda rows: pieces_of(0, 2, rows), own_outer)
    x_across = after(x_across, mod_a)
    g_across = x_swap(after(g_own, x_across))
    x_parts = (x_own, core_swap(x_own), x_across, core_swap(x_across))
    g_parts = (g_own, core_swap(g_own), g_across, core_swap(g_across))

    def attend(pair):
        return lambda parts: attn_forward(scalars, pair, parts, mod_a, attn_kernel, qkv_rows, out_weight)

    fwd_a = order(attend(0), x_parts)
    here_a = order(sum_pair, fwd_a[6], core_swap(fwd_a[7]))
    fwd_b = order(attend(1), after(x_parts, g_across))
    att_a = order(sum_pair, here_a, x_swap(here_a))
    here_b = order(sum_pair, fwd_b[6], core_swap(fwd_b[7]))
    mod_b = order(lambda rows: pieces_of(2, 4, rows), own_outer)
    att_a = (att_a, core_swap(att_a))

    slots = 2 * per_dev

    def feed(pair, full, held=()):
        return lambda att, parts: feed_forward(
            scalars, pair, full, att, parts, mod_b, up_weight, down_weight, ffn_kernel, slots, held
        )

    ffn_a = order(feed(0, fwd_a[0]), att_a, g_parts)
    att_b = order(sum_pair, here_b, x_swap(here_b))
    att_b = (att_b, core_swap(att_b))
    here_a = order(sum_pair, ffn_a[5], core_swap(ffn_a[6]))
    ffn_b = order(feed(1, fwd_b[0], ffn_a[9:11]), att_b, g_parts)
    sec_a = order(sum_pair, here_a, x_swap(here_a))
    sec_a = (sec_a, core_swap(sec_a))
    down_product = order(token_product, [ffn_a[2], ffn_b[2]], [ffn_a[3], ffn_b[3]])
    down_sum = WideSum(order, down_product, wide_at, wide_count)
    here_b = order(sum_pair, ffn_b[5], core_swap(ffn_b[6]))
    up_product = order(token_product, [ffn_a[1], ffn_b[1]], [ffn_a[4], ffn_b[4]])
    up_sum = WideSum(order, up_product, wide_at, wide_count)

    def attend_back(pair, full, gfull, qkv, held):
        return lambda att, sec: attn_backward(
            scalars, pair, full, att, sec, gfull, mod_a, mod_b, qkv, attn_kernel, qkv_rows, out_weight, slots, held
        )

    back_a = order(attend_back(0, fwd_a[0], ffn_a[0], fwd_a[2:5], ffn_b[9:11]), att_a, sec_a)
    sec_b = order(sum_pair, here_b, x_swap(here_b))
    sec_b = (sec_b, core_swap(sec_b))
    down_sum.step()
    back_b = order(attend_back(1, fwd_b[0], ffn_b[0], fwd_b[2:5], back_a[6:8]), att_b, sec_b)
    forward, back = (fwd_a, fwd_b), (back_a, back_b)

    lefts = [[r[5] for r in forward]] + [[g[k] for g in back] for k in (1, 2, 3)]
    rights = [[g[0] for g in back]] + [[r[1] for r in forward]] * 3
    attn_product = order(
        lambda *v: jnp.concatenate([token_product(v[2 * i], v[2 * i + 1]) for i in range(len(v) // 2)], 0),
        *[v for i in range(4) for v in (lefts[i], rights[i])],
    )
    attn_sum = WideSum(order, attn_product, wide_at, wide_count)
    down_sum.step()
    up_sum.step()

    rows_a, rows_b = 4 * per_dev, 2 * per_dev

    def pack_rows(back_mods, gates, taps, units_taps):
        mods = jnp.concatenate(back_mods, 0)
        late = jnp.concatenate([mods[:, 0], mods[:, 1], taps[0] + taps[1]], 0)
        early = jnp.concatenate([mods[:, 2], mods[:, 3], mods[:, 4], jnp.concatenate(gates, 0)[:, 0]], 0)
        ffn = (units_taps[0] + units_taps[1]).reshape(9 * units // width, width)
        return jnp.concatenate([early, late], 0).astype(BF), ffn.astype(BF)

    packed, ffn_taps = order(
        pack_rows, [g[4] for g in back], [ffn_a[7], ffn_b[7]], [g[5] for g in back], [ffn_a[8], ffn_b[8]]
    )
    packed = order(sum_pair, packed, core_swap(packed))
    down_sum.step()
    attn_sum.step()
    packed = order(lambda a, b, c: jnp.concatenate([sum_pair(a, b), c], 0), packed, x_swap(packed), ffn_taps)
    held, bit = packed[None], 1
    made = order(functools.partial(slice_halves, x), back_b[6], core_swap(back_b[7]))
    sums = (up_sum, down_sum, attn_sum)
    while bit < wide_count:
        for each in sums:
            if not each.ready():
                each.step()
        held = order(lambda a, b: jnp.concatenate([a, b], 0), held, wide_swap(held, bit, wide_count))
        bit *= 2
    def by_piece(v, rows):
        split = v[:, :rows].reshape(wide_count, rows // per_dev, per_dev, width)
        return jnp.swapaxes(split, 0, 1).reshape(rows // per_dev, latent_total, width)

    def unpack(held):
        both = by_piece(held, rows_a + rows_b)
        taps = jnp.sum(held[:, rows_a + rows_b :].astype(F32), 0) * factor
        return both[:4], both[4:], taps[:9], taps[9:].reshape(9, units)

    gmod_a, gmod_b, attn_taps, ffn_taps = order(unpack, held)
    for each in sums:
        if not each.ready():
            each.step()
    *ada_grads, outer_grad = order(lambda g: ada_backward(g, outer, ada_weight, factor), gmod_a)
    for each in sums:
        if not each.ready():
            each.step()
    finals = order(sum_pair, made[0], x_swap(made[1]))
    ada_weight_grad, ada_bias_grad, time_out_grad, time_in_grad = order(
        lambda g, held_grads, so_far: time_backward(
            g, outer, ada_weight, factor, held_grads, so_far, embedded, inner, inner_pre, outer_pre, time_out
        ),
        gmod_b, ada_grads, outer_grad,
    )
    ada_bias_grad = ada_bias_grad.reshape(6 * width)
    while not all(each.ready() for each in sums):
        for each in sums:
            if not each.ready():
                each.step()
    down_grad = down_sum.finish()
    up_grad = up_sum.finish()
    attn_grads = attn_sum.finish()
    out_grad, qkv_rows_grad = attn_grads[:share], attn_grads[share:]
    qkv_grad = jnp.swapaxes(qkv_rows_grad.reshape(3, share, width), 1, 2)
    final_out = jnp.swapaxes(finals[:per_dev], 1, 2)
    final_grad = jnp.swapaxes(finals[per_dev:], 1, 2)
    return (
        final_out, final_grad, time_in_grad, time_out_grad, ada_weight_grad, ada_bias_grad,
        attn_taps, qkv_grad, out_grad, up_grad, ffn_taps, down_grad,
    )


def solution(mesh):
    tokens = P("wide", None, "narrow")
    weights = (P(None, None, "narrow"), P("narrow", None), P(None, "narrow"), P(None, "narrow"), P("narrow", None))
    return jax.shard_map(
        body,
        mesh=mesh,
        in_specs=(tokens, tokens, P(), P(), P(), P(), P(), P()) + weights,
        out_specs=(tokens, tokens, P(), P(), P(), P(), P()) + weights,
        check_vma=False,
    )
```

time: 422 us -> 256 us (0.61)
  waiting for transfers between devices: 109 us -> 42.3 us
  matrix products: 62.4 us -> 19.8 us
  starting transfers between devices: 65.8 us -> 39.6 us
  local copies, waits for them, and re-layouts: 35.1 us -> 16.6 us
  Pallas kernels: 112 us -> 100 us
    ppermute x11 -> x8, waiting for transfers between devices: 51.4 us -> 0.48 us  [x_swap(): return lax.ppermute(v, 'narrow', [(0, 2), (2, 0), (1, 3), (3, 1)])]
    ppermute x18 -> x0, waiting for transfers between devices: 43.1 us -> none  [shift(): lax.ppermute(v, 'wide', [(i, (i + 2 * d) % count) for i in range(count)])]
    dot_general x20 -> x16, matrix products: 62.4 us -> 19.8 us  [the longest x2 9.74 us: pieces_of(): out = jnp.dot(rows, ada_weight[:, cols], precision=high) + ada_bias[cols]]
    ppermute x18 -> x0, starting transfers between devices: 32.2 us -> none  [shift(): lax.ppermute(v, 'wide', [(i, (i + 2 * d) % count) for i in range(count)])]
    ppermute x9 -> x21, waiting for transfers between devices: 14.8 us -> 36.7 us  [wide_swap(): return lax.ppermute(v, 'wide', [(i, i ^ bit) for i in range(count)])]
    ppermute x9 -> x21, starting transfers between devices: 14.7 us -> 26.3 us  [wide_swap(): return lax.ppermute(v, 'wide', [(i, i ^ bit) for i in range(count)])]
    pallas_call x6 -> x8, Pallas kernels: 112 us -> 100 us  [the longest x6 81.5 us: call(): pl.pallas_call(run, name=name, out_shape=[o for o, _ in outs], grid_spec=...]
    dynamic_update_slice x10 -> x0, local copies, waits for them, and re-layouts: 8.34 us -> none  [the longest x9 6.96 us: wide_sum(): lax.dynamic_update_index_in_dim(gathered, shift(total, d), (place - d) %...]
  transfers between devices with their start and end apart: 55 -> 43, of which waited for: 18 -> 17; matrix products, arithmetic and copies ran while one was open for 28% -> 22% of each run, Pallas kernels for 24% -> 40%
where the time goes in v2:
time: 256 us; the launch traced here: 252 us
  Pallas kernels  100 us (39%)
  waiting for transfers between devices  42.3 us (17%)
  starting transfers between devices  39.6 us (15%)
  other arithmetic  31.5 us (12%)
  matrix products  19.8 us (8%)
  local copies, waits for them, and re-layouts  16.6 us (6%)
    pallas_call x6, Pallas kernels, call(): pl.pallas_call(run, name=name, out_shape=[o for o, _ in outs], grid_spec=...  81.5 us
    ppermute x21, waiting for transfers between devices, wide_swap(): return lax.ppermute(v, 'wide', [(i, i ^ bit) for i in range(count)])  36.7 us
    ppermute x21, starting transfers between devices, wide_swap(): return lax.ppermute(v, 'wide', [(i, i ^ bit) for i in range(count)])  26.3 us
    convert_element_type x21, other arithmetic, sum_pair(): return (a.astype(F32) + b.astype(F32)).astype(BF)  18 us
    ppermute x8, starting transfers between devices, x_swap(): return lax.ppermute(v, 'narrow', [(0, 2), (2, 0), (1, 3), (3, 1)])  10.4 us
    pallas_call x1, Pallas kernels, ada_backward(): pl.pallas_call(functools.partial(ada_body, factor), name='ada_bwd', grid=...  9.81 us
    dot_general x2, matrix products, pieces_of(): out = jnp.dot(rows, ada_weight[:, cols], precision=high) + ada_bias[cols]  9.74 us
    pallas_call x1, Pallas kernels, time_backward(): pl.pallas_call(functools.partial(time_body, factor), name='time_bwd', gri...  8.96 us
  transfers between devices with their start and end apart: 43, of which 17 were waited for; matrix products, arithmetic and copies ran while one was open for 22% of the time, Pallas kernels for 40%

profile of v2, /device:TPU:0, one launch (start us, length us, event | category | flops | bytes accessed | tf_op | source)
XLA Modules:
  0.0 251.9 jit_solution(10040143991667399535)
XLA Ops:
  0.7 3.0 %collective-permute-start.1 = (bf16[4,192,256]{2,1,0:T(8,128)(2,1)}, bf16[4,192,256]{2,1,0:T(8,128)(2,1)S(1)}, u32[]{:S(2)}, u32[]{:S(2)}) collective-permute-start(bf16[4,192,256]{2,1,0:T(8,128)(2,1)} %bitcast.69), channel_id=1, source_target_pairs={{0,2},{2,0},{1,3},{3,1},{4,6},{6,4},{5,7},{7,5},{8,10},{10,8},{9,1... | collective-permute-start | bytes 1179656 | tf_op jit(solution)/shard_map/ppermute | solution.py:660
  6.9 3.1 %divide_multiply_fusion = (f32[32,768]{1,0:T(8,128)S(1)}, f32[32,768]{1,0:T(8,128)}) fusion(f32[768,768]{1,0:T(8,128)} %time_out.1, f32[32,768]{1,0:T(8,128)S(1)} %get-tuple-element.470.inner_pre), kind=kOutput, calls=%fused_computation.83 | convolution fusion | flops 113442816 | bytes 2654208 | tf_op jit(solution)/shard_map/dot_general | solution.py:777
  10.0 3.6 %fusion.7 = f32[4,1536]{1,0:T(4,128)S(1)} fusion(f32[4,768]{1,0:T(4,128)S(1)} %slice.95, f32[768,4608]{1,0:T(8,128)} %ada.3, f32[1536]{0:T(1024)S(1)} %slice-done), kind=kOutput, calls=%fused_computation.11 | convolution fusion | flops 28317696 | bytes 4761600 | tf_op jit(solution)/shard_map/dot_general | solution.py:784
  16.9 9.1 %attn_fwd.2 = (bf16[512,768]{1,0:T(8,128)(2,1)}, bf16[512,768]{1,0:T(8,128)(2,1)}, bf16[512,192]{1,0:T(8,128)(2,1)}, bf16[512,192]{1,0:T(8,128)(2,1)}, bf16[512,...) custom-call(s32[2]{0:T(128)} %pad_add_fusion.refs_0_, ...), custom_call_target="tpu_custom_call" | custom-call | flops 6000000000 | bytes 3145728 | tf_op jit(solution)/shard_map/attn_fwd/pallas_call | solution.py:460
  26.5 1.4 collective-permute-done.4
  29.0 1.5 collective-permute-start.6
  30.6 8.9 %attn_fwd.3 = (bf16[512,768]{1,0:T(8,128)(2,1)}, bf16[512,768]{1,0:T(8,128)(2,1)}, bf16[512,192]{1,0:T(8,128)(2,1)}, bf16[512,192]{1,0:T(8,128)(2,1)}, bf16[512,...) custom-call(s32[2]{0:T(128)} %pad_add_fusion.refs_0_, ...), custom_call_target="tpu_custom_call" | custom-call | flops 6000000000 | bytes 3145728 | tf_op jit(solution)/shard_map/attn_fwd/pallas_call | solution.py:460
  43.2 6.1 %fusion.4 = f32[4,3072]{1,0:T(4,128)S(1)} fusion(f32[4,768]{1,0:T(4,128)S(1)} %slice.95, f32[768,4608]{1,0:T(8,128)} %ada.3, f32[3072]{0:T(1024)S(1)} %slice.75), kind=kOutput, calls=%fused_computation.5 | convolution fusion | flops 56635392 | bytes 9510912 | tf_op jit(solution)/shard_map/dot_general | solution.py:784
  51.6 16.3 %ffn.2 = (bf16[512,768]{1,0:T(8,128)(2,1)}, bf16[512,768]{1,0:T(8,128)(2,1)}, bf16[512,768]{1,0:T(8,128)(2,1)}, bf16[512,768]{1,0:T(8,128)(2,1)}, bf16[512,768]{...) custom-call(s32[2]{0:T(128)} %pad_add_fusion.refs_0_, ...), custom_call_target="tpu_custom_call" | custom-call | flops 10000000000 | bytes 7898112 | tf_op jit(solution)/shard_map/ffn/pallas_call | solution.py:460
  68.6 1.2 collective-permute-done.12
  70.9 1.5 collective-permute-start.14
  73.2 16.1 %ffn.3 = (bf16[512,768]{1,0:T(8,128)(2,1)}, bf16[512,768]{1,0:T(8,128)(2,1)}, bf16[512,768]{1,0:T(8,128)(2,1)}, bf16[512,768]{1,0:T(8,128)(2,1)}, bf16[512,768]{...) custom-call(s32[2]{0:T(128)} %pad_add_fusion.refs_0_, ...), custom_call_target="tpu_custom_call", output_to_operand_aliasing={{9}: (12, {}), {10}: (13, {})} | custom-call | flops 10000000000 | bytes 7898112 | tf_op jit(solution)/shard_map/ffn/pallas_call | solution.py:460
  97.8 1.5 collective-permute-start.18
  100.2 15.4 %attn_bwd.2 = (bf16[512,768]{1,0:T(8,128)(2,1)}, bf16[512,192]{1,0:T(8,128)(2,1)}, bf16[512,192]{1,0:T(8,128)(2,1)}, bf16[512,192]{1,0:T(8,128)(2,1)}, f32[2,8,7...) custom-call(s32[2]{0:T(128)} %pad_add_fusion.refs_0_, ...), custom_call_target="tpu_custom_call", output_to_operand_aliasing={{6}: (15, {}), {7}: (16, {})} | custom-call | flops 10000000000 | bytes 4598784 | tf_op jit(solution)/shard_map/attn_bwd/pallas_call | solution.py:460
  115.6 1.8 add_convert_fusion.2.refs_4_
  118.6 2.0 add_convert_fusion.14
  120.6 1.6 collective-permute-start.21
  122.2 15.6 %attn_bwd.3 = (bf16[512,768]{1,0:T(8,128)(2,1)}, bf16[512,192]{1,0:T(8,128)(2,1)}, bf16[512,192]{1,0:T(8,128)(2,1)}, bf16[512,192]{1,0:T(8,128)(2,1)}, f32[2,8,7...) custom-call(s32[2]{0:T(128)} %pad_add_fusion.refs_0_, ...), custom_call_target="tpu_custom_call", output_to_operand_aliasing={{6}: (15, {}), {7}: (16, {})} | custom-call | flops 10000000000 | bytes 4598784 | tf_op jit(solution)/shard_map/attn_bwd/pallas_call | solution.py:460
  142.8 1.6 collective-permute-start.24
  144.4 1.7 add_convert_fusion.23
  146.1 2.6 %collective-permute-start.25 = (bf16[96,768]{1,0:T(8,128)(2,1)}, bf16[96,768]{1,0:T(8,128)(2,1)}, u32[]{:S(2)}, u32[]{:S(2)}) collective-permute-start(bf16[96,768]{1,0:T(8,128)(2,1)} %get-tuple-element.451), channel_id=1, source_target_pairs={{0,16},{4,20},{8,24},{12,28},{16,0},{20,4},{24,8},{28,12},{1,17},{... | collective-permute-start | bytes 442376 | tf_op jit(solution)/shard_map/ppermute | solution.py:676
  148.7 2.0 add_convert_fusion.10
  152.8 1.5 collective-permute-start.23
  154.2 2.5 collective-permute-done.25
  158.1 1.3 add_convert_fusion.11
  159.4 2.8 %collective-permute-start.28 = (bf16[192,768]{1,0:T(8,128)(2,1)S(1)}, bf16[192,768]{1,0:T(8,128)(2,1)S(1)}, u32[]{:S(2)}, u32[]{:S(2)}) collective-permute-start(bf16[192,768]{1,0:T(8,128)(2,1)S(1)} %get-tuple-element.427), channel_id=1, source_target_pairs={{0,8},{4,12},{8,0},{12,4},{16,24},{20,28},{24,16},{28,20},{1,9},{5... | collective-permute-start | bytes 884744 | tf_op jit(solution)/shard_map/ppermute | solution.py:676
  162.8 2.4 add_convert_fusion
  166.3 1.4 collective-permute-start.34
  167.7 1.6 collective-permute-start.33
  169.4 7.0 %collective-permute-done.28 = bf16[192,768]{1,0:T(8,128)(2,1)S(1)} collective-permute-done((bf16[192,768]{1,0:T(8,128)(2,1)S(1)}, bf16[192,768]{1,0:T(8,128)(2,1)S(1)}, u32[]{:S(2)}, u32[]{:S(2)}) %collective-permute-start.28) | collective-permute-done | bytes 294944 | tf_op jit(solution)/shard_map/ppermute | solution.py:676
  177.6 2.7 %collective-permute-start.31 = (bf16[2,42,768]{2,1,0:T(8,128)(2,1)S(1)}, bf16[2,42,768]{2,1,0:T(8,128)(2,1)S(1)}, u32[]{:S(2)}, u32[]{:S(2)}) collective-permute-start(bf16[2,42,768]{2,1,0:T(8,128)(2,1)S(1)} %constant_dynamic-update-slice_fusion), channel_id=1, source_target_pairs={{0,8},{4,12},{8,0},{12,4},{16,24},{20,28},{24,16},{28,20},{1,9},{5... | collective-permute-start | bytes 387080 | tf_op jit(solution)/shard_map/ppermute | solution.py:676
  180.3 1.4 collective-permute-start.26
  181.9 6.2 %collective-permute-done.33 = bf16[192,768]{1,0:T(8,128)(2,1)S(1)} collective-permute-done((bf16[192,768]{1,0:T(8,128)(2,1)S(1)}, bf16[192,768]{1,0:T(8,128)(2,1)S(1)}, u32[]{:S(2)}, u32[]{:S(2)}) %collective-permute-start.33) | collective-permute-done | bytes 294944 | tf_op jit(solution)/shard_map/ppermute | solution.py:676
  191.5 7.3 %collective-permute-done.37 = bf16[96,768]{1,0:T(8,128)(2,1)S(1)} collective-permute-done((bf16[96,768]{1,0:T(8,128)(2,1)S(1)}, bf16[96,768]{1,0:T(8,128)(2,1)S(1)}, u32[]{:S(2)}, u32[]{:S(2)}) %collective-permute-start.37) | collective-permute-done | bytes 147488 | tf_op jit(solution)/shard_map/ppermute | solution.py:676
  198.9 1.7 collective-permute-start.39
  200.6 3.2 %collective-permute-done.36 = bf16[96,768]{1,0:T(8,128)(2,1)S(1)} collective-permute-done((bf16[96,768]{1,0:T(8,128)(2,1)S(1)}, bf16[96,768]{1,0:T(8,128)(2,1)S(1)}, u32[]{:S(2)}, u32[]{:S(2)}) %collective-permute-start.36) | collective-permute-done | bytes 147488 | tf_op jit(solution)/shard_map/ppermute | solution.py:676
  204.5 4.8 %collective-permute-done.35 = bf16[4,42,768]{2,1,0:T(8,128)(2,1)S(1)} collective-permute-done((bf16[4,42,768]{2,1,0:T(8,128)(2,1)S(1)}, bf16[4,42,768]{2,1,0:T(8,128)(2,1)S(1)}, u32[]{:S(2)}, u32[]{:S(2)}) %collective-permute-start.35) | collective-permute-done | bytes 258080 | tf_op jit(solution)/shard_map/ppermute | solution.py:676
  211.8 3.7 %collective-permute-done.39 = bf16[192,768]{1,0:T(8,128)(2,1)} collective-permute-done((bf16[192,768]{1,0:T(8,128)(2,1)S(1)}, bf16[192,768]{1,0:T(8,128)(2,1)}, u32[]{:S(2)}, u32[]{:S(2)}) %collective-permute-start.39) | collective-permute-done | bytes 294944 | tf_op jit(solution)/shard_map/ppermute | solution.py:676
  216.6 1.6 collective-permute-start.41
  219.8 1.5 collective-permute-start.40
  221.3 9.8 %ada_bwd.1 = (f32[768,4608]{1,0:T(8,128)}, f32[1,4608]{1,0:T(1,128)}, f32[32,768]{1,0:T(8,128)}) custom-call(bf16[4,32,768]{2,1,0:T(8,128)(2,1)} %slice.83.gmod, f32[32,768]{1,0:T(8,128)} %copy-done.6, f32[768,4608]{1,0:T(8,128)} %ada.3), custom_call_target="tpu_custom_call" | custom-call | flops 1000000000 | bytes 24000000 | tf_op jit(solution)/shard_map/ada_bwd/pallas_call | solution.py:564
  232.3 9.0 %time_bwd.1 = (f32[768,4608]{1,0:T(8,128)}, f32[1,4608]{1,0:T(1,128)}, f32[768,768]{1,0:T(8,128)}, f32[256,768]{1,0:T(8,128)}) custom-call(bf16[2,32,768]{2,1,0:T(8,128)(2,1)} %slice.87.gmod, f32[32,768]{1,0:T(8,128)} %copy-done.6, f32[768,4608]{1,0:T(8,128)} %ada.3, ...), custom_call_target="tpu_custom_call", output_to_operand_aliasing={{0}: (3, {}), {1}: (4, {})} | custom-call | flops 1000000000 | bytes 16000000 | tf_op jit(solution)/shard_map/time_bwd/pallas_call | solution.py:581
  241.2 1.4 reduce
  242.6 1.2 convert_select_fusion.5
  243.8 1.6 pad_maximum_fusion
  245.4 1.2 convert_select_fusion.3
  246.6 1.6 pad_maximum_fusion.1
  250.3 1.3 pad_maximum_fusion.2
  (245 shorter events, 50.8 us)
Async XLA Ops:
  0.7 13.6 %collective-permute-start.1 = (bf16[4,192,256]{2,1,0:T(8,128)(2,1)}, bf16[4,192,256]{2,1,0:T(8,128)(2,1)S(1)}, u32[]{:S(2)}, u32[]{:S(2)}) collective-permute-start(bf16[4,192,256]{2,1,0:T(8,128)(2,1)} %bitcast.69), channel_id=1, source_target_pairs={{0,2},{2,0},{1,3},{3,1},{4,6},{6,4},{5,7},{7,5},{8,10},{10,8},{9,1... | collective-permute-start | bytes 1179656 | tf_op jit(solution)/shard_map/ppermute | solution.py:660
  3.7 11.9 %collective-permute-start = (bf16[4,192,256]{2,1,0:T(8,128)(2,1)}, bf16[4,192,256]{2,1,0:T(8,128)(2,1)S(1)}, u32[]{:S(2)}, u32[]{:S(2)}) collective-permute-start(bf16[4,192,256]{2,1,0:T(8,128)(2,1)} %bitcast.70), channel_id=1, source_target_pairs={{0,1},{1,0},{2,3},{3,2},{4,5},{5,4},{6,7},{7,6},{8,9},{9,8},{10,11... | collective-permute-start | bytes 1179656 | tf_op jit(solution)/shard_map/ppermute | solution.py:656
  14.3 1.8 collective-permute-start.2
  15.4 11.1 %collective-permute-start.3 = (bf16[4,192,256]{2,1,0:T(8,128)(2,1)S(1)}, bf16[4,192,256]{2,1,0:T(8,128)(2,1)S(1)}, u32[]{:S(2)}, u32[]{:S(2)}) collective-permute-start(bf16[4,192,256]{2,1,0:T(8,128)(2,1)S(1)} %bitcast.75), channel_id=1, source_target_pairs={{0,2},{2,0},{1,3},{3,1},{4,6},{6,4},{5,7},{7,5},{8,10},{10,8},{9,1... | collective-permute-start | bytes 1179656 | tf_op jit(solution)/shard_map/ppermute | solution.py:660
  26.0 1.9 collective-permute-start.4
  26.5 13.5 %copy-start.42 = (bf16[4,192,256]{2,1,0:T(8,128)(2,1)}, bf16[4,192,256]{2,1,0:T(8,128)(2,1)S(1)}, u32[]{:S(2)}) copy-start(bf16[4,192,256]{2,1,0:T(8,128)(2,1)S(1)} %collective-permute-done.3.refs_6_) | copy-start | bytes 1179652
  29.0 11.5 %collective-permute-start.6 = (bf16[256,768]{1,0:T(8,128)(2,1)S(1)}, bf16[256,768]{1,0:T(8,128)(2,1)S(1)}, u32[]{:S(2)}, u32[]{:S(2)}) collective-permute-start(bf16[256,768]{1,0:T(8,128)(2,1)S(1)} %add_convert_fusion.9), channel_id=1, source_target_pairs={{0,2},{2,0},{1,3},{3,1},{4,6},{6,4},{5,7},{7,5},{8,10},{10,8},{9,1... | collective-permute-start | bytes 1179656 | tf_op jit(solution)/shard_map/ppermute | solution.py:660
  39.5 1.9 collective-permute-start.5
  39.5 10.5 %collective-permute-start.9 = (bf16[4,192,256]{2,1,0:T(8,128)(2,1)S(1)}, bf16[4,192,256]{2,1,0:T(8,128)(2,1)S(1)}, u32[]{:S(2)}, u32[]{:S(2)}) collective-permute-start(bf16[4,192,256]{2,1,0:T(8,128)(2,1)S(1)} %bitcast.76), channel_id=1, source_target_pairs={{0,1},{1,0},{2,3},{3,2},{4,5},{5,4},{6,7},{7,6},{8,9},{9,8},{10,11... | collective-permute-start | bytes 1179656 | tf_op jit(solution)/shard_map/ppermute | solution.py:656
  40.0 9.9 %collective-permute-start.10 = (bf16[4,192,256]{2,1,0:T(8,128)(2,1)S(1)}, bf16[4,192,256]{2,1,0:T(8,128)(2,1)S(1)}, u32[]{:S(2)}, u32[]{:S(2)}) collective-permute-start(bf16[4,192,256]{2,1,0:T(8,128)(2,1)S(1)} %collective-permute-done.3.refs_6_), channel_id=1, source_target_pairs={{0,1},{1,0},{2,3},{3,2},{4,5},{5,4},{6,7},{7,6},{8,9},{9,8},{10,11... | collective-permute-start | bytes 1179656 | tf_op jit(solution)/shard_map/ppermute | solution.py:656
  40.6 9.4 %collective-permute-start.8 = (bf16[256,768]{1,0:T(8,128)(2,1)S(1)}, bf16[256,768]{1,0:T(8,128)(2,1)S(1)}, u32[]{:S(2)}, u32[]{:S(2)}) collective-permute-start(bf16[256,768]{1,0:T(8,128)(2,1)S(1)} %add_convert_fusion.8.refs_2_), channel_id=1, source_target_pairs={{0,1},{1,0},{2,3},{3,2},{4,5},{5,4},{6,7},{7,6},{8,9},{9,8},{10,11... | collective-permute-start | bytes 1179656 | tf_op jit(solution)/shard_map/ppermute | solution.py:656
  42.5 25.5 %collective-permute-start.7 = (bf16[256,768]{1,0:T(8,128)(2,1)S(1)}, bf16[256,768]{1,0:T(8,128)(2,1)S(1)}, u32[]{:S(2)}, u32[]{:S(2)}) collective-permute-start(bf16[256,768]{1,0:T(8,128)(2,1)S(1)} %add_convert_fusion.7), channel_id=1, source_target_pairs={{0,2},{2,0},{1,3},{3,1},{4,6},{6,4},{5,7},{7,5},{8,10},{10,8},{9,1... | collective-permute-start | bytes 1179656 | tf_op jit(solution)/shard_map/ppermute | solution.py:660
  67.9 1.9 collective-permute-start.12
  68.1 4.3 %collective-permute-start.11 = (bf16[256,768]{1,0:T(8,128)(2,1)S(1)}, bf16[256,768]{1,0:T(8,128)(2,1)S(1)}, u32[]{:S(2)}, u32[]{:S(2)}) collective-permute-start(bf16[256,768]{1,0:T(8,128)(2,1)S(1)} %add_convert_fusion.6.refs_2_), channel_id=1, source_target_pairs={{0,1},{1,0},{2,3},{3,2},{4,5},{5,4},{6,7},{7,6},{8,9},{9,8},{10,11... | collective-permute-start | bytes 1179656 | tf_op jit(solution)/shard_map/ppermute | solution.py:656
  70.9 18.4 %collective-permute-start.14 = (bf16[256,768]{1,0:T(8,128)(2,1)S(1)}, bf16[256,768]{1,0:T(8,128)(2,1)S(1)}, u32[]{:S(2)}, u32[]{:S(2)}) collective-permute-start(bf16[256,768]{1,0:T(8,128)(2,1)S(1)} %add_convert_fusion.5), channel_id=1, source_target_pairs={{0,2},{2,0},{1,3},{3,1},{4,6},{6,4},{5,7},{7,5},{8,10},{10,8},{9,1... | collective-permute-start | bytes 1179656 | tf_op jit(solution)/shard_map/ppermute | solution.py:660
  73.2 17.5 %copy-start.15 = (bf16[512,768]{1,0:T(8,128)(2,1)S(1)}, bf16[512,768]{1,0:T(8,128)(2,1)}, u32[]{:S(2)}) copy-start(bf16[512,768]{1,0:T(8,128)(2,1)} %get-tuple-element.276) | copy-start | bytes 2359300
  89.3 4.5 %collective-permute-start.13 = (bf16[256,768]{1,0:T(8,128)(2,1)}, bf16[256,768]{1,0:T(8,128)(2,1)}, u32[]{:S(2)}, u32[]{:S(2)}) collective-permute-start(bf16[256,768]{1,0:T(8,128)(2,1)} %get-tuple-element.267), channel_id=1, source_target_pairs={{0,1},{1,0},{2,3},{3,2},{4,5},{5,4},{6,7},{7,6},{8,9},{9,8},{10,11... | collective-permute-start | bytes 1179656 | tf_op jit(solution)/shard_map/ppermute | solution.py:656
  90.2 10.0 %collective-permute-start.16 = (bf16[256,768]{1,0:T(8,128)(2,1)}, bf16[256,768]{1,0:T(8,128)(2,1)}, u32[]{:S(2)}, u32[]{:S(2)}) collective-permute-start(bf16[256,768]{1,0:T(8,128)(2,1)} %add_convert_fusion.4.refs_4_), channel_id=1, source_target_pairs={{0,1},{1,0},{2,3},{3,2},{4,5},{5,4},{6,7},{7,6},{8,9},{9,8},{10,11... | collective-permute-start | bytes 1179656 | tf_op jit(solution)/shard_map/ppermute | solution.py:656
  97.1 18.5 %collective-permute-start.15 = (bf16[256,768]{1,0:T(8,128)(2,1)S(1)}, bf16[256,768]{1,0:T(8,128)(2,1)}, u32[]{:S(2)}, u32[]{:S(2)}) collective-permute-start(bf16[256,768]{1,0:T(8,128)(2,1)S(1)} %add_convert_fusion.3), channel_id=1, source_target_pairs={{0,2},{2,0},{1,3},{3,1},{4,6},{6,4},{5,7},{7,5},{8,10},{10,8},{9,1... | collective-permute-start | bytes 1179656 | tf_op jit(solution)/shard_map/ppermute | solution.py:660
  97.8 20.8 %collective-permute-start.18 = (bf16[384,768]{1,0:T(8,128)(2,1)S(1)}, bf16[384,768]{1,0:T(8,128)(2,1)}, u32[]{:S(2)}, u32[]{:S(2)}) collective-permute-start(bf16[384,768]{1,0:T(8,128)(2,1)S(1)} %copy-done.16), channel_id=1, source_target_pairs={{0,4},{4,0},{8,12},{12,8},{16,20},{20,16},{24,28},{28,24},{1,5},{5... | collective-permute-start | bytes 1769480 | tf_op jit(solution)/shard_map/ppermute | solution.py:676
  100.2 17.3 %copy-start.29 = (f32[32,128]{1,0:T(8,128)S(1)}, f32[32,128]{1,0:T(8,128)}, u32[]{:S(2)}) copy-start(f32[32,128]{1,0:T(8,128)} %copy-done.28) | copy-start | bytes 49156
  117.5 4.7 %collective-permute-start.17 = (bf16[256,768]{1,0:T(8,128)(2,1)}, bf16[256,768]{1,0:T(8,128)(2,1)}, u32[]{:S(2)}, u32[]{:S(2)}) collective-permute-start(bf16[256,768]{1,0:T(8,128)(2,1)} %add_convert_fusion.2.refs_4_), channel_id=1, source_target_pairs={{0,1},{1,0},{2,3},{3,2},{4,5},{5,4},{6,7},{7,6},{8,9},{9,8},{10,11... | collective-permute-start | bytes 1179656 | tf_op jit(solution)/shard_map/ppermute | solution.py:656
  118.1 30.6 %collective-permute-start.20 = (bf16[384,768]{1,0:T(8,128)(2,1)}, bf16[384,768]{1,0:T(8,128)(2,1)}, u32[]{:S(2)}, u32[]{:S(2)}) collective-permute-start(bf16[384,768]{1,0:T(8,128)(2,1)} %constant_dynamic-slice_fusion.1), channel_id=1, source_target_pairs={{0,4},{4,0},{8,12},{12,8},{16,20},{20,16},{24,28},{28,24},{1,5},{5... | collective-permute-start | bytes 1769480 | tf_op jit(solution)/shard_map/ppermute | solution.py:676
  120.6 23.7 %collective-permute-start.21 = (bf16[192,768]{1,0:T(8,128)(2,1)}, bf16[192,768]{1,0:T(8,128)(2,1)}, u32[]{:S(2)}, u32[]{:S(2)}) collective-permute-start(bf16[192,768]{1,0:T(8,128)(2,1)} %get-tuple-element.429), channel_id=1, source_target_pairs={{0,8},{4,12},{8,0},{12,4},{16,24},{20,28},{24,16},{28,20},{1,9},{5... | collective-permute-start | bytes 884744 | tf_op jit(solution)/shard_map/ppermute | solution.py:676
  122.2 15.6 %copy-start.12 = (bf16[512,768]{1,0:T(8,128)(2,1)S(1)}, bf16[512,768]{1,0:T(8,128)(2,1)}, u32[]{:S(2)}) copy-start(bf16[512,768]{1,0:T(8,128)(2,1)} %get-tuple-element.338) | copy-start | bytes 2359300
  122.2 15.6 %copy-start.20 = (bf16[512,192]{1,0:T(8,128)(2,1)S(1)}, bf16[512,192]{1,0:T(8,128)(2,1)}, u32[]{:S(2)}) copy-start(bf16[512,192]{1,0:T(8,128)(2,1)} %get-tuple-element.337) | copy-start | bytes 589828
  142.8 15.4 %collective-permute-start.24 = (bf16[384,768]{1,0:T(8,128)(2,1)S(1)}, bf16[384,768]{1,0:T(8,128)(2,1)}, u32[]{:S(2)}, u32[]{:S(2)}) collective-permute-start(bf16[384,768]{1,0:T(8,128)(2,1)S(1)} %constant_dynamic-slice_fusion), channel_id=1, source_target_pairs={{0,4},{4,0},{8,12},{12,8},{16,20},{20,16},{24,28},{28,24},{1,5},{5... | collective-permute-start | bytes 1769480 | tf_op jit(solution)/shard_map/ppermute | solution.py:676
  144.3 18.5 %collective-permute-start.19 = (bf16[2,8,192,256]{3,2,1,0:T(8,128)(2,1)}, bf16[2,8,192,256]{3,2,1,0:T(8,128)(2,1)}, u32[]{:S(2)}, u32[]{:S(2)}) collective-permute-start(bf16[2,8,192,256]{3,2,1,0:T(8,128)(2,1)} %get-tuple-element.317), channel_id=1, source_target_pairs={{0,1},{1,0},{2,3},{3,2},{4,5},{5,4},{6,7},{7,6},{8,9},{9,8},{10,11... | collective-permute-start | bytes 4718600 | tf_op jit(solution)/shard_map/ppermute | solution.py:656
  146.1 10.6 %collective-permute-start.25 = (bf16[96,768]{1,0:T(8,128)(2,1)}, bf16[96,768]{1,0:T(8,128)(2,1)}, u32[]{:S(2)}, u32[]{:S(2)}) collective-permute-start(bf16[96,768]{1,0:T(8,128)(2,1)} %get-tuple-element.451), channel_id=1, source_target_pairs={{0,16},{4,20},{8,24},{12,28},{16,0},{20,4},{24,8},{28,12},{1,17},{... | collective-permute-start | bytes 442376 | tf_op jit(solution)/shard_map/ppermute | solution.py:676
  150.7 15.5 %collective-permute-start.30 = (bf16[192,768]{1,0:T(8,128)(2,1)}, bf16[192,768]{1,0:T(8,128)(2,1)S(1)}, u32[]{:S(2)}, u32[]{:S(2)}) collective-permute-start(bf16[192,768]{1,0:T(8,128)(2,1)} %get-tuple-element.425), channel_id=1, source_target_pairs={{0,8},{4,12},{8,0},{12,4},{16,24},{20,28},{24,16},{28,20},{1,9},{5... | collective-permute-start | bytes 884744 | tf_op jit(solution)/shard_map/ppermute | solution.py:676
  151.4 1.3 collective-permute-start.22
  152.8 9.5 %collective-permute-start.23 = (bf16[33,768]{1,0:T(8,128)(2,1)S(1)}, bf16[33,768]{1,0:T(8,128)(2,1)S(1)}, u32[]{:S(2)}, u32[]{:S(2)}) collective-permute-start(bf16[33,768]{1,0:T(8,128)(2,1)S(1)} %add_convert_fusion.26), channel_id=1, source_target_pairs={{0,2},{2,0},{1,3},{3,1},{4,6},{6,4},{5,7},{7,5},{8,10},{10,8},{9,1... | collective-permute-start | bytes 152072 | tf_op jit(solution)/shard_map/ppermute | solution.py:660
  157.6 10.0 %collective-permute-start.29 = (bf16[96,768]{1,0:T(8,128)(2,1)S(1)}, bf16[96,768]{1,0:T(8,128)(2,1)S(1)}, u32[]{:S(2)}, u32[]{:S(2)}) collective-permute-start(bf16[96,768]{1,0:T(8,128)(2,1)S(1)} %add_convert_fusion.22), channel_id=1, source_target_pairs={{0,16},{4,20},{8,24},{12,28},{16,0},{20,4},{24,8},{28,12},{1,17},{... | collective-permute-start | bytes 442376 | tf_op jit(solution)/shard_map/ppermute | solution.py:676
  159.4 17.0 %collective-permute-start.28 = (bf16[192,768]{1,0:T(8,128)(2,1)S(1)}, bf16[192,768]{1,0:T(8,128)(2,1)S(1)}, u32[]{:S(2)}, u32[]{:S(2)}) collective-permute-start(bf16[192,768]{1,0:T(8,128)(2,1)S(1)} %get-tuple-element.427), channel_id=1, source_target_pairs={{0,8},{4,12},{8,0},{12,4},{16,24},{20,28},{24,16},{28,20},{1,9},{5... | collective-permute-start | bytes 884744 | tf_op jit(solution)/shard_map/ppermute | solution.py:676
  162.3 15.4 %collective-permute-start.27 = (bf16[1,42,768]{2,1,0:T(8,128)(2,1)S(1)}, bf16[1,42,768]{2,1,0:T(8,128)(2,1)S(1)}, u32[]{:S(2)}, u32[]{:S(2)}) collective-permute-start(bf16[1,42,768]{2,1,0:T(8,128)(2,1)S(1)} %fusion.62), channel_id=1, source_target_pairs={{0,4},{4,0},{8,12},{12,8},{16,20},{20,16},{24,28},{28,24},{1,5},{5... | collective-permute-start | bytes 193544 | tf_op jit(solution)/shard_map/ppermute | solution.py:676
  166.3 15.4 %collective-permute-start.34 = (bf16[96,768]{1,0:T(8,128)(2,1)S(1)}, bf16[96,768]{1,0:T(8,128)(2,1)S(1)}, u32[]{:S(2)}, u32[]{:S(2)}) collective-permute-start(bf16[96,768]{1,0:T(8,128)(2,1)S(1)} %get-tuple-element.447), channel_id=1, source_target_pairs={{0,16},{4,20},{8,24},{12,28},{16,0},{20,4},{24,8},{28,12},{1,17},{... | collective-permute-start | bytes 442376 | tf_op jit(solution)/shard_map/ppermute | solution.py:676
  167.7 20.3 %collective-permute-start.33 = (bf16[192,768]{1,0:T(8,128)(2,1)S(1)}, bf16[192,768]{1,0:T(8,128)(2,1)S(1)}, u32[]{:S(2)}, u32[]{:S(2)}) collective-permute-start(bf16[192,768]{1,0:T(8,128)(2,1)S(1)} %pad_maximum_fusion.8), channel_id=1, source_target_pairs={{0,8},{4,12},{8,0},{12,4},{16,24},{20,28},{24,16},{28,20},{1,9},{5... | collective-permute-start | bytes 884744 | tf_op jit(solution)/shard_map/ppermute | solution.py:676
  176.4 12.0 %collective-permute-start.32 = (bf16[96,768]{1,0:T(8,128)(2,1)S(1)}, bf16[96,768]{1,0:T(8,128)(2,1)S(1)}, u32[]{:S(2)}, u32[]{:S(2)}) collective-permute-start(bf16[96,768]{1,0:T(8,128)(2,1)S(1)} %get-tuple-element.449), channel_id=1, source_target_pairs={{0,16},{4,20},{8,24},{12,28},{16,0},{20,4},{24,8},{28,12},{1,17},{... | collective-permute-start | bytes 442376 | tf_op jit(solution)/shard_map/ppermute | solution.py:676
  177.6 12.7 %collective-permute-start.31 = (bf16[2,42,768]{2,1,0:T(8,128)(2,1)S(1)}, bf16[2,42,768]{2,1,0:T(8,128)(2,1)S(1)}, u32[]{:S(2)}, u32[]{:S(2)}) collective-permute-start(bf16[2,42,768]{2,1,0:T(8,128)(2,1)S(1)} %constant_dynamic-update-slice_fusion), channel_id=1, source_target_pairs={{0,8},{4,12},{8,0},{12,4},{16,24},{20,28},{24,16},{28,20},{1,9},{5... | collective-permute-start | bytes 387080 | tf_op jit(solution)/shard_map/ppermute | solution.py:676
  180.3 50.8 %collective-permute-start.26 = (bf16[8,192,256]{2,1,0:T(8,128)(2,1)}, bf16[8,192,256]{2,1,0:T(8,128)(2,1)S(1)}, u32[]{:S(2)}, u32[]{:S(2)}) collective-permute-start(bf16[8,192,256]{2,1,0:T(8,128)(2,1)} %get-tuple-element.430), channel_id=1, source_target_pairs={{0,2},{2,0},{1,3},{3,1},{4,6},{6,4},{5,7},{7,5},{8,10},{10,8},{9,1... | collective-permute-start | bytes 2359304 | tf_op jit(solution)/shard_map/ppermute | solution.py:660
  181.8 17.1 %collective-permute-start.37 = (bf16[96,768]{1,0:T(8,128)(2,1)S(1)}, bf16[96,768]{1,0:T(8,128)(2,1)S(1)}, u32[]{:S(2)}, u32[]{:S(2)}) collective-permute-start(bf16[96,768]{1,0:T(8,128)(2,1)S(1)} %add_convert_fusion.17), channel_id=1, source_target_pairs={{0,16},{4,20},{8,24},{12,28},{16,0},{20,4},{24,8},{28,12},{1,17},{... | collective-permute-start | bytes 442376 | tf_op jit(solution)/shard_map/ppermute | solution.py:676
  188.2 54.4 %collective-permute-start.42 = (bf16[384,768]{1,0:T(8,128)(2,1)S(1)}, bf16[384,768]{1,0:T(8,128)(2,1)}, u32[]{:S(2)}, u32[]{:S(2)}) collective-permute-start(bf16[384,768]{1,0:T(8,128)(2,1)S(1)} %pad_maximum_fusion.4), channel_id=1, source_target_pairs={{0,4},{4,0},{8,12},{12,8},{16,20},{20,16},{24,28},{28,24},{1,5},{5... | collective-permute-start | bytes 1769480 | tf_op jit(solution)/shard_map/ppermute | solution.py:676
  188.4 15.4 %collective-permute-start.36 = (bf16[96,768]{1,0:T(8,128)(2,1)S(1)}, bf16[96,768]{1,0:T(8,128)(2,1)S(1)}, u32[]{:S(2)}, u32[]{:S(2)}) collective-permute-start(bf16[96,768]{1,0:T(8,128)(2,1)S(1)} %add_convert_fusion.16), channel_id=1, source_target_pairs={{0,16},{4,20},{8,24},{12,28},{16,0},{20,4},{24,8},{28,12},{1,17},{... | collective-permute-start | bytes 442376 | tf_op jit(solution)/shard_map/ppermute | solution.py:676
  190.4 19.0 %collective-permute-start.35 = (bf16[4,42,768]{2,1,0:T(8,128)(2,1)S(1)}, bf16[4,42,768]{2,1,0:T(8,128)(2,1)S(1)}, u32[]{:S(2)}, u32[]{:S(2)}) collective-permute-start(bf16[4,42,768]{2,1,0:T(8,128)(2,1)S(1)} %constant_dynamic-update-slice_fusion.2), channel_id=1, source_target_pairs={{0,16},{4,20},{8,24},{12,28},{16,0},{20,4},{24,8},{28,12},{1,17},{... | collective-permute-start | bytes 774152 | tf_op jit(solution)/shard_map/ppermute | solution.py:676
  198.9 16.6 %collective-permute-start.39 = (bf16[192,768]{1,0:T(8,128)(2,1)S(1)}, bf16[192,768]{1,0:T(8,128)(2,1)}, u32[]{:S(2)}, u32[]{:S(2)}) collective-permute-start(bf16[192,768]{1,0:T(8,128)(2,1)S(1)} %pad_maximum_fusion.9), channel_id=1, source_target_pairs={{0,8},{4,12},{8,0},{12,4},{16,24},{20,28},{24,16},{28,20},{1,9},{5... | collective-permute-start | bytes 884744 | tf_op jit(solution)/shard_map/ppermute | solution.py:676
  203.9 14.9 %collective-permute-start.38 = (bf16[192,768]{1,0:T(8,128)(2,1)S(1)}, bf16[192,768]{1,0:T(8,128)(2,1)}, u32[]{:S(2)}, u32[]{:S(2)}) collective-permute-start(bf16[192,768]{1,0:T(8,128)(2,1)S(1)} %pad_maximum_fusion.10), channel_id=1, source_target_pairs={{0,8},{4,12},{8,0},{12,4},{16,24},{20,28},{24,16},{28,20},{1,9},{5... | collective-permute-start | bytes 884744 | tf_op jit(solution)/shard_map/ppermute | solution.py:676
  216.6 28.8 %collective-permute-start.41 = (bf16[384,768]{1,0:T(8,128)(2,1)S(1)}, bf16[384,768]{1,0:T(8,128)(2,1)}, u32[]{:S(2)}, u32[]{:S(2)}) collective-permute-start(bf16[384,768]{1,0:T(8,128)(2,1)S(1)} %pad_maximum_fusion.6), channel_id=1, source_target_pairs={{0,4},{4,0},{8,12},{12,8},{16,20},{20,16},{24,28},{28,24},{1,5},{5... | collective-permute-start | bytes 1769480 | tf_op jit(solution)/shard_map/ppermute | solution.py:676
  219.8 28.3 %collective-permute-start.40 = (bf16[384,768]{1,0:T(8,128)(2,1)S(1)}, bf16[384,768]{1,0:T(8,128)(2,1)}, u32[]{:S(2)}, u32[]{:S(2)}) collective-permute-start(bf16[384,768]{1,0:T(8,128)(2,1)S(1)} %pad_maximum_fusion.7), channel_id=1, source_target_pairs={{0,4},{4,0},{8,12},{12,8},{16,20},{20,16},{24,28},{28,24},{1,5},{5... | collective-permute-start | bytes 1769480 | tf_op jit(solution)/shard_map/ppermute | solution.py:676
  (44 other events, 141.6 us)
